TPU v7x, 256 devices: a whole 4x4x8 slice. The times are simulated.
256 devices in a mesh: gx: 8 (over x, z_hi), gy: 8 (over y, core), gz: 4 (over z_lo).
Axes of the slice: x: 4, y: 4, z: 8 (z_hi: 2, z_lo: 4; z = z_hi * 4 + z_lo), core: 2. Of those that a mesh axis runs over, the one named last changes fastest.
Arguments:
- features: bfloat16 [8, 8, 4, 512, 128], P('gx', 'gy', 'gz'), may hold values from -6 to 6
- positions: float32 [8, 8, 4, 3, 512], P('gx', 'gy', 'gz'), may hold values from 0 to 1
- counts: int32 [8, 8, 4], P('gx', 'gy', 'gz'), may hold values from 256 to 512, as said below
- pair_first: int32 [8, 8, 4, 128, 128], P('gx', 'gy', 'gz'), may hold values from 0 to 511, as said below
- pair_second: int32 [8, 8, 4, 128, 128], P('gx', 'gy', 'gz'), may hold values from 0 to 13823, as said below
- pair_mask: int32 [8, 8, 4, 128, 128], P('gx', 'gy', 'gz'), may hold values from 0 to 1, as said below
- w_centre: bfloat16 [128, 256], replicated, may hold values from -0.5 to 0.5
- w_neighbour: bfloat16 [128, 256], replicated, may hold values from -0.5 to 0.5
- w_charge: bfloat16 [128], replicated, may hold values from -0.5 to 0.5
- w_radial: float32 [8, 256], replicated, may hold values from -3.5 to 3.5
- w_hidden: bfloat16 [256, 256], replicated, may hold values from -0.375 to 0.375
- w_energy: float32 [256], replicated, may hold values from -0.375 to 0.375
Outputs:
- forces: float32 [8, 8, 4, 3, 512], P('gx', 'gy', 'gz')
- charge_grad: float32 [8, 8, 4, 512], P('gx', 'gy', 'gz')
Inputs may be any that keep to these rules, and one draw needn't show every extreme that they name: `counts`: every brick holds at least half of its slots; some brick is full and some holds exactly half; the atoms present fill the lowest slots. `pair_first`: every listed pair names a present atom of its own brick. `pair_second`: every listed pair names a present atom of the image brick of its slot s (entry s * 512 + a); within slot 13 it differs from the pair's first atom. `pair_mask`: on every brick the tiles that hold a valid pair come before those that hold none; tile 0 always holds valid pairs.
All inputs are finite; a program needn't handle non-finite values.
Results may differ from a plain program's by a relative error of at most 0.0032.
Values may be sent and summed in bfloat16 or wider, within the bound.
No kernel may reach another device: no remote copies, remote signals or barrier semaphores. Data moves between devices by JAX's collectives and lax.ppermute only.
A program may use at most 64 MiB of HBM per device.

v0:
```python
import jax
import jax.numpy as jnp
from jax import lax
from jax.sharding import PartitionSpec as P

delta_sq = 0.04
spread = 0.3
coulomb = 0.2
root_pi = 1.7724538509055159
block_tiles = 8


def with_halo(block, sides, width):
    for axis, dim in sides:
        count = lax.axis_size(axis)
        forward = [(i, i + 1) for i in range(count - 1)]
        forward.append((count - 1, 0))
        backward = [(target, source) for source, target in forward]
        low = lax.ppermute(
            lax.slice_in_dim(block, block.shape[dim] - width, None, axis=dim), axis, forward
        )
        high = lax.ppermute(lax.slice_in_dim(block, 0, width, axis=dim), axis, backward)
        block = jnp.concatenate([low, block, high], axis=dim)
    return block


def silu_parts(value):
    logistic = jax.nn.sigmoid(value)
    return (value * logistic, logistic * (1.0 + value * (1.0 - logistic)))


def shifted_coords(neighbours):
    steps_axis = jnp.arange(3, dtype=jnp.float32) - 1.0
    zero_grid = jnp.zeros((3, 3, 3), jnp.float32)
    shift_grid = jnp.stack(
        [
            steps_axis[:, None, None] + zero_grid,
            steps_axis[None, :, None] + zero_grid,
            steps_axis[None, None, :] + zero_grid,
            zero_grid,
        ],
        axis=3,
    )
    moved_grid = neighbours + shift_grid[..., None]
    return jnp.moveaxis(moved_grid, 3, 0).reshape(4, -1)


def pair_block(
    centre_proj,
    image_proj,
    coords_own,
    coords_all,
    pick_first,
    pick_second,
    pick_mask,
    w_radial,
    w_hidden,
    w_energy,
):
    rows_i = pick_first.reshape(-1)
    rows_j = pick_second.reshape(-1)
    weight = pick_mask.reshape(-1).astype(jnp.float32)
    place_i = coords_own[:3][:, rows_i]
    place_j = coords_all[:3][:, rows_j]
    charge_i = coords_own[3][rows_i]
    charge_j = coords_all[3][rows_j]
    separation = place_j - place_i
    dist_sq = jnp.sum(separation * separation, axis=0) + delta_sq
    distance = jnp.sqrt(dist_sq)
    centres = 0.25 + 0.3 * jnp.arange(w_radial.shape[0], dtype=jnp.float32)
    offset = distance[None, :] - centres[:, None]
    radial_basis = jnp.exp(-(offset / spread) * (offset / spread))
    radial = lax.dot_general(
        radial_basis, w_radial, (((0,), (0,)), ((), ())), precision=lax.Precision.HIGHEST
    )
    pre_one = (
        centre_proj[rows_i].astype(jnp.float32) + image_proj[rows_j].astype(jnp.float32) + radial
    )
    act_one, slope_one = silu_parts(pre_one)
    hidden = act_one.astype(jnp.bfloat16)
    pre_two = jnp.dot(hidden, w_hidden, preferred_element_type=jnp.float32)
    act_two, slope_two = silu_parts(pre_two)
    envelope = jnp.exp(-0.5 * dist_sq)
    readout = jnp.dot(act_two, w_energy, precision=lax.Precision.HIGHEST)
    back_two = (envelope[:, None] * w_energy[None, :] * slope_two).astype(jnp.bfloat16)
    back_one = (
        lax.dot_general(
            back_two, w_hidden, (((1,), (1,)), ((), ())), preferred_element_type=jnp.float32
        )
        * slope_one
    )
    back_basis = lax.dot_general(
        w_radial, back_one, (((1,), (1,)), ((), ())), precision=lax.Precision.HIGHEST
    )
    slope_nn = (
        jnp.sum(back_basis * radial_basis * (-2.0 * offset / (spread * spread)), axis=0)
        - readout * distance * envelope
    )
    screened = lax.erfc(distance)
    coulomb_pot = screened / distance
    slope_coul = -(2.0 / root_pi) * jnp.exp(-dist_sq) / distance - screened / dist_sq
    slope_all = weight * (slope_nn + coulomb * charge_i * charge_j * slope_coul)
    push_pair = separation * (slope_all / distance)[None, :]
    term_i = jnp.concatenate(
        [push_pair, (weight * coulomb * charge_j * coulomb_pot)[None, :]], axis=0
    )
    term_j = jnp.concatenate(
        [-push_pair, (weight * coulomb * charge_i * coulomb_pot)[None, :]], axis=0
    )
    return (rows_i, term_i, rows_j, term_j)


def brick_sum(
    centre_proj,
    image_proj,
    coords_own,
    coords_all,
    pair_first,
    pair_second,
    pair_mask,
    w_radial,
    w_hidden,
    w_energy,
    block_count,
):
    atom_slots = centre_proj.shape[0]

    def advance(index, summed):
        begin_row = index * block_tiles
        rows_i, term_i, rows_j, term_j = pair_block(
            centre_proj,
            image_proj,
            coords_own,
            coords_all,
            lax.dynamic_slice_in_dim(pair_first, begin_row, block_tiles, 0),
            lax.dynamic_slice_in_dim(pair_second, begin_row, block_tiles, 0),
            lax.dynamic_slice_in_dim(pair_mask, begin_row, block_tiles, 0),
            w_radial,
            w_hidden,
            w_energy,
        )
        summed = summed.at[13, :, rows_i].add(term_i.T)
        summed = summed.at[rows_j // atom_slots, :, rows_j % atom_slots].add(term_j.T)
        return summed

    start_sum = jnp.zeros((27, 4, atom_slots), jnp.float32)
    return lax.fori_loop(0, block_count, advance, start_sum)


def local(
    features,
    positions,
    counts,
    pair_first,
    pair_second,
    pair_mask,
    w_centre,
    w_neighbour,
    w_charge,
    w_radial,
    w_hidden,
    w_energy,
):
    own_feat = features[0, 0, 0]
    atom_slots = own_feat.shape[0]
    raw_charge = jnp.dot(own_feat, w_charge, preferred_element_type=jnp.float32)
    filled = counts[0, 0, 0]
    alive_slot = jnp.arange(atom_slots, dtype=jnp.int32) < filled
    average = jnp.sum(jnp.where(alive_slot, raw_charge, 0.0)) / filled.astype(jnp.float32)
    charges = jnp.where(alive_slot, raw_charge - average, 0.0)
    coords_own = jnp.concatenate([positions[0, 0, 0], charges[None, :]], axis=0)
    centre_proj = jnp.dot(own_feat, w_centre, preferred_element_type=jnp.float32).astype(
        jnp.bfloat16
    )
    neighbours = with_halo(coords_own[None, None, None], (("gx", 0), ("gy", 1), ("gz", 2)), 1)
    nearby = with_halo(features, (("gx", 0), ("gy", 1), ("gz", 2)), 1)
    image_proj = jnp.dot(
        nearby.reshape(27 * atom_slots, own_feat.shape[1]),
        w_neighbour,
        preferred_element_type=jnp.float32,
    ).astype(jnp.bfloat16)
    coords_all = shifted_coords(neighbours)
    first_tab = pair_first[0, 0, 0]
    second_tab = pair_second[0, 0, 0]
    mask_tab = pair_mask[0, 0, 0]
    busy_tiles = jnp.sum(jnp.any(mask_tab != 0, axis=1).astype(jnp.int32))
    block_count = (busy_tiles + block_tiles - 1) // block_tiles
    partial_value = brick_sum(
        centre_proj,
        image_proj,
        coords_own,
        coords_all,
        first_tab,
        second_tab,
        mask_tab,
        w_radial,
        w_hidden,
        w_energy,
        block_count,
    ).reshape(3, 3, 3, 4, atom_slots)
    sectioned = with_halo(partial_value, (("gx", 0),), 1)
    sectioned = sectioned[0] + sectioned[2] + sectioned[4]
    sectioned = with_halo(sectioned, (("gy", 0),), 1)
    sectioned = sectioned[0] + sectioned[2] + sectioned[4]
    sectioned = with_halo(sectioned, (("gz", 0),), 1)
    summed = sectioned[0] + sectioned[2] + sectioned[4]
    return (summed[:3][None, None, None], summed[3][None, None, None])


def solution(mesh):
    placed = (
        P("gx", "gy", "gz", None, None),
        P("gx", "gy", "gz", None, None),
        P("gx", "gy", "gz"),
        P("gx", "gy", "gz", None, None),
        P("gx", "gy", "gz", None, None),
        P("gx", "gy", "gz", None, None),
        P(),
        P(),
        P(),
        P(),
        P(),
        P(),
    )
    return jax.shard_map(
        local,
        mesh=mesh,
        in_specs=placed,
        out_specs=(P("gx", "gy", "gz", None, None), P("gx", "gy", "gz", None)),
        check_vma=False,
    )
```

profile of v0, /device:TPU:2, one launch (start us, length us, event | category | flops | bytes accessed | tf_op | source)
XLA Modules:
  0.0 1192.0 jit_solution(9471897687505593760)
XLA Ops:
  0.7 7.3 collective-permute-start.6
  24.1 6.9 collective-permute-start
  48.6 40.5 %collective-permute-done.4 = f32[3,3,1,4,512]{4,3,2,1,0:T(4,128)S(1)} collective-permute-done((f32[3,3,1,4,512]{4,3,2,1,0:T(4,128)S(1)}, f32[3,3,1,4,512]{4,3,2,1,0:T(4,128)S(1)}, u32[]{:S(2)}, u32[]{:S(2)}) %collective-permute-start.4) | collective-permute-done | bytes 73760 | tf_op jit(solution)/shard_map/ppermute | solution.py:19
  103.6 330.6 %while.12 = (s32[]{:T(128)}, f32[27,4,512]{1,2,0:T(8,128)}, s32[]{:T(128)}, s32[128,128]{1,0:T(8,128)}, f32[4,13824]{0,1:T(8,128)}, /*index=5*/s32[128,128]{1,0:...) while((s32[]{:T(128)}, f32[27,4,512]{1,2,0:T(8,128)}, ...), condition=%wide.region_8.9_spmd, body=%wide.region_3.8_spmd.sunk | while | flops 330377216 | bytes 33843600 | solution.py:147
  113.6 7.4 gather_fusion.4
  133.5 6.2 gather_fusion.3
  139.6 6.9 gather_fusion
  147.2 11.2 scatter_fusion
  158.7 11.2 scatter_fusion.1
  179.7 7.4 gather_fusion.4
  199.6 6.2 gather_fusion.3
  205.7 6.9 gather_fusion
  213.3 11.2 scatter_fusion
  224.7 11.2 scatter_fusion.1
  245.8 7.4 gather_fusion.4
  265.6 6.2 gather_fusion.3
  271.8 6.9 gather_fusion
  279.3 11.2 scatter_fusion
  290.8 11.2 scatter_fusion.1
  311.9 7.4 gather_fusion.4
  337.9 6.9 gather_fusion
  345.4 11.2 scatter_fusion
  356.9 11.2 scatter_fusion.1
  378.0 7.4 gather_fusion.4
  404.0 6.9 gather_fusion
  411.5 11.2 scatter_fusion
  423.0 11.2 scatter_fusion.1
  444.8 269.6 %collective-permute-start.13 = (f32[1,3,3,4,512]{4,3,2,1,0:T(4,128)S(1)}, f32[1,3,3,4,512]{4,3,2,1,0:T(4,128)S(1)}, u32[]{:S(2)}, u32[]{:S(2)}) collective-permute-start(f32[1,3,3,4,512]{4,3,2,1,0:T(4,128)S(1)} %bitcast.161), channel_id=1, source_target_pairs={{32,0},{64,32},{96,64},{128,96},{160,128},{192,160},{224,192},{0,2... | collective-permute-start | bytes 221192 | tf_op jit(solution)/shard_map/ppermute | solution.py:22
  716.5 63.8 %collective-permute-start.14 = (f32[1,3,4,512]{3,2,1,0:T(4,128)S(1)}, f32[1,3,4,512]{3,2,1,0:T(4,128)S(1)}, u32[]{:S(2)}, u32[]{:S(2)}) collective-permute-start(f32[1,3,4,512]{3,2,1,0:T(4,128)S(1)} %get-tuple-element.281), channel_id=1, source_target_pairs={{0,4},{4,8},{8,12},{12,16},{16,20},{20,24},{24,28},{28,0},{1,5},{5... | collective-permute-start | bytes 73736 | tf_op jit(solution)/shard_map/ppermute | solution.py:19
  780.3 7.6 collective-permute-start.15
  789.3 327.5 %collective-permute-done.15 = f32[1,3,4,512]{3,2,1,0:T(4,128)S(1)} collective-permute-done((f32[1,3,4,512]{3,2,1,0:T(4,128)S(1)}, f32[1,3,4,512]{3,2,1,0:T(4,128)S(1)}, u32[]{:S(2)}, u32[]{:S(2)}) %collective-permute-start.15) | collective-permute-done | bytes 24608 | tf_op jit(solution)/shard_map/ppermute | solution.py:22
  1116.9 70.2 %collective-permute-start.16 = (f32[1,4,512]{2,1,0:T(4,128)S(1)}, f32[1,4,512]{2,1,0:T(4,128)S(1)}, u32[]{:S(2)}, u32[]{:S(2)}) collective-permute-start(f32[1,4,512]{2,1,0:T(4,128)S(1)} %get-tuple-element.283), channel_id=1, source_target_pairs={{0,1},{1,2},{2,3},{3,0},{4,5},{5,6},{6,7},{7,4},{8,9},{9,10},{10,1... | collective-permute-start | bytes 24584 | tf_op jit(solution)/shard_map/ppermute | solution.py:19
  (272 shorter events, 192.6 us)
Async XLA Ops:
  0.6 94.4 %copy-start = (bf16[128,256]{1,0:T(8,128)(2,1)S(1)}, bf16[128,256]{1,0:T(8,128)(2,1)}, u32[]{:S(2)}) copy-start(bf16[128,256]{1,0:T(8,128)(2,1)} %param.21) | copy-start | bytes 196612
  0.6 41.0 %copy-start.2 = (s32[1,1,1,128,128]{4,3,2,1,0:T(8,128)S(1)}, s32[1,1,1,128,128]{4,3,2,1,0:T(8,128)}, u32[]{:S(2)}) copy-start(s32[1,1,1,128,128]{4,3,2,1,0:T(8,128)} %param.19) | copy-start | bytes 196612
  0.7 14.0 %collective-permute-start.6 = (bf16[1,1,1,512,128]{4,3,2,1,0:T(8,128)(2,1)}, bf16[1,1,1,512,128]{4,3,2,1,0:T(8,128)(2,1)S(1)}, u32[]{:S(2)}, u32[]{:S(2)}) collective-permute-start(bf16[1,1,1,512,128]{4,3,2,1,0:T(8,128)(2,1)} %param.14), channel_id=1, source_target_pairs={{0,32},{32,64},{64,96},{96,128},{128,160},{160,192},{192,224},{224... | collective-permute-start | bytes 393224 | tf_op jit(solution)/shard_map/ppermute | solution.py:19
  7.9 11.9 collective-permute-start.7
  19.8 11.3 collective-permute-start.8
  19.8 11.3 collective-permute-start.9
  24.1 13.9 %collective-permute-start = (f32[1,1,1,4,512]{4,3,2,1,0:T(4,128)S(1)}, f32[1,1,1,4,512]{4,3,2,1,0:T(4,128)S(1)}, u32[]{:S(2)}, u32[]{:S(2)}) collective-permute-start(f32[1,1,1,4,512]{4,3,2,1,0:T(4,128)S(1)} %maximum_bitcast_fusion.2), channel_id=1, source_target_pairs={{0,32},{32,64},{64,96},{96,128},{128,160},{160,192},{192,224},{224... | collective-permute-start | bytes 24584 | tf_op jit(solution)/shard_map/ppermute | solution.py:19
  31.0 7.7 collective-permute-start.1
  32.3 61.2 %collective-permute-start.10 = (bf16[3,3,1,512,128]{4,3,2,1,0:T(8,128)(2,1)}, bf16[3,3,1,512,128]{4,3,2,1,0:T(8,128)(2,1)S(1)}, u32[]{:S(2)}, u32[]{:S(2)}) collective-permute-start(bf16[3,3,1,512,128]{4,3,2,1,0:T(8,128)(2,1)} %pad_maximum_fusion.1), channel_id=1, source_target_pairs={{0,1},{1,2},{2,3},{3,0},{4,5},{5,6},{6,7},{7,4},{8,9},{9,10},{10,1... | collective-permute-start | bytes 3538952 | tf_op jit(solution)/shard_map/ppermute | solution.py:19
  33.2 60.2 %collective-permute-start.11 = (bf16[3,3,1,512,128]{4,3,2,1,0:T(8,128)(2,1)}, bf16[3,3,1,512,128]{4,3,2,1,0:T(8,128)(2,1)}, u32[]{:S(2)}, u32[]{:S(2)}) collective-permute-start(bf16[3,3,1,512,128]{4,3,2,1,0:T(8,128)(2,1)} %pad_maximum_fusion.1), channel_id=1, source_target_pairs={{1,0},{2,1},{3,2},{0,3},{5,4},{6,5},{7,6},{4,7},{9,8},{10,9},{11,1... | collective-permute-start | bytes 3538952 | tf_op jit(solution)/shard_map/ppermute | solution.py:22
  38.7 4.5 collective-permute-start.2
  38.7 4.5 collective-permute-start.3
  43.2 45.9 %collective-permute-start.4 = (f32[3,3,1,4,512]{4,3,2,1,0:T(4,128)S(1)}, f32[3,3,1,4,512]{4,3,2,1,0:T(4,128)S(1)}, u32[]{:S(2)}, u32[]{:S(2)}) collective-permute-start(f32[3,3,1,4,512]{4,3,2,1,0:T(4,128)S(1)} %pad_maximum_fusion.2), channel_id=1, source_target_pairs={{0,1},{1,2},{2,3},{3,0},{4,5},{5,6},{6,7},{7,4},{8,9},{9,10},{10,1... | collective-permute-start | bytes 221192 | tf_op jit(solution)/shard_map/ppermute | solution.py:19
  44.4 44.7 %collective-permute-start.5 = (f32[3,3,1,4,512]{4,3,2,1,0:T(4,128)S(1)}, f32[3,3,1,4,512]{4,3,2,1,0:T(4,128)S(1)}, u32[]{:S(2)}, u32[]{:S(2)}) collective-permute-start(f32[3,3,1,4,512]{4,3,2,1,0:T(4,128)S(1)} %pad_maximum_fusion.2), channel_id=1, source_target_pairs={{1,0},{2,1},{3,2},{0,3},{5,4},{6,5},{7,6},{4,7},{9,8},{10,9},{11,1... | collective-permute-start | bytes 221192 | tf_op jit(solution)/shard_map/ppermute | solution.py:22
  99.9 3.6 copy-start.1
  99.9 3.6 copy-start.3
  99.9 3.6 copy-start.4
  99.9 3.6 copy-start.5
  99.9 3.6 copy-start.6
  126.5 3.0 slice-start
  126.5 3.1 slice-start.1
  192.6 3.1 slice-start.1
  258.7 3.1 slice-start.1
  324.8 3.0 slice-start
  324.8 3.1 slice-start.1
  390.9 3.1 slice-start.1
  442.4 272.7 %collective-permute-start.12 = (f32[1,3,3,4,512]{4,3,2,1,0:T(4,128)S(1)}, f32[1,3,3,4,512]{4,3,2,1,0:T(4,128)S(1)}, u32[]{:S(2)}, u32[]{:S(2)}) collective-permute-start(f32[1,3,3,4,512]{4,3,2,1,0:T(4,128)S(1)} %bitcast.160), channel_id=1, source_target_pairs={{0,32},{32,64},{64,96},{96,128},{128,160},{160,192},{192,224},{224... | collective-permute-start | bytes 221192 | tf_op jit(solution)/shard_map/ppermute | solution.py:19
  444.8 271.6 %collective-permute-start.13 = (f32[1,3,3,4,512]{4,3,2,1,0:T(4,128)S(1)}, f32[1,3,3,4,512]{4,3,2,1,0:T(4,128)S(1)}, u32[]{:S(2)}, u32[]{:S(2)}) collective-permute-start(f32[1,3,3,4,512]{4,3,2,1,0:T(4,128)S(1)} %bitcast.161), channel_id=1, source_target_pairs={{32,0},{64,32},{96,64},{128,96},{160,128},{192,160},{224,192},{0,2... | collective-permute-start | bytes 221192 | tf_op jit(solution)/shard_map/ppermute | solution.py:22
  716.5 72.8 %collective-permute-start.14 = (f32[1,3,4,512]{3,2,1,0:T(4,128)S(1)}, f32[1,3,4,512]{3,2,1,0:T(4,128)S(1)}, u32[]{:S(2)}, u32[]{:S(2)}) collective-permute-start(f32[1,3,4,512]{3,2,1,0:T(4,128)S(1)} %get-tuple-element.281), channel_id=1, source_target_pairs={{0,4},{4,8},{8,12},{12,16},{16,20},{20,24},{24,28},{28,0},{1,5},{5... | collective-permute-start | bytes 73736 | tf_op jit(solution)/shard_map/ppermute | solution.py:19
  780.3 336.6 %collective-permute-start.15 = (f32[1,3,4,512]{3,2,1,0:T(4,128)S(1)}, f32[1,3,4,512]{3,2,1,0:T(4,128)S(1)}, u32[]{:S(2)}, u32[]{:S(2)}) collective-permute-start(f32[1,3,4,512]{3,2,1,0:T(4,128)S(1)} %get-tuple-element.282), channel_id=1, source_target_pairs={{4,0},{8,4},{12,8},{16,12},{20,16},{24,20},{28,24},{0,28},{5,1},{9... | collective-permute-start | bytes 73736 | tf_op jit(solution)/shard_map/ppermute | solution.py:22
  1116.9 71.6 %collective-permute-start.16 = (f32[1,4,512]{2,1,0:T(4,128)S(1)}, f32[1,4,512]{2,1,0:T(4,128)S(1)}, u32[]{:S(2)}, u32[]{:S(2)}) collective-permute-start(f32[1,4,512]{2,1,0:T(4,128)S(1)} %get-tuple-element.283), channel_id=1, source_target_pairs={{0,1},{1,2},{2,3},{3,0},{4,5},{5,6},{6,7},{7,4},{8,9},{9,10},{10,1... | collective-permute-start | bytes 24584 | tf_op jit(solution)/shard_map/ppermute | solution.py:19
  1187.1 3.7 collective-permute-start.17
  (3 other events, 9.1 us)
where the time goes:
time: 1200 us; the launch traced here: 1190 us
  starting transfers between devices  440 us (37%)
  waiting for transfers between devices  385 us (32%)
  local copies, waits for them, and re-layouts  214 us (18%)
  other arithmetic  119 us (10%)
  matrix products  29.7 us (2%)
    ppermute x9, waiting for transfers between devices, with_halo(): lax.ppermute(lax.slice_in_dim(block, 0, width, axis=dim), axis, backward)  336 us
    ppermute x9, starting transfers between devices, with_halo(): lax.ppermute(lax.slice_in_dim(block, 0, width, axis=dim), axis, backward)  289 us
    ppermute x9, starting transfers between devices, with_halo(): lax.ppermute(lax.slice_in_dim(block, block.shape[dim] - width, None, axis...  150 us
    while x35, other arithmetic  113 us
    ppermute x9, waiting for transfers between devices, with_halo(): lax.ppermute(lax.slice_in_dim(block, block.shape[dim] - width, None, axis...  49.1 us
    gather x5, local copies, waits for them, and re-layouts, pair_block(): image_proj[rows_j].astype(jnp.float32)  36.9 us
    gather x5, local copies, waits for them, and re-layouts, pair_block(): charge_i = coords_own[3][rows_i]  34.3 us
    gather x5, local copies, waits for them, and re-layouts, pair_block(): charge_j = coords_all[3][rows_j]  30.8 us
  transfers between devices with their start and end apart: 18, of which 10 were waited for; matrix products, arithmetic and copies ran while one was open for 1% of the time, Pallas kernels for 0%

commit v1 on v0

v1 whole, which is shorter than its diff:
```python
import jax
import jax.numpy as jnp
from jax import lax
from jax.experimental import pallas as pl
from jax.experimental.pallas import tpu as pltpu
from jax.sharding import PartitionSpec as P

delta_sq = 0.04
spread = 0.3
coulomb = 0.2
root_pi = 1.7724538509055159
chunk = 256
macro_chunks = 4
macro = chunk * macro_chunks

erfc_p = (
    2.326819970068386e-2, -1.387039388740657e-1, 3.687424674597105e-1, -5.824733027278666e-1,
    6.210004621745983e-1, -4.944515323274145e-1, 3.404879937665872e-1, -2.741127028184656e-1,
    5.638259427386472e-1,
)
erfc_r = (
    -1.047766399936249e1, 1.297719955372516e1, -7.495518717768503e0, 2.921019019210786e0,
    -1.015265279202700e0, 4.218463358204948e-1, -2.820767439740514e-1, 5.641895067754075e-1,
)
erf_t = (
    7.853861353153693e-5, -8.010193625184903e-4, 5.188327685732524e-3, -2.685381193529856e-2,
    1.128358514861418e-1, -3.761262582423300e-1, 1.128379165726710e0,
)


def poly(x, coefficients):
    total = jnp.full_like(x, coefficients[0])
    for value in coefficients[1:]:
        total = total * x + value
    return total


def erfc_positive(x, exp_minus_sq):
    square = x * x
    inverse = 1.0 / square
    tail = exp_minus_sq / x * jnp.where(x < 2.0, poly(inverse, erfc_p), poly(inverse, erfc_r))
    return jnp.where(x < 1.0, 1.0 - x * poly(square, erf_t), tail)


def geometry_kernel(coords_ref, first_ref, second_ref, mask_ref, out_ref):
    rows = 32

    def group(index, carry):
        base = pl.multiple_of(index * rows, rows)
        first = first_ref[pl.ds(base, rows), :]
        second = second_ref[pl.ds(base, rows), :]
        weight = mask_ref[pl.ds(base, rows), :].astype(jnp.float32)
        lane_j = second & 127
        row_j = second >> 7
        lane_i = first & 127
        row_i = first >> 7

        def pick(row, lanes):
            wide = jnp.broadcast_to(row, (rows, 128))
            return jnp.take_along_axis(wide, lanes, axis=1, mode="promise_in_bounds")

        def scan(slot, found):
            block = coords_ref[pl.ds(pl.multiple_of(slot * 16, 16), 16), :]
            for part in range(4):
                hit = row_j == slot * 4 + part
                found = tuple(
                    jnp.where(hit, pick(block[c * 4 + part : c * 4 + part + 1], lane_j), found[c])
                    for c in range(4)
                )
            return found

        zeros = jnp.zeros((rows, 128), jnp.float32)
        place_j = lax.fori_loop(0, 27, scan, (zeros,) * 4)
        own = coords_ref[13 * 16 : 14 * 16, :]
        place_i = [zeros] * 4
        for part in range(4):
            hit = row_i == part
            for c in range(4):
                place_i[c] = jnp.where(
                    hit, pick(own[c * 4 + part : c * 4 + part + 1], lane_i), place_i[c]
                )
        slot = second >> 9
        step_x = (slot * 57) >> 9
        rest = slot - step_x * 9
        step_y = (rest * 11) >> 5
        step_z = rest - step_y * 3
        sep = [
            (place_j[c] + (step.astype(jnp.float32) - 1.0)) - place_i[c]
            for c, step in enumerate((step_x, step_y, step_z))
        ]
        dist_sq = sep[0] * sep[0] + sep[1] * sep[1] + sep[2] * sep[2] + delta_sq
        distance = jnp.sqrt(dist_sq)
        inverse = 1.0 / distance
        exp_minus = jnp.exp(-dist_sq)
        screened = erfc_positive(distance, exp_minus)
        potential = screened * inverse
        slope_coul = -(2.0 / root_pi) * exp_minus * inverse - screened / dist_sq
        envelope = jnp.exp(-0.5 * dist_sq)
        values = (
            sep[0],
            sep[1],
            sep[2],
            distance,
            weight * envelope * inverse,
            weight * coulomb * place_i[3] * place_j[3] * slope_coul * inverse,
            weight * coulomb * place_j[3] * potential,
            weight * coulomb * place_i[3] * potential,
            jnp.where(first < 256, first, 512).astype(jnp.float32),
            jnp.where(first < 256, 512, first - 256).astype(jnp.float32),
            (second & 255).astype(jnp.float32),
            (second >> 8).astype(jnp.float32),
        )
        for position, value in enumerate(values):
            out_ref[pl.ds(base, rows), position, :] = value
        return carry

    lax.fori_loop(0, 128 // rows, group, 0)
    out_ref[:, 12:16, :] = jnp.zeros((128, 4, 128), jnp.float32)


def geometry(coords, first, second, mask):
    return pl.pallas_call(
        geometry_kernel,
        out_shape=jax.ShapeDtypeStruct((128, 16, 128), jnp.float32),
        name="geometry",
    )(coords, first, second, mask)


def pair_kernel(
    blocks_ref,
    rows_ref,
    low_ref,
    mid_ref,
    high_ref,
    geo_ref,
    centre_ref,
    neighbour_ref,
    radial_ref,
    hidden_ref,
    hidden_t_ref,
    energy_ref,
    back_ref,
    out_low,
    out_mid,
    out_high,
    stage_ref,
    table_ref,
    gather_ref,
    iota_ref,
    hot_ref,
    term_ref,
    acc_i_ref,
    acc_j_ref,
    sems,
):
    copies = [
        pltpu.make_async_copy(source, stage_ref.at[k], sems.at[k])
        for k, source in enumerate((low_ref, mid_ref, high_ref))
    ]
    for copy in copies:
        copy.start()
    iota_ref[...] = lax.broadcasted_iota(jnp.int32, (256, 128), 0).astype(jnp.float32).astype(jnp.bfloat16)
    acc_i_ref[...] = jnp.zeros_like(acc_i_ref)
    acc_j_ref[...] = jnp.zeros_like(acc_j_ref)
    for k in range(3):
        copies[k].wait()

        def widen(step, carry, k=k):
            rows = pl.ds(pl.multiple_of(step * 128, 128), 128)
            table_ref[pl.ds(pl.multiple_of(k * 4608 + step * 128, 128), 128), :] = stage_ref[
                k, rows, :
            ].astype(jnp.float32)
            return carry

        lax.fori_loop(0, 36, widen, 0)

    def fetch(index):
        for p in range(chunk):
            row = rows_ref[index * 2 + p // 128, p % 128]
            gather_ref[pl.ds(p, 1), :] = table_ref[pl.ds(row, 1), :]

    def wide(row):
        return jnp.broadcast_to(row.astype(jnp.bfloat16), (256, chunk))

    def one_hot(row):
        iota = jnp.concatenate([iota_ref[...]] * (chunk // 128), axis=1)
        return jnp.where(
            iota == wide(row), jnp.ones((), jnp.bfloat16), jnp.zeros((), jnp.bfloat16)
        )

    def step(part, first_chunk):
        index = first_chunk + part
        lanes = pl.ds(pl.multiple_of(part * chunk, chunk), chunk)
        geo = jnp.concatenate([geo_ref[index * 2], geo_ref[index * 2 + 1]], axis=1)
        features = gather_ref[...].astype(jnp.bfloat16)
        fetch(jnp.minimum(index + 1, 63))
        distance = geo[3:4]
        offset = distance - (
            0.25 + 0.3 * lax.broadcasted_iota(jnp.int32, (8, chunk), 0).astype(jnp.float32)
        )
        basis = jnp.exp(-(offset / spread) * (offset / spread))
        basis_slope = basis * offset * (-2.0 / (spread * spread))
        top = basis.astype(jnp.bfloat16).astype(jnp.float32)
        basis_parts = jnp.concatenate([top, top, basis - top, jnp.zeros_like(top)], axis=0)
        hot_low = one_hot(geo[8:9])
        hot_high = one_hot(geo[9:10])
        hot_ref[0:256, lanes] = hot_low
        hot_ref[256:512, lanes] = hot_high
        half_one = (
            jnp.dot(centre_ref[:, 0:256], hot_low, preferred_element_type=jnp.float32)
            + jnp.dot(centre_ref[:, 256:512], hot_high, preferred_element_type=jnp.float32)
            + lax.dot_general(
                neighbour_ref[...],
                features,
                (((1,), (1,)), ((), ())),
                preferred_element_type=jnp.float32,
            )
            + jnp.dot(
                radial_ref[...],
                basis_parts.astype(jnp.bfloat16),
                preferred_element_type=jnp.float32,
            )
        )
        bend_one = jnp.tanh(half_one)
        gain_one = 1.0 + bend_one
        act_one = half_one * gain_one
        slope_one = gain_one + act_one * (1.0 - bend_one)
        half_two = jnp.dot(
            hidden_t_ref[...], act_one.astype(jnp.bfloat16), preferred_element_type=jnp.float32
        )
        bend_two = jnp.tanh(half_two)
        gain_two = 1.0 + bend_two
        act_two = half_two * gain_two
        slope_two = gain_two + act_two * (1.0 - bend_two)
        energy = jnp.concatenate([energy_ref[...]] * (chunk // 128), axis=1)
        readout = jnp.sum(act_two * energy, axis=0, keepdims=True)
        back_two = (slope_two * energy).astype(jnp.bfloat16)
        back_one = (
            jnp.dot(hidden_ref[...], back_two, preferred_element_type=jnp.float32) * slope_one
        )
        back_basis = jnp.dot(
            back_ref[...], back_one.astype(jnp.bfloat16), preferred_element_type=jnp.float32
        )
        total = jnp.sum(
            (back_basis[0:8] + back_basis[8:16]) * basis_slope, axis=0, keepdims=True
        ) - (readout * distance)
        push = geo[4:5] * total + geo[5:6]
        term_ref[0:3, lanes] = geo[0:3] * push
        term_ref[3:5, lanes] = geo[6:8]
        return first_chunk

    fetch(0)

    def block(index, carry):
        lax.fori_loop(0, macro_chunks, step, index * macro_chunks)
        terms = term_ref[...]
        push = terms[0:3]
        own = jnp.concatenate([push, terms[3:4], jnp.zeros((4, macro), jnp.float32)], axis=0)
        own_top = own.astype(jnp.bfloat16).astype(jnp.float32)
        own_parts = jnp.concatenate([own_top, own - own_top], axis=0).astype(jnp.bfloat16)
        acc_i_ref[...] += lax.dot_general(
            own_parts, hot_ref[...], (((1,), (1,)), ((), ())), preferred_element_type=jnp.float32
        )
        far = jnp.concatenate([-push, terms[4:5]], axis=0)
        far_top = far.astype(jnp.bfloat16)
        far_rest = (far - far_top.astype(jnp.float32)).astype(jnp.bfloat16)
        geo = jnp.concatenate([geo_ref[index * 2 * macro_chunks + k] for k in range(macro // 128)], axis=1)
        iota = jnp.concatenate([iota_ref[...]] * (macro // 128), axis=1)
        one = jnp.ones((), jnp.bfloat16)
        zero = jnp.zeros((), jnp.bfloat16)
        hot = jnp.where(
            iota == jnp.broadcast_to(geo[10:11].astype(jnp.bfloat16), (256, macro)), one, zero
        )
        block_hit = jnp.where(
            iota[0:64] == jnp.broadcast_to(geo[11:12].astype(jnp.bfloat16), (64, macro)), one, zero
        )
        spread_rows = jnp.concatenate(
            [
                block_hit * jnp.broadcast_to(part[c : c + 1], (64, macro))
                for c in range(4)
                for part in (far_top, far_rest)
            ],
            axis=0,
        )
        acc_j_ref[...] += lax.dot_general(
            spread_rows, hot, (((1,), (1,)), ((), ())), preferred_element_type=jnp.float32
        )
        return carry

    lax.fori_loop(0, blocks_ref[0], block, 0)
    acc_i = acc_i_ref[...]
    acc_i = acc_i[0:8] + acc_i[8:16]
    for c in range(4):
        plane = acc_j_ref[c * 128 : c * 128 + 64, :] + acc_j_ref[c * 128 + 64 : c * 128 + 128, :]
        for slot in range(27):
            step_x, step_y, step_z = slot // 9, slot // 3 % 3, slot % 3
            target = (out_low, out_mid, out_high)[step_y]
            for half in range(2):
                row = plane[slot * 2 + half : slot * 2 + half + 1]
                if slot == 13:
                    row = row + acc_i[c : c + 1, half * 256 : half * 256 + 256]
                target[step_z * 3 + step_x, c * 2 + half : c * 2 + half + 1, :] = row


def pair_sums(block_count, rows, low, mid, high, geo, weights):
    vmem = pl.BlockSpec(memory_space=pltpu.VMEM)
    smem = pl.BlockSpec(memory_space=pltpu.SMEM)
    far = pl.BlockSpec(memory_space=pl.ANY)
    out = jax.ShapeDtypeStruct((9, 8, 256), jnp.float32)
    return pl.pallas_call(
        pair_kernel,
        out_shape=(out, out, out),
        in_specs=[smem, smem, far, far, far, vmem] + [vmem] * 7,
        out_specs=(vmem, vmem, vmem),
        scratch_shapes=[
            pltpu.VMEM((3, 4608, 128), jnp.bfloat16),
            pltpu.VMEM((13824, 128), jnp.float32),
            pltpu.VMEM((chunk, 128), jnp.float32),
            pltpu.VMEM((256, 128), jnp.bfloat16),
            pltpu.VMEM((512, macro), jnp.bfloat16),
            pltpu.VMEM((8, macro), jnp.float32),
            pltpu.VMEM((16, 512), jnp.float32),
            pltpu.VMEM((512, 256), jnp.float32),
            pltpu.SemaphoreType.DMA((3,)),
        ],
        compiler_params=pltpu.CompilerParams(vmem_limit_bytes=48 * 1024 * 1024),
        name="pairs",
    )(block_count, rows, low, mid, high, geo, *weights)


def swap(block, axis):
    count = lax.axis_size(axis)
    forward = [(i, (i + 1) % count) for i in range(count)]
    backward = [(target, source) for source, target in forward]
    return lax.ppermute(block, axis, forward), lax.ppermute(block, axis, backward)


def split(value):
    top = lax.reduce_precision(value, 8, 7)
    return top, value - top


def indices(second_tab, mask_tab, atom_slots):
    slot = second_tab >> 9
    step_x = slot // 9
    step_y = slot // 3 % 3
    step_z = slot % 3
    rows = (step_y * 9 + step_z * 3 + step_x) * atom_slots + (second_tab & (atom_slots - 1))
    busy_tiles = jnp.sum(jnp.any(mask_tab != 0, axis=1).astype(jnp.int32))
    tiles = macro // 128
    block_count = ((busy_tiles + tiles - 1) // tiles).reshape(1)
    return block_count, rows


def arrange(own_feat, w_centre, w_neighbour, w_radial, w_hidden, w_energy):
    centre_t = jnp.dot(own_feat, w_centre, preferred_element_type=jnp.float32).astype(
        jnp.bfloat16
    ).T * jnp.bfloat16(0.5)
    half = jnp.bfloat16(0.5)
    radial_top, radial_rest = split(w_radial * 0.5)
    zero_rows = jnp.zeros_like(radial_top)
    radial_t = (
        jnp.concatenate([radial_top, radial_rest, radial_top, zero_rows], axis=0)
        .astype(jnp.bfloat16)
        .T
    )
    back = jnp.concatenate([radial_top, radial_rest], axis=0).astype(jnp.bfloat16)
    energy = jnp.broadcast_to(w_energy[:, None], (w_energy.shape[0], 128))
    return (
        centre_t,
        w_neighbour.T * half,
        radial_t,
        w_hidden * half,
        w_hidden.T * half,
        energy,
        back,
    )


def local(
    features,
    positions,
    counts,
    pair_first,
    pair_second,
    pair_mask,
    w_centre,
    w_neighbour,
    w_charge,
    w_radial,
    w_hidden,
    w_energy,
):
    own_feat = features[0, 0, 0]
    atom_slots = own_feat.shape[0]
    raw_charge = jnp.dot(own_feat, w_charge, preferred_element_type=jnp.float32)
    filled = counts[0, 0, 0]
    alive_slot = jnp.arange(atom_slots, dtype=jnp.int32) < filled
    average = jnp.sum(jnp.where(alive_slot, raw_charge, 0.0)) / filled.astype(jnp.float32)
    charges = jnp.where(alive_slot, raw_charge - average, 0.0)
    coords_own = jnp.concatenate([positions[0, 0, 0], charges[None, :]], axis=0).reshape(16, 128)

    def collect(block):
        low, high = swap(block, "gx")
        line = jnp.stack([low, block, high], axis=0)
        low, high = swap(line, "gz")
        plane = jnp.concatenate([low, line, high], axis=0)
        low, high = swap(plane, "gy")
        return low, plane, high

    near_coords = jnp.stack(collect(coords_own), axis=0)
    low, mid, high = [part.reshape(9 * atom_slots, -1) for part in collect(own_feat)]
    coords_all = (
        near_coords.reshape(3, 3, 3, 16, 128).transpose(2, 0, 1, 3, 4).reshape(27 * 16, 128)
    )
    first_tab = pair_first[0, 0, 0]
    second_tab = pair_second[0, 0, 0]
    mask_tab = pair_mask[0, 0, 0]
    geo = geometry(coords_all, first_tab, second_tab, mask_tab)

    block_count, rows = indices(second_tab, mask_tab, atom_slots)
    weights = arrange(own_feat, w_centre, w_neighbour, w_radial, w_hidden, w_energy)
    out_low, out_mid, out_high = pair_sums(block_count, rows, low, mid, high, geo, weights)

    def give(low, mid, high, axis):
        count = lax.axis_size(axis)
        forward = [(i, (i + 1) % count) for i in range(count)]
        backward = [(target, source) for source, target in forward]
        return mid + lax.ppermute(high, axis, forward) + lax.ppermute(low, axis, backward)

    plane = give(out_low, out_mid, out_high, "gy")
    line = give(plane[0:3], plane[3:6], plane[6:9], "gz")
    summed = give(line[0], line[1], line[2], "gx").reshape(4, atom_slots)
    return (summed[:3][None, None, None], summed[3][None, None, None])


def solution(mesh):
    placed = (
        P("gx", "gy", "gz", None, None),
        P("gx", "gy", "gz", None, None),
        P("gx", "gy", "gz"),
        P("gx", "gy", "gz", None, None),
        P("gx", "gy", "gz", None, None),
        P("gx", "gy", "gz", None, None),
        P(),
        P(),
        P(),
        P(),
        P(),
        P(),
    )
    return jax.shard_map(
        local,
        mesh=mesh,
        in_specs=placed,
        out_specs=(P("gx", "gy", "gz", None, None), P("gx", "gy", "gz", None)),
        check_vma=False,
    )
```

time: 1200 us -> 198 us (0.17)
  the two profiles are of different devices: /device:TPU:2 before, /device:TPU:1 now
where the time goes in v1:
time: 198 us; the launch traced here: 197 us
  starting transfers between devices  92 us (46%)
  Pallas kernels  47.1 us (24%)
  waiting for transfers between devices  43.8 us (22%)
  local copies, waits for them, and re-layouts  7.35 us (4%)
  between operations  2.94 us (1%)
  other arithmetic  2.57 us (1%)
    ppermute x3, starting transfers between devices, give(): lax.ppermute(high, axis, forward)  57 us
    pallas_call x1, Pallas kernels, geometry(): pl.pallas_call(geometry_kernel, out_shape=jax.ShapeDtypeStruct((128, 16,...  29.9 us
    ppermute x6, starting transfers between devices, swap(): lax.ppermute(block, axis, backward)  26.5 us
    ppermute x6, waiting for transfers between devices, swap(): lax.ppermute(block, axis, backward)  17.1 us
    pallas_call x1, Pallas kernels, pair_sums(): pl.pallas_call(pair_kernel, out_shape=(out, out, out), in_specs=[smem, sm...  17.1 us
    ppermute x6, waiting for transfers between devices, swap(): lax.ppermute(block, axis, forward)  16.3 us
    ppermute x3, waiting for transfers between devices, give(): lax.ppermute(low, axis, backward)  6.72 us
    ppermute x3, starting transfers between devices, give(): lax.ppermute(low, axis, backward)  5.98 us
  transfers between devices with their start and end apart: 18, of which 11 were waited for; matrix products, arithmetic and copies ran while one was open for 3% of the time, Pallas kernels for 15%

profile of v1, /device:TPU:1, one launch (start us, length us, event | category | flops | bytes accessed | tf_op | source)
XLA Modules:
  0.0 197.0 jit_solution(2783132337370230022)
XLA Ops:
  2.1 1.0 fusion.16
  4.4 10.0 %collective-permute-start.7 = (f32[16,128]{1,0:T(8,128)S(1)}, f32[16,128]{1,0:T(8,128)S(1)}, u32[]{:S(2)}, u32[]{:S(2)}) collective-permute-start(f32[16,128]{1,0:T(8,128)S(1)} %reshape.39), channel_id=1, source_target_pairs={{32,0},{64,32},{96,64},{128,96},{160,128},{192,160},{224,192},{0,2... | collective-permute-start | bytes 24584 | tf_op jit(solution)/shard_map/ppermute | solution.py:335
  14.4 7.5 %collective-permute-start.1 = (bf16[512,128]{1,0:T(8,128)(2,1)}, bf16[512,128]{1,0:T(8,128)(2,1)S(1)}, u32[]{:S(2)}, u32[]{:S(2)}) collective-permute-start(bf16[512,128]{1,0:T(8,128)(2,1)} %bitcast.62), channel_id=1, source_target_pairs={{32,0},{64,32},{96,64},{128,96},{160,128},{192,160},{224,192},{0,2... | collective-permute-start | bytes 393224 | tf_op jit(solution)/shard_map/ppermute | solution.py:335
  21.9 0.9 copy.20
  22.9 1.0 fusion.6.rows_ref
  23.9 1.0 copy.21
  25.0 2.0 %collective-permute-done.1 = bf16[512,128]{1,0:T(8,128)(2,1)S(1)} collective-permute-done((bf16[512,128]{1,0:T(8,128)(2,1)}, bf16[512,128]{1,0:T(8,128)(2,1)S(1)}, u32[]{:S(2)}, u32[]{:S(2)}) %collective-permute-start.1) | collective-permute-done | bytes 131104 | tf_op jit(solution)/shard_map/ppermute | solution.py:335
  27.1 9.3 %collective-permute-done = bf16[512,128]{1,0:T(8,128)(2,1)S(1)} collective-permute-done((bf16[512,128]{1,0:T(8,128)(2,1)}, bf16[512,128]{1,0:T(8,128)(2,1)S(1)}, u32[]{:S(2)}, u32[]{:S(2)}) %collective-permute-start) | collective-permute-done | bytes 131104 | tf_op jit(solution)/shard_map/ppermute | solution.py:335
  37.0 3.3 %collective-permute-start.3 = (bf16[3,512,128]{2,1,0:T(8,128)(2,1)S(1)}, bf16[3,512,128]{2,1,0:T(8,128)(2,1)S(1)}, u32[]{:S(2)}, u32[]{:S(2)}) collective-permute-start(bf16[3,512,128]{2,1,0:T(8,128)(2,1)S(1)} %pad_maximum_fusion), channel_id=1, source_target_pairs={{1,0},{2,1},{3,2},{0,3},{5,4},{6,5},{7,6},{4,7},{9,8},{10,9},{11,1... | collective-permute-start | bytes 1179656 | tf_op jit(solution)/shard_map/ppermute | solution.py:335
  40.3 7.0 %collective-permute-done.2 = bf16[3,512,128]{2,1,0:T(8,128)(2,1)} collective-permute-done((bf16[3,512,128]{2,1,0:T(8,128)(2,1)S(1)}, bf16[3,512,128]{2,1,0:T(8,128)(2,1)}, u32[]{:S(2)}, u32[]{:S(2)}) %collective-permute-start.2) | collective-permute-done | bytes 393248 | tf_op jit(solution)/shard_map/ppermute | solution.py:335
  47.3 1.0 constant_dynamic-update-slice_fusion.4
  48.4 6.8 %collective-permute-done.3 = bf16[3,512,128]{2,1,0:T(8,128)(2,1)S(1)} collective-permute-done((bf16[3,512,128]{2,1,0:T(8,128)(2,1)S(1)}, bf16[3,512,128]{2,1,0:T(8,128)(2,1)S(1)}, u32[]{:S(2)}, u32[]{:S(2)}) %collective-permute-start.3) | collective-permute-done | bytes 393248 | tf_op jit(solution)/shard_map/ppermute | solution.py:335
  55.3 1.8 collective-permute-start.5
  57.1 1.2 collective-permute-start.4
  58.3 0.8 collective-permute-start.8
  60.6 2.6 %collective-permute-start.9 = (f32[3,16,128]{2,1,0:T(8,128)S(1)}, f32[3,16,128]{2,1,0:T(8,128)S(1)}, u32[]{:S(2)}, u32[]{:S(2)}) collective-permute-start(f32[3,16,128]{2,1,0:T(8,128)S(1)} %pad_maximum_fusion.1), channel_id=1, source_target_pairs={{1,0},{2,1},{3,2},{0,3},{5,4},{6,5},{7,6},{4,7},{9,8},{10,9},{11,1... | collective-permute-start | bytes 73736 | tf_op jit(solution)/shard_map/ppermute | solution.py:335
  63.3 0.9 collective-permute-done.9
  64.2 1.3 collective-permute-start.11
  65.9 7.4 %collective-permute-done.11 = f32[9,16,128]{2,1,0:T(8,128)S(1)} collective-permute-done((f32[9,16,128]{2,1,0:T(8,128)S(1)}, f32[9,16,128]{2,1,0:T(8,128)S(1)}, u32[]{:S(2)}, u32[]{:S(2)}) %collective-permute-start.11) | collective-permute-done | bytes 73760 | tf_op jit(solution)/shard_map/ppermute | solution.py:335
  74.0 29.9 %geometry.1.geo_ref = f32[128,16,128]{2,1,0:T(8,128)} custom-call(f32[432,128]{1,0:T(8,128)} %bitcast.65, s32[128,128]{1,0:T(8,128)} %bitcast.73, s32[128,128]{1,0:T(8,128)} %bitcast.69, s32[128,128]{1,0:T(8,128)} %bitcast.68), custom_call_target="tpu_custom_call" | custom-call | tf_op jit(solution)/shard_map/geometry/pallas_call | solution.py:122
  104.1 1.2 copy-done.1
  105.3 17.1 %pairs.1 = (f32[9,8,256]{2,1,0:T(8,128)S(1)}, f32[9,8,256]{2,1,0:T(8,128)S(1)}, f32[9,8,256]{2,1,0:T(8,128)S(1)}) custom-call(s32[1]{0:T(128)} %bitcast.1.blocks_ref, s32[128,128]{1,0:T(8,128)S(1)} %fusion.6.rows_ref, bf16[4608,128]{1,0:T(8,128)(2,1)} %bitcast.7.low_ref, bf16[4608,128]{1,0:T(8,128)(2,1)S(1)} %bitcast.60, bf16[4608,128]{1,0:T(8,128)(2,1)S(1)} %bitcast.61, ...), custom_call_target="tpu_custom_call" | custom-call | tf_op jit(solution)/shard_map/pairs/pallas_call | solution.py:310
  122.5 49.6 %collective-permute-start.12 = (f32[9,8,256]{2,1,0:T(8,128)S(1)}, f32[9,8,256]{2,1,0:T(8,128)S(1)}, u32[]{:S(2)}, u32[]{:S(2)}) collective-permute-start(f32[9,8,256]{2,1,0:T(8,128)S(1)} %get-tuple-element.6), channel_id=1, source_target_pairs={{0,4},{4,8},{8,12},{12,16},{16,20},{20,24},{24,28},{28,0},{1,5},{5... | collective-permute-start | bytes 221192 | tf_op jit(solution)/shard_map/ppermute | solution.py:429
  172.0 1.4 collective-permute-done.12
  173.4 2.4 %collective-permute-done.13 = f32[9,8,256]{2,1,0:T(8,128)S(1)} collective-permute-done((f32[9,8,256]{2,1,0:T(8,128)S(1)}, f32[9,8,256]{2,1,0:T(8,128)S(1)}, u32[]{:S(2)}, u32[]{:S(2)}) %collective-permute-start.13) | collective-permute-done | bytes 73760 | tf_op jit(solution)/shard_map/ppermute | solution.py:429
  175.8 0.8 collective-permute-start.14
  176.7 5.0 %collective-permute-start.15 = (f32[3,8,256]{2,1,0:T(8,128)S(1)}, f32[3,8,256]{2,1,0:T(8,128)S(1)}, u32[]{:S(2)}, u32[]{:S(2)}) collective-permute-start(f32[3,8,256]{2,1,0:T(8,128)S(1)} %get-tuple-element.15), channel_id=1, source_target_pairs={{1,0},{2,1},{3,2},{0,3},{5,4},{6,5},{7,6},{4,7},{9,8},{10,9},{11,1... | collective-permute-start | bytes 73736 | tf_op jit(solution)/shard_map/ppermute | solution.py:429
  181.6 1.1 collective-permute-done.14
  182.8 6.6 %collective-permute-start.16 = (f32[8,256]{1,0:T(8,128)S(1)}, f32[8,256]{1,0:T(8,128)S(1)}, u32[]{:S(2)}, u32[]{:S(2)}) collective-permute-start(f32[8,256]{1,0:T(8,128)S(1)} %get-tuple-element.16), channel_id=1, source_target_pairs={{0,32},{32,64},{64,96},{96,128},{128,160},{160,192},{192,224},{224... | collective-permute-start | bytes 24584 | tf_op jit(solution)/shard_map/ppermute | solution.py:429
  189.4 1.0 collective-permute-start.17
  190.4 1.1 collective-permute-done.16
  191.4 4.4 %collective-permute-done.17 = f32[8,256]{1,0:T(8,128)S(1)} collective-permute-done((f32[8,256]{1,0:T(8,128)S(1)}, f32[8,256]{1,0:T(8,128)S(1)}, u32[]{:S(2)}, u32[]{:S(2)}) %collective-permute-start.17) | collective-permute-done | bytes 8224 | tf_op jit(solution)/shard_map/ppermute | solution.py:429
  (63 shorter events, 5.5 us)
Async XLA Ops:
  0.6 36.1 %copy-start = (bf16[128,256]{1,0:T(8,128)(2,1)S(1)}, bf16[128,256]{1,0:T(8,128)(2,1)}, u32[]{:S(2)}) copy-start(bf16[128,256]{1,0:T(8,128)(2,1)} %param.18) | copy-start | bytes 196612
  0.6 35.7 %copy-start.2 = (bf16[1,1,1,512,128]{4,3,2,1,0:T(8,128)(2,1)S(1)}, bf16[1,1,1,512,128]{4,3,2,1,0:T(8,128)(2,1)}, u32[]{:S(2)}) copy-start(bf16[1,1,1,512,128]{4,3,2,1,0:T(8,128)(2,1)} %param.12) | copy-start | bytes 393220
  0.7 24.4 %copy-start.4 = (f32[8,256]{1,0:T(8,128)S(1)}, f32[8,256]{1,0:T(8,128)}, u32[]{:S(2)}) copy-start(f32[8,256]{1,0:T(8,128)} %param.21) | copy-start | bytes 24580
  0.7 35.9 %copy-start.3 = (s32[1,1,1,128,128]{4,3,2,1,0:T(8,128)S(1)}, s32[1,1,1,128,128]{4,3,2,1,0:T(8,128)}, u32[]{:S(2)}) copy-start(s32[1,1,1,128,128]{4,3,2,1,0:T(8,128)} %param.17) | copy-start | bytes 196612
  4.4 53.8 %collective-permute-start.7 = (f32[16,128]{1,0:T(8,128)S(1)}, f32[16,128]{1,0:T(8,128)S(1)}, u32[]{:S(2)}, u32[]{:S(2)}) collective-permute-start(f32[16,128]{1,0:T(8,128)S(1)} %reshape.39), channel_id=1, source_target_pairs={{32,0},{64,32},{96,64},{128,96},{160,128},{192,160},{224,192},{0,2... | collective-permute-start | bytes 24584 | tf_op jit(solution)/shard_map/ppermute | solution.py:335
  14.4 43.8 %collective-permute-start.6 = (f32[16,128]{1,0:T(8,128)S(1)}, f32[16,128]{1,0:T(8,128)S(1)}, u32[]{:S(2)}, u32[]{:S(2)}) collective-permute-start(f32[16,128]{1,0:T(8,128)S(1)} %reshape.39), channel_id=1, source_target_pairs={{0,32},{32,64},{64,96},{96,128},{128,160},{160,192},{192,224},{224... | collective-permute-start | bytes 24584 | tf_op jit(solution)/shard_map/ppermute | solution.py:335
  14.4 12.6 %collective-permute-start.1 = (bf16[512,128]{1,0:T(8,128)(2,1)}, bf16[512,128]{1,0:T(8,128)(2,1)S(1)}, u32[]{:S(2)}, u32[]{:S(2)}) collective-permute-start(bf16[512,128]{1,0:T(8,128)(2,1)} %bitcast.62), channel_id=1, source_target_pairs={{32,0},{64,32},{96,64},{128,96},{160,128},{192,160},{224,192},{0,2... | collective-permute-start | bytes 393224 | tf_op jit(solution)/shard_map/ppermute | solution.py:335
  21.9 14.4 %collective-permute-start = (bf16[512,128]{1,0:T(8,128)(2,1)}, bf16[512,128]{1,0:T(8,128)(2,1)S(1)}, u32[]{:S(2)}, u32[]{:S(2)}) collective-permute-start(bf16[512,128]{1,0:T(8,128)(2,1)} %bitcast.63), channel_id=1, source_target_pairs={{0,32},{32,64},{64,96},{96,128},{128,160},{160,192},{192,224},{224... | collective-permute-start | bytes 393224 | tf_op jit(solution)/shard_map/ppermute | solution.py:335
  36.4 10.9 %collective-permute-start.2 = (bf16[3,512,128]{2,1,0:T(8,128)(2,1)S(1)}, bf16[3,512,128]{2,1,0:T(8,128)(2,1)}, u32[]{:S(2)}, u32[]{:S(2)}) collective-permute-start(bf16[3,512,128]{2,1,0:T(8,128)(2,1)S(1)} %pad_maximum_fusion), channel_id=1, source_target_pairs={{0,1},{1,2},{2,3},{3,0},{4,5},{5,6},{6,7},{7,4},{8,9},{9,10},{10,1... | collective-permute-start | bytes 1179656 | tf_op jit(solution)/shard_map/ppermute | solution.py:335
  37.0 18.3 %collective-permute-start.3 = (bf16[3,512,128]{2,1,0:T(8,128)(2,1)S(1)}, bf16[3,512,128]{2,1,0:T(8,128)(2,1)S(1)}, u32[]{:S(2)}, u32[]{:S(2)}) collective-permute-start(bf16[3,512,128]{2,1,0:T(8,128)(2,1)S(1)} %pad_maximum_fusion), channel_id=1, source_target_pairs={{1,0},{2,1},{3,2},{0,3},{5,4},{6,5},{7,6},{4,7},{9,8},{10,9},{11,1... | collective-permute-start | bytes 1179656 | tf_op jit(solution)/shard_map/ppermute | solution.py:335
  55.3 48.7 %collective-permute-start.5 = (bf16[9,512,128]{2,1,0:T(8,128)(2,1)S(1)}, bf16[9,512,128]{2,1,0:T(8,128)(2,1)S(1)}, u32[]{:S(2)}, u32[]{:S(2)}) collective-permute-start(bf16[9,512,128]{2,1,0:T(8,128)(2,1)S(1)} %constant_dynamic-update-slice_fusion), channel_id=1, source_target_pairs={{4,0},{8,4},{12,8},{16,12},{20,16},{24,20},{28,24},{0,28},{5,1},{9... | collective-permute-start | bytes 3538952 | tf_op jit(solution)/shard_map/ppermute | solution.py:335
  57.1 46.9 %collective-permute-start.4 = (bf16[9,512,128]{2,1,0:T(8,128)(2,1)S(1)}, bf16[9,512,128]{2,1,0:T(8,128)(2,1)}, u32[]{:S(2)}, u32[]{:S(2)}) collective-permute-start(bf16[9,512,128]{2,1,0:T(8,128)(2,1)S(1)} %constant_dynamic-update-slice_fusion), channel_id=1, source_target_pairs={{0,4},{4,8},{8,12},{12,16},{16,20},{20,24},{24,28},{28,0},{1,5},{5... | collective-permute-start | bytes 3538952 | tf_op jit(solution)/shard_map/ppermute | solution.py:335
  58.3 5.0 %collective-permute-start.8 = (f32[3,16,128]{2,1,0:T(8,128)S(1)}, f32[3,16,128]{2,1,0:T(8,128)S(1)}, u32[]{:S(2)}, u32[]{:S(2)}) collective-permute-start(f32[3,16,128]{2,1,0:T(8,128)S(1)} %pad_maximum_fusion.1), channel_id=1, source_target_pairs={{0,1},{1,2},{2,3},{3,0},{4,5},{5,6},{6,7},{7,4},{8,9},{9,10},{10,1... | collective-permute-start | bytes 73736 | tf_op jit(solution)/shard_map/ppermute | solution.py:335
  60.6 3.5 %collective-permute-start.9 = (f32[3,16,128]{2,1,0:T(8,128)S(1)}, f32[3,16,128]{2,1,0:T(8,128)S(1)}, u32[]{:S(2)}, u32[]{:S(2)}) collective-permute-start(f32[3,16,128]{2,1,0:T(8,128)S(1)} %pad_maximum_fusion.1), channel_id=1, source_target_pairs={{1,0},{2,1},{3,2},{0,3},{5,4},{6,5},{7,6},{4,7},{9,8},{10,9},{11,1... | collective-permute-start | bytes 73736 | tf_op jit(solution)/shard_map/ppermute | solution.py:335
  64.2 9.1 %collective-permute-start.11 = (f32[9,16,128]{2,1,0:T(8,128)S(1)}, f32[9,16,128]{2,1,0:T(8,128)S(1)}, u32[]{:S(2)}, u32[]{:S(2)}) collective-permute-start(f32[9,16,128]{2,1,0:T(8,128)S(1)} %constant_dynamic-update-slice_fusion.5), channel_id=1, source_target_pairs={{4,0},{8,4},{12,8},{16,12},{20,16},{24,20},{28,24},{0,28},{5,1},{9... | collective-permute-start | bytes 221192 | tf_op jit(solution)/shard_map/ppermute | solution.py:335
  65.5 7.8 %collective-permute-start.10 = (f32[9,16,128]{2,1,0:T(8,128)S(1)}, f32[9,16,128]{2,1,0:T(8,128)S(1)}, u32[]{:S(2)}, u32[]{:S(2)}) collective-permute-start(f32[9,16,128]{2,1,0:T(8,128)S(1)} %constant_dynamic-update-slice_fusion.5), channel_id=1, source_target_pairs={{0,4},{4,8},{8,12},{12,16},{16,20},{20,24},{24,28},{28,0},{1,5},{5... | collective-permute-start | bytes 221192 | tf_op jit(solution)/shard_map/ppermute | solution.py:335
  73.3 30.7 %copy-start.5 = (f32[256]{0:T(256)S(1)}, f32[256]{0:T(256)}, u32[]{:S(2)}) copy-start(f32[256]{0:T(256)} %param.23) | copy-start | bytes 3076
  104.1 1.2 copy-start.1
  122.5 51.0 %collective-permute-start.12 = (f32[9,8,256]{2,1,0:T(8,128)S(1)}, f32[9,8,256]{2,1,0:T(8,128)S(1)}, u32[]{:S(2)}, u32[]{:S(2)}) collective-permute-start(f32[9,8,256]{2,1,0:T(8,128)S(1)} %get-tuple-element.6), channel_id=1, source_target_pairs={{0,4},{4,8},{8,12},{12,16},{16,20},{20,24},{24,28},{28,0},{1,5},{5... | collective-permute-start | bytes 221192 | tf_op jit(solution)/shard_map/ppermute | solution.py:429
  172.0 3.8 %collective-permute-start.13 = (f32[9,8,256]{2,1,0:T(8,128)S(1)}, f32[9,8,256]{2,1,0:T(8,128)S(1)}, u32[]{:S(2)}, u32[]{:S(2)}) collective-permute-start(f32[9,8,256]{2,1,0:T(8,128)S(1)} %get-tuple-element.7), channel_id=1, source_target_pairs={{4,0},{8,4},{12,8},{16,12},{20,16},{24,20},{28,24},{0,28},{5,1},{9... | collective-permute-start | bytes 221192 | tf_op jit(solution)/shard_map/ppermute | solution.py:429
  175.8 6.9 %collective-permute-start.14 = (f32[3,8,256]{2,1,0:T(8,128)S(1)}, f32[3,8,256]{2,1,0:T(8,128)S(1)}, u32[]{:S(2)}, u32[]{:S(2)}) collective-permute-start(f32[3,8,256]{2,1,0:T(8,128)S(1)} %get-tuple-element.14), channel_id=1, source_target_pairs={{0,1},{1,2},{2,3},{3,0},{4,5},{5,6},{6,7},{7,4},{8,9},{9,10},{10,1... | collective-permute-start | bytes 73736 | tf_op jit(solution)/shard_map/ppermute | solution.py:429
  176.7 6.1 %collective-permute-start.15 = (f32[3,8,256]{2,1,0:T(8,128)S(1)}, f32[3,8,256]{2,1,0:T(8,128)S(1)}, u32[]{:S(2)}, u32[]{:S(2)}) collective-permute-start(f32[3,8,256]{2,1,0:T(8,128)S(1)} %get-tuple-element.15), channel_id=1, source_target_pairs={{1,0},{2,1},{3,2},{0,3},{5,4},{6,5},{7,6},{4,7},{9,8},{10,9},{11,1... | collective-permute-start | bytes 73736 | tf_op jit(solution)/shard_map/ppermute | solution.py:429
  182.8 8.6 %collective-permute-start.16 = (f32[8,256]{1,0:T(8,128)S(1)}, f32[8,256]{1,0:T(8,128)S(1)}, u32[]{:S(2)}, u32[]{:S(2)}) collective-permute-start(f32[8,256]{1,0:T(8,128)S(1)} %get-tuple-element.16), channel_id=1, source_target_pairs={{0,32},{32,64},{64,96},{96,128},{128,160},{160,192},{192,224},{224... | collective-permute-start | bytes 24584 | tf_op jit(solution)/shard_map/ppermute | solution.py:429
  189.4 6.4 %collective-permute-start.17 = (f32[8,256]{1,0:T(8,128)S(1)}, f32[8,256]{1,0:T(8,128)S(1)}, u32[]{:S(2)}, u32[]{:S(2)}) collective-permute-start(f32[8,256]{1,0:T(8,128)S(1)} %get-tuple-element.17), channel_id=1, source_target_pairs={{32,0},{64,32},{96,64},{128,96},{160,128},{192,160},{224,192},{0,2... | collective-permute-start | bytes 24584 | tf_op jit(solution)/shard_map/ppermute | solution.py:429

commit v2 on v1

--- a/solution.py
+++ b/solution.py
@@ -10,7 +10,7 @@
 coulomb = 0.2
 root_pi = 1.7724538509055159
 chunk = 256
-macro_chunks = 4
+macro_chunks = 2
 macro = chunk * macro_chunks
 
 erfc_p = (
@@ -42,16 +42,50 @@
     return jnp.where(x < 1.0, 1.0 - x * poly(square, erf_t), tail)
 
 
-def geometry_kernel(coords_ref, first_ref, second_ref, mask_ref, out_ref):
+def geometry_kernel(coords_ref, first_ref, second_ref, mask_ref, out_ref, place_ref, top_ref):
     rows = 32
+    wide = 512
+    coords = jnp.concatenate([coords_ref[:, 0:8, :], coords_ref[:, 8:16, :]], axis=2)
+    coords = coords.reshape(216, 256)
+    coords_top = coords.astype(jnp.bfloat16)
+    top_ref[:, 0:256] = coords_top
+    top_ref[:, 256:512] = (coords - coords_top.astype(jnp.float32)).astype(jnp.bfloat16)
+
+    def locate(index, carry):
+        second = jnp.concatenate(
+            [second_ref[pl.ds(index * 4 + k, 1), :] for k in range(4)], axis=1
+        )
+        low = (second & 255).astype(jnp.float32).astype(jnp.bfloat16)
+        high = jnp.broadcast_to(second >> 8, (8, wide))
+        iota = lax.broadcasted_iota(jnp.int32, (256, wide), 0).astype(jnp.float32)
+        hot = jnp.where(
+            iota.astype(jnp.bfloat16) == jnp.broadcast_to(low, (256, wide)),
+            jnp.ones((), jnp.bfloat16),
+            jnp.zeros((), jnp.bfloat16),
+        )
+        found = jnp.dot(
+            top_ref[...],
+            jnp.concatenate([hot, hot], axis=0),
+            preferred_element_type=jnp.float32,
+        )
+        odd = lax.broadcasted_iota(jnp.int32, (8, wide), 0) & 1
+        total = jnp.zeros((8, wide), jnp.float32)
+        for slot in range(27):
+            hit = high == odd + 2 * slot
+            total = total + jnp.where(hit, found[slot * 8 : slot * 8 + 8], 0.0)
+        for c in range(4):
+            row = total[2 * c : 2 * c + 1] + total[2 * c + 1 : 2 * c + 2]
+            for k in range(4):
+                place_ref[c, pl.ds(index * 4 + k, 1), :] = row[:, k * 128 : k * 128 + 128]
+        return carry
+
+    lax.fori_loop(0, 32, locate, 0)
 
     def group(index, carry):
         base = pl.multiple_of(index * rows, rows)
         first = first_ref[pl.ds(base, rows), :]
         second = second_ref[pl.ds(base, rows), :]
         weight = mask_ref[pl.ds(base, rows), :].astype(jnp.float32)
-        lane_j = second & 127
-        row_j = second >> 7
         lane_i = first & 127
         row_i = first >> 7
 
@@ -59,25 +93,15 @@
             wide = jnp.broadcast_to(row, (rows, 128))
             return jnp.take_along_axis(wide, lanes, axis=1, mode="promise_in_bounds")
 
-        def scan(slot, found):
-            block = coords_ref[pl.ds(pl.multiple_of(slot * 16, 16), 16), :]
-            for part in range(4):
-                hit = row_j == slot * 4 + part
-                found = tuple(
-                    jnp.where(hit, pick(block[c * 4 + part : c * 4 + part + 1], lane_j), found[c])
-                    for c in range(4)
-                )
-            return found
-
         zeros = jnp.zeros((rows, 128), jnp.float32)
-        place_j = lax.fori_loop(0, 27, scan, (zeros,) * 4)
-        own = coords_ref[13 * 16 : 14 * 16, :]
+        place_j = [place_ref[c, pl.ds(base, rows), :] for c in range(4)]
         place_i = [zeros] * 4
         for part in range(4):
             hit = row_i == part
             for c in range(4):
+                at = (part & 1) * 8 + c * 2 + (part >> 1)
                 place_i[c] = jnp.where(
-                    hit, pick(own[c * 4 + part : c * 4 + part + 1], lane_i), place_i[c]
+                    hit, pick(coords_ref[13, at : at + 1, :], lane_i), place_i[c]
                 )
         slot = second >> 9
         step_x = (slot * 57) >> 9
@@ -105,8 +129,8 @@
             weight * coulomb * place_i[3] * place_j[3] * slope_coul * inverse,
             weight * coulomb * place_j[3] * potential,
             weight * coulomb * place_i[3] * potential,
-            jnp.where(first < 256, first, 512).astype(jnp.float32),
-            jnp.where(first < 256, 512, first - 256).astype(jnp.float32),
+            (first & 255).astype(jnp.float32),
+            (first >> 8).astype(jnp.float32),
             (second & 255).astype(jnp.float32),
             (second >> 8).astype(jnp.float32),
         )
@@ -122,6 +146,10 @@
     return pl.pallas_call(
         geometry_kernel,
         out_shape=jax.ShapeDtypeStruct((128, 16, 128), jnp.float32),
+        scratch_shapes=[
+            pltpu.VMEM((4, 128, 128), jnp.float32),
+            pltpu.VMEM((216, 512), jnp.bfloat16),
+        ],
         name="geometry",
     )(coords, first, second, mask)
 
@@ -133,9 +161,7 @@
     mid_ref,
     high_ref,
     geo_ref,
-    centre_ref,
-    neighbour_ref,
-    radial_ref,
+    first_ref,
     hidden_ref,
     hidden_t_ref,
     energy_ref,
@@ -145,9 +171,11 @@
     out_high,
     stage_ref,
     table_ref,
-    gather_ref,
+    gather_a,
+    gather_b,
+    half_a,
+    half_b,
     iota_ref,
-    hot_ref,
     term_ref,
     acc_i_ref,
     acc_j_ref,
@@ -159,9 +187,14 @@
     ]
     for copy in copies:
         copy.start()
-    iota_ref[...] = lax.broadcasted_iota(jnp.int32, (256, 128), 0).astype(jnp.float32).astype(jnp.bfloat16)
+    one = jnp.ones((), jnp.bfloat16)
+    zero = jnp.zeros((), jnp.bfloat16)
+    iota_ref[...] = (
+        lax.broadcasted_iota(jnp.int32, (256, 128), 0).astype(jnp.float32).astype(jnp.bfloat16)
+    )
     acc_i_ref[...] = jnp.zeros_like(acc_i_ref)
     acc_j_ref[...] = jnp.zeros_like(acc_j_ref)
+    term_ref[...] = jnp.zeros_like(term_ref)
     for k in range(3):
         copies[k].wait()
 
@@ -174,53 +207,52 @@
 
         lax.fori_loop(0, 36, widen, 0)
 
-    def fetch(index):
+    def fetch(index, gather_ref):
+        index = jnp.minimum(index, 63)
         for p in range(chunk):
             row = rows_ref[index * 2 + p // 128, p % 128]
             gather_ref[pl.ds(p, 1), :] = table_ref[pl.ds(row, 1), :]
 
-    def wide(row):
-        return jnp.broadcast_to(row.astype(jnp.bfloat16), (256, chunk))
-
-    def one_hot(row):
-        iota = jnp.concatenate([iota_ref[...]] * (chunk // 128), axis=1)
+    def geo_of(index, count):
+        return jnp.concatenate([geo_ref[index + k] for k in range(count)], axis=1)
+
+    def equal(rows, row):
+        width = row.shape[1]
+        iota = jnp.concatenate([iota_ref[0:rows, :]] * (width // 128), axis=1)
         return jnp.where(
-            iota == wide(row), jnp.ones((), jnp.bfloat16), jnp.zeros((), jnp.bfloat16)
-        )
-
-    def step(part, first_chunk):
-        index = first_chunk + part
-        lanes = pl.ds(pl.multiple_of(part * chunk, chunk), chunk)
-        geo = jnp.concatenate([geo_ref[index * 2], geo_ref[index * 2 + 1]], axis=1)
-        features = gather_ref[...].astype(jnp.bfloat16)
-        fetch(jnp.minimum(index + 1, 63))
-        distance = geo[3:4]
+            iota == jnp.broadcast_to(row.astype(jnp.bfloat16), (rows, width)), one, zero
+        )
+
+    def basis_of(distance):
         offset = distance - (
             0.25 + 0.3 * lax.broadcasted_iota(jnp.int32, (8, chunk), 0).astype(jnp.float32)
         )
-        basis = jnp.exp(-(offset / spread) * (offset / spread))
-        basis_slope = basis * offset * (-2.0 / (spread * spread))
+        return offset, jnp.exp(-(offset / spread) * (offset / spread))
+
+    def enter(index, gather_ref, half_ref):
+        geo = geo_of(jnp.minimum(index, 63) * 2, 2)
+        offset, basis = basis_of(geo[3:4])
         top = basis.astype(jnp.bfloat16).astype(jnp.float32)
-        basis_parts = jnp.concatenate([top, top, basis - top, jnp.zeros_like(top)], axis=0)
-        hot_low = one_hot(geo[8:9])
-        hot_high = one_hot(geo[9:10])
-        hot_ref[0:256, lanes] = hot_low
-        hot_ref[256:512, lanes] = hot_high
-        half_one = (
-            jnp.dot(centre_ref[:, 0:256], hot_low, preferred_element_type=jnp.float32)
-            + jnp.dot(centre_ref[:, 256:512], hot_high, preferred_element_type=jnp.float32)
-            + lax.dot_general(
-                neighbour_ref[...],
-                features,
-                (((1,), (1,)), ((), ())),
-                preferred_element_type=jnp.float32,
-            )
-            + jnp.dot(
-                radial_ref[...],
-                basis_parts.astype(jnp.bfloat16),
-                preferred_element_type=jnp.float32,
-            )
-        )
+        low = geo[8:9]
+        side = geo[9:10]
+        operand = jnp.concatenate(
+            [
+                equal(256, jnp.where(side == 0.0, low, 512.0)),
+                equal(256, jnp.where(side == 0.0, 512.0, low)),
+                gather_ref[...].T.astype(jnp.bfloat16),
+                jnp.concatenate([top, top, basis - top, jnp.zeros_like(top)], axis=0).astype(
+                    jnp.bfloat16
+                ),
+                jnp.zeros((96, chunk), jnp.bfloat16),
+            ],
+            axis=0,
+        )
+        half_ref[...] = jnp.dot(first_ref[...], operand, preferred_element_type=jnp.float32)
+
+    def leave(index, part, half_ref):
+        lanes = slice(part * chunk, part * chunk + chunk)
+        geo = geo_of(index * 2, 2)
+        half_one = half_ref[...]
         bend_one = jnp.tanh(half_one)
         gain_one = 1.0 + bend_one
         act_one = half_one * gain_one
@@ -241,64 +273,81 @@
         back_basis = jnp.dot(
             back_ref[...], back_one.astype(jnp.bfloat16), preferred_element_type=jnp.float32
         )
+        distance = geo[3:4]
+        offset, basis = basis_of(distance)
         total = jnp.sum(
-            (back_basis[0:8] + back_basis[8:16]) * basis_slope, axis=0, keepdims=True
+            (back_basis[0:8] + back_basis[8:16])
+            * (basis * offset * (-2.0 / (spread * spread))),
+            axis=0,
+            keepdims=True,
         ) - (readout * distance)
         push = geo[4:5] * total + geo[5:6]
         term_ref[0:3, lanes] = geo[0:3] * push
         term_ref[3:5, lanes] = geo[6:8]
-        return first_chunk
-
-    fetch(0)
-
-    def block(index, carry):
-        lax.fori_loop(0, macro_chunks, step, index * macro_chunks)
+
+    def deposit(index):
+        width = 2 * chunk
+        geo = geo_of(jnp.maximum(index, 0) * 4, 4)
         terms = term_ref[...]
-        push = terms[0:3]
-        own = jnp.concatenate([push, terms[3:4], jnp.zeros((4, macro), jnp.float32)], axis=0)
+        own = terms[0:4]
         own_top = own.astype(jnp.bfloat16).astype(jnp.float32)
-        own_parts = jnp.concatenate([own_top, own - own_top], axis=0).astype(jnp.bfloat16)
-        acc_i_ref[...] += lax.dot_general(
-            own_parts, hot_ref[...], (((1,), (1,)), ((), ())), preferred_element_type=jnp.float32
-        )
-        far = jnp.concatenate([-push, terms[4:5]], axis=0)
-        far_top = far.astype(jnp.bfloat16)
-        far_rest = (far - far_top.astype(jnp.float32)).astype(jnp.bfloat16)
-        geo = jnp.concatenate([geo_ref[index * 2 * macro_chunks + k] for k in range(macro // 128)], axis=1)
-        iota = jnp.concatenate([iota_ref[...]] * (macro // 128), axis=1)
-        one = jnp.ones((), jnp.bfloat16)
-        zero = jnp.zeros((), jnp.bfloat16)
-        hot = jnp.where(
-            iota == jnp.broadcast_to(geo[10:11].astype(jnp.bfloat16), (256, macro)), one, zero
-        )
-        block_hit = jnp.where(
-            iota[0:64] == jnp.broadcast_to(geo[11:12].astype(jnp.bfloat16), (64, macro)), one, zero
-        )
-        spread_rows = jnp.concatenate(
+        own_rest = own - own_top
+        side = geo[9:10]
+        own_rows = jnp.concatenate(
             [
-                block_hit * jnp.broadcast_to(part[c : c + 1], (64, macro))
-                for c in range(4)
-                for part in (far_top, far_rest)
+                jnp.where(side == half, part, 0.0)
+                for half in (0.0, 1.0)
+                for part in (own_top, own_rest)
             ],
             axis=0,
+        ).astype(jnp.bfloat16)
+        acc_i_ref[...] += lax.dot_general(
+            own_rows,
+            equal(256, geo[8:9]),
+            (((1,), (1,)), ((), ())),
+            preferred_element_type=jnp.float32,
+        )
+        far = jnp.concatenate([-terms[0:3], terms[4:5]], axis=0).astype(jnp.bfloat16)
+        hit = equal(64, geo[11:12])
+        far_rows = jnp.concatenate(
+            [hit * jnp.broadcast_to(far[c : c + 1], (64, width)) for c in range(4)], axis=0
         )
         acc_j_ref[...] += lax.dot_general(
-            spread_rows, hot, (((1,), (1,)), ((), ())), preferred_element_type=jnp.float32
-        )
+            far_rows,
+            equal(256, geo[10:11]),
+            (((1,), (1,)), ((), ())),
+            preferred_element_type=jnp.float32,
+        )
+
+    fetch(0, gather_a)
+    enter(0, gather_a, half_a)
+    fetch(1, gather_b)
+
+    def block(index, carry):
+        first = index * 2
+        deposit(index - 1)
+        enter(first + 1, gather_b, half_b)
+        leave(first, 0, half_a)
+        fetch(first + 2, gather_a)
+        enter(first + 2, gather_a, half_a)
+        leave(first + 1, 1, half_b)
+        fetch(first + 3, gather_b)
         return carry
 
-    lax.fori_loop(0, blocks_ref[0], block, 0)
+    blocks = blocks_ref[0]
+    lax.fori_loop(0, blocks, block, 0)
+    deposit(blocks - 1)
     acc_i = acc_i_ref[...]
-    acc_i = acc_i[0:8] + acc_i[8:16]
+    acc_i = jnp.concatenate([acc_i[0:4] + acc_i[4:8], acc_i[8:12] + acc_i[12:16]], axis=0)
     for c in range(4):
-        plane = acc_j_ref[c * 128 : c * 128 + 64, :] + acc_j_ref[c * 128 + 64 : c * 128 + 128, :]
+        plane = acc_j_ref[c * 64 : c * 64 + 64, :]
         for slot in range(27):
             step_x, step_y, step_z = slot // 9, slot // 3 % 3, slot % 3
             target = (out_low, out_mid, out_high)[step_y]
             for half in range(2):
                 row = plane[slot * 2 + half : slot * 2 + half + 1]
                 if slot == 13:
-                    row = row + acc_i[c : c + 1, half * 256 : half * 256 + 256]
+                    row = row + acc_i[half * 4 + c : half * 4 + c + 1]
                 target[step_z * 3 + step_x, c * 2 + half : c * 2 + half + 1, :] = row
 
 
@@ -310,17 +359,19 @@
     return pl.pallas_call(
         pair_kernel,
         out_shape=(out, out, out),
-        in_specs=[smem, smem, far, far, far, vmem] + [vmem] * 7,
+        in_specs=[smem, smem, far, far, far, vmem] + [vmem] * 5,
         out_specs=(vmem, vmem, vmem),
         scratch_shapes=[
             pltpu.VMEM((3, 4608, 128), jnp.bfloat16),
             pltpu.VMEM((13824, 128), jnp.float32),
             pltpu.VMEM((chunk, 128), jnp.float32),
+            pltpu.VMEM((chunk, 128), jnp.float32),
+            pltpu.VMEM((256, chunk), jnp.float32),
+            pltpu.VMEM((256, chunk), jnp.float32),
             pltpu.VMEM((256, 128), jnp.bfloat16),
-            pltpu.VMEM((512, macro), jnp.bfloat16),
-            pltpu.VMEM((8, macro), jnp.float32),
-            pltpu.VMEM((16, 512), jnp.float32),
-            pltpu.VMEM((512, 256), jnp.float32),
+            pltpu.VMEM((8, 2 * chunk), jnp.float32),
+            pltpu.VMEM((16, 256), jnp.float32),
+            pltpu.VMEM((256, 256), jnp.float32),
             pltpu.SemaphoreType.DMA((3,)),
         ],
         compiler_params=pltpu.CompilerParams(vmem_limit_bytes=48 * 1024 * 1024),
@@ -366,10 +417,12 @@
     )
     back = jnp.concatenate([radial_top, radial_rest], axis=0).astype(jnp.bfloat16)
     energy = jnp.broadcast_to(w_energy[:, None], (w_energy.shape[0], 128))
+    first = jnp.concatenate(
+        [centre_t, w_neighbour.T * half, radial_t, jnp.zeros((radial_t.shape[0], 96), jnp.bfloat16)],
+        axis=1,
+    )
     return (
-        centre_t,
-        w_neighbour.T * half,
-        radial_t,
+        first,
         w_hidden * half,
         w_hidden.T * half,
         energy,
@@ -398,7 +451,8 @@
     alive_slot = jnp.arange(atom_slots, dtype=jnp.int32) < filled
     average = jnp.sum(jnp.where(alive_slot, raw_charge, 0.0)) / filled.astype(jnp.float32)
     charges = jnp.where(alive_slot, raw_charge - average, 0.0)
-    coords_own = jnp.concatenate([positions[0, 0, 0], charges[None, :]], axis=0).reshape(16, 128)
+    coords_own = jnp.concatenate([positions[0, 0, 0], charges[None, :]], axis=0)
+    coords_own = coords_own.reshape(8, 2, 128).transpose(1, 0, 2).reshape(16, 128)
 
     def collect(block):
         low, high = swap(block, "gx")
@@ -411,7 +465,7 @@
     near_coords = jnp.stack(collect(coords_own), axis=0)
     low, mid, high = [part.reshape(9 * atom_slots, -1) for part in collect(own_feat)]
     coords_all = (
-        near_coords.reshape(3, 3, 3, 16, 128).transpose(2, 0, 1, 3, 4).reshape(27 * 16, 128)
+        near_coords.reshape(3, 3, 3, 16, 128).transpose(2, 0, 1, 3, 4).reshape(27, 16, 128)
     )
     first_tab = pair_first[0, 0, 0]
     second_tab = pair_second[0, 0, 0]

time: 198 us -> 156 us (0.79)
  the two profiles are of different devices: /device:TPU:1 before, /device:TPU:2 now
where the time goes in v2:
time: 156 us; the launch traced here: 155 us
  Pallas kernels  53 us (34%)
  starting transfers between devices  46.9 us (30%)
  waiting for transfers between devices  41 us (26%)
  local copies, waits for them, and re-layouts  6.45 us (4%)
  between operations  2.92 us (2%)
  other arithmetic  2.51 us (2%)
  matrix products  2.22 us (1%)
    pallas_call x1, Pallas kernels, pair_sums(): pl.pallas_call(pair_kernel, out_shape=(out, out, out), in_specs=[smem, sm...  40.2 us
    ppermute x6, waiting for transfers between devices, swap(): lax.ppermute(block, axis, backward)  17.7 us
    ppermute x6, starting transfers between devices, swap(): lax.ppermute(block, axis, backward)  16.3 us
    pallas_call x1, Pallas kernels, geometry(): pl.pallas_call(geometry_kernel, out_shape=jax.ShapeDtypeStruct((128, 16,...  12.9 us
    ppermute x3, starting transfers between devices, give(): lax.ppermute(high, axis, forward)  12.6 us
    ppermute x6, starting transfers between devices, swap(): lax.ppermute(block, axis, forward)  12.6 us
    ppermute x6, waiting for transfers between devices, swap(): lax.ppermute(block, axis, forward)  12.4 us
    ppermute x3, waiting for transfers between devices, give(): lax.ppermute(low, axis, backward)  5.58 us
  transfers between devices with their start and end apart: 18, of which 12 were waited for; matrix products, arithmetic and copies ran while one was open for 4% of the time, Pallas kernels for 8%

profile of v2, /device:TPU:2, one launch (start us, length us, event | category | flops | bytes accessed | tf_op | source)
XLA Modules:
  0.0 155.1 jit_solution(10349491298538520384)
XLA Ops:
  2.0 1.0 fusion.16
  4.4 7.3 %collective-permute-start.6 = (f32[16,128]{1,0:T(8,128)S(1)}, f32[16,128]{1,0:T(8,128)S(1)}, u32[]{:S(2)}, u32[]{:S(2)}) collective-permute-start(f32[16,128]{1,0:T(8,128)S(1)} %bitcast.88), channel_id=1, source_target_pairs={{0,32},{32,64},{64,96},{96,128},{128,160},{160,192},{192,224},{224... | collective-permute-start | bytes 24584 | tf_op jit(solution)/shard_map/ppermute | solution.py:386
  11.7 5.8 %collective-permute-start.1 = (bf16[512,128]{1,0:T(8,128)(2,1)}, bf16[512,128]{1,0:T(8,128)(2,1)S(1)}, u32[]{:S(2)}, u32[]{:S(2)}) collective-permute-start(bf16[512,128]{1,0:T(8,128)(2,1)} %bitcast.70), channel_id=1, source_target_pairs={{32,0},{64,32},{96,64},{128,96},{160,128},{192,160},{224,192},{0,2... | collective-permute-start | bytes 393224 | tf_op jit(solution)/shard_map/ppermute | solution.py:386
  17.8 0.7 fusion.13
  18.7 1.0 copy.28
  19.7 1.0 copy.30
  20.8 1.2 fusion
  22.1 3.0 %collective-permute-done.1 = bf16[512,128]{1,0:T(8,128)(2,1)S(1)} collective-permute-done((bf16[512,128]{1,0:T(8,128)(2,1)}, bf16[512,128]{1,0:T(8,128)(2,1)S(1)}, u32[]{:S(2)}, u32[]{:S(2)}) %collective-permute-start.1) | collective-permute-done | bytes 131104 | tf_op jit(solution)/shard_map/ppermute | solution.py:386
  25.1 3.5 %collective-permute-done = bf16[512,128]{1,0:T(8,128)(2,1)S(1)} collective-permute-done((bf16[512,128]{1,0:T(8,128)(2,1)}, bf16[512,128]{1,0:T(8,128)(2,1)S(1)}, u32[]{:S(2)}, u32[]{:S(2)}) %collective-permute-start) | collective-permute-done | bytes 131104 | tf_op jit(solution)/shard_map/ppermute | solution.py:386
  28.7 4.0 %collective-permute-start.2 = (bf16[3,512,128]{2,1,0:T(8,128)(2,1)S(1)}, bf16[3,512,128]{2,1,0:T(8,128)(2,1)S(1)}, u32[]{:S(2)}, u32[]{:S(2)}) collective-permute-start(bf16[3,512,128]{2,1,0:T(8,128)(2,1)S(1)} %pad_maximum_fusion), channel_id=1, source_target_pairs={{0,1},{1,2},{2,3},{3,0},{4,5},{5,6},{6,7},{7,4},{8,9},{9,10},{10,1... | collective-permute-start | bytes 1179656 | tf_op jit(solution)/shard_map/ppermute | solution.py:386
  32.9 1.3 collective-permute-start.8
  34.2 2.6 %collective-permute-start.3 = (bf16[3,512,128]{2,1,0:T(8,128)(2,1)S(1)}, bf16[3,512,128]{2,1,0:T(8,128)(2,1)S(1)}, u32[]{:S(2)}, u32[]{:S(2)}) collective-permute-start(bf16[3,512,128]{2,1,0:T(8,128)(2,1)S(1)} %pad_maximum_fusion), channel_id=1, source_target_pairs={{1,0},{2,1},{3,2},{0,3},{5,4},{6,5},{7,6},{4,7},{9,8},{10,9},{11,1... | collective-permute-start | bytes 1179656 | tf_op jit(solution)/shard_map/ppermute | solution.py:386
  36.8 5.7 %collective-permute-done.2 = bf16[3,512,128]{2,1,0:T(8,128)(2,1)S(1)} collective-permute-done((bf16[3,512,128]{2,1,0:T(8,128)(2,1)S(1)}, bf16[3,512,128]{2,1,0:T(8,128)(2,1)S(1)}, u32[]{:S(2)}, u32[]{:S(2)}) %collective-permute-start.2) | collective-permute-done | bytes 393248 | tf_op jit(solution)/shard_map/ppermute | solution.py:386
  42.7 6.9 %collective-permute-done.3 = bf16[3,512,128]{2,1,0:T(8,128)(2,1)S(1)} collective-permute-done((bf16[3,512,128]{2,1,0:T(8,128)(2,1)S(1)}, bf16[3,512,128]{2,1,0:T(8,128)(2,1)S(1)}, u32[]{:S(2)}, u32[]{:S(2)}) %collective-permute-start.3) | collective-permute-done | bytes 393248 | tf_op jit(solution)/shard_map/ppermute | solution.py:386
  49.6 2.5 %collective-permute-start.5 = (bf16[9,512,128]{2,1,0:T(8,128)(2,1)S(1)}, bf16[9,512,128]{2,1,0:T(8,128)(2,1)S(1)}, u32[]{:S(2)}, u32[]{:S(2)}) collective-permute-start(bf16[9,512,128]{2,1,0:T(8,128)(2,1)S(1)} %constant_dynamic-update-slice_fusion), channel_id=1, source_target_pairs={{4,0},{8,4},{12,8},{16,12},{20,16},{24,20},{28,24},{0,28},{5,1},{9... | collective-permute-start | bytes 3538952 | tf_op jit(solution)/shard_map/ppermute | solution.py:386
  53.6 3.1 %collective-permute-start.9 = (f32[3,16,128]{2,1,0:T(8,128)S(1)}, f32[3,16,128]{2,1,0:T(8,128)S(1)}, u32[]{:S(2)}, u32[]{:S(2)}) collective-permute-start(f32[3,16,128]{2,1,0:T(8,128)S(1)} %pad_maximum_fusion.1), channel_id=1, source_target_pairs={{1,0},{2,1},{3,2},{0,3},{5,4},{6,5},{7,6},{4,7},{9,8},{10,9},{11,1... | collective-permute-start | bytes 73736 | tf_op jit(solution)/shard_map/ppermute | solution.py:386
  56.6 1.5 collective-permute-done.9
  58.1 2.2 %collective-permute-start.11 = (f32[9,16,128]{2,1,0:T(8,128)S(1)}, f32[9,16,128]{2,1,0:T(8,128)S(1)}, u32[]{:S(2)}, u32[]{:S(2)}) collective-permute-start(f32[9,16,128]{2,1,0:T(8,128)S(1)} %constant_dynamic-update-slice_fusion.5), channel_id=1, source_target_pairs={{4,0},{8,4},{12,8},{16,12},{20,16},{24,20},{28,24},{0,28},{5,1},{9... | collective-permute-start | bytes 221192 | tf_op jit(solution)/shard_map/ppermute | solution.py:386
  60.3 6.3 %collective-permute-done.11 = f32[9,16,128]{2,1,0:T(8,128)S(1)} collective-permute-done((f32[9,16,128]{2,1,0:T(8,128)S(1)}, f32[9,16,128]{2,1,0:T(8,128)S(1)}, u32[]{:S(2)}, u32[]{:S(2)}) %collective-permute-start.11) | collective-permute-done | bytes 73760 | tf_op jit(solution)/shard_map/ppermute | solution.py:386
  66.6 3.1 %collective-permute-done.10 = f32[9,16,128]{2,1,0:T(8,128)S(1)} collective-permute-done((f32[9,16,128]{2,1,0:T(8,128)S(1)}, f32[9,16,128]{2,1,0:T(8,128)S(1)}, u32[]{:S(2)}, u32[]{:S(2)}) %collective-permute-start.10) | collective-permute-done | bytes 73760 | tf_op jit(solution)/shard_map/ppermute | solution.py:386
  70.5 12.9 %geometry.1.geo_ref = f32[128,16,128]{2,1,0:T(8,128)} custom-call(f32[27,16,128]{2,1,0:T(8,128)} %bitcast.73, s32[128,128]{1,0:T(8,128)} %bitcast.83, s32[128,128]{1,0:T(8,128)} %bitcast.77, s32[128,128]{1,0:T(8,128)} %bitcast.76), custom_call_target="tpu_custom_call" | custom-call | tf_op jit(solution)/shard_map/geometry/pallas_call | solution.py:146
  83.5 1.2 copy-done.1
  84.7 40.2 %pairs.1 = (f32[9,8,256]{2,1,0:T(8,128)S(1)}, f32[9,8,256]{2,1,0:T(8,128)S(1)}, f32[9,8,256]{2,1,0:T(8,128)S(1)}) custom-call(s32[1]{0:T(128)} %bitcast.1.blocks_ref, s32[128,128]{1,0:T(8,128)S(1)} %fusion.6.rows_ref, bf16[4608,128]{1,0:T(8,128)(2,1)} %bitcast.7.low_ref, bf16[4608,128]{1,0:T(8,128)(2,1)S(1)} %bitcast.68, bf16[4608,128]{1,0:T(8,128)(2,1)S(1)} %bitcast.69, ...), custom_call_target="tpu_custom_call" | custom-call | tf_op jit(solution)/shard_map/pairs/pallas_call | solution.py:359
  124.9 2.9 %collective-permute-start.13 = (f32[9,8,256]{2,1,0:T(8,128)S(1)}, f32[9,8,256]{2,1,0:T(8,128)S(1)}, u32[]{:S(2)}, u32[]{:S(2)}) collective-permute-start(f32[9,8,256]{2,1,0:T(8,128)S(1)} %get-tuple-element.7), channel_id=1, source_target_pairs={{4,0},{8,4},{12,8},{16,12},{20,16},{24,20},{28,24},{0,28},{5,1},{9... | collective-permute-start | bytes 221192 | tf_op jit(solution)/shard_map/ppermute | solution.py:483
  127.8 2.0 %collective-permute-done.12 = f32[9,8,256]{2,1,0:T(8,128)S(1)} collective-permute-done((f32[9,8,256]{2,1,0:T(8,128)S(1)}, f32[9,8,256]{2,1,0:T(8,128)S(1)}, u32[]{:S(2)}, u32[]{:S(2)}) %collective-permute-start.12) | collective-permute-done | bytes 73760 | tf_op jit(solution)/shard_map/ppermute | solution.py:483
  129.9 7.7 %collective-permute-start.14 = (f32[3,8,256]{2,1,0:T(8,128)S(1)}, f32[3,8,256]{2,1,0:T(8,128)S(1)}, u32[]{:S(2)}, u32[]{:S(2)}) collective-permute-start(f32[3,8,256]{2,1,0:T(8,128)S(1)} %get-tuple-element.16), channel_id=1, source_target_pairs={{0,1},{1,2},{2,3},{3,0},{4,5},{5,6},{6,7},{7,4},{8,9},{9,10},{10,1... | collective-permute-start | bytes 73736 | tf_op jit(solution)/shard_map/ppermute | solution.py:483
  138.1 1.7 %collective-permute-done.14 = f32[3,8,256]{2,1,0:T(8,128)S(1)} collective-permute-done((f32[3,8,256]{2,1,0:T(8,128)S(1)}, f32[3,8,256]{2,1,0:T(8,128)S(1)}, u32[]{:S(2)}, u32[]{:S(2)}) %collective-permute-start.14) | collective-permute-done | bytes 24608 | tf_op jit(solution)/shard_map/ppermute | solution.py:483
  139.8 1.6 %collective-permute-done.15 = f32[3,8,256]{2,1,0:T(8,128)S(1)} collective-permute-done((f32[3,8,256]{2,1,0:T(8,128)S(1)}, f32[3,8,256]{2,1,0:T(8,128)S(1)}, u32[]{:S(2)}, u32[]{:S(2)}) %collective-permute-start.15) | collective-permute-done | bytes 24608 | tf_op jit(solution)/shard_map/ppermute | solution.py:483
  141.4 4.9 %collective-permute-start.16 = (f32[8,256]{1,0:T(8,128)S(1)}, f32[8,256]{1,0:T(8,128)S(1)}, u32[]{:S(2)}, u32[]{:S(2)}) collective-permute-start(f32[8,256]{1,0:T(8,128)S(1)} %get-tuple-element.18), channel_id=1, source_target_pairs={{0,32},{32,64},{64,96},{96,128},{128,160},{160,192},{192,224},{224... | collective-permute-start | bytes 24584 | tf_op jit(solution)/shard_map/ppermute | solution.py:483
  146.4 2.0 %collective-permute-start.17 = (f32[8,256]{1,0:T(8,128)S(1)}, f32[8,256]{1,0:T(8,128)S(1)}, u32[]{:S(2)}, u32[]{:S(2)}) collective-permute-start(f32[8,256]{1,0:T(8,128)S(1)} %get-tuple-element.19), channel_id=1, source_target_pairs={{32,0},{64,32},{96,64},{128,96},{160,128},{192,160},{224,192},{0,2... | collective-permute-start | bytes 24584 | tf_op jit(solution)/shard_map/ppermute | solution.py:483
  148.3 1.6 %collective-permute-done.16 = f32[8,256]{1,0:T(8,128)S(1)} collective-permute-done((f32[8,256]{1,0:T(8,128)S(1)}, f32[8,256]{1,0:T(8,128)S(1)}, u32[]{:S(2)}, u32[]{:S(2)}) %collective-permute-start.16) | collective-permute-done | bytes 8224 | tf_op jit(solution)/shard_map/ppermute | solution.py:483
  150.0 4.0 %collective-permute-done.17 = f32[8,256]{1,0:T(8,128)S(1)} collective-permute-done((f32[8,256]{1,0:T(8,128)S(1)}, f32[8,256]{1,0:T(8,128)S(1)}, u32[]{:S(2)}, u32[]{:S(2)}) %collective-permute-start.17) | collective-permute-done | bytes 8224 | tf_op jit(solution)/shard_map/ppermute | solution.py:483
  (66 shorter events, 5.8 us)
Async XLA Ops:
  0.6 20.1 %copy-start = (bf16[128,256]{1,0:T(8,128)(2,1)S(1)}, bf16[128,256]{1,0:T(8,128)(2,1)}, u32[]{:S(2)}) copy-start(bf16[128,256]{1,0:T(8,128)(2,1)} %param.18) | copy-start | bytes 196612
  4.3 24.3 %copy-start.2 = (bf16[1,1,1,512,128]{4,3,2,1,0:T(8,128)(2,1)S(1)}, bf16[1,1,1,512,128]{4,3,2,1,0:T(8,128)(2,1)}, u32[]{:S(2)}) copy-start(bf16[1,1,1,512,128]{4,3,2,1,0:T(8,128)(2,1)} %param.12) | copy-start | bytes 393220
  4.4 28.5 %collective-permute-start.6 = (f32[16,128]{1,0:T(8,128)S(1)}, f32[16,128]{1,0:T(8,128)S(1)}, u32[]{:S(2)}, u32[]{:S(2)}) collective-permute-start(f32[16,128]{1,0:T(8,128)S(1)} %bitcast.88), channel_id=1, source_target_pairs={{0,32},{32,64},{64,96},{96,128},{128,160},{160,192},{192,224},{224... | collective-permute-start | bytes 24584 | tf_op jit(solution)/shard_map/ppermute | solution.py:386
  11.7 21.2 %collective-permute-start.7 = (f32[16,128]{1,0:T(8,128)S(1)}, f32[16,128]{1,0:T(8,128)S(1)}, u32[]{:S(2)}, u32[]{:S(2)}) collective-permute-start(f32[16,128]{1,0:T(8,128)S(1)} %bitcast.89), channel_id=1, source_target_pairs={{32,0},{64,32},{96,64},{128,96},{160,128},{192,160},{224,192},{0,2... | collective-permute-start | bytes 24584 | tf_op jit(solution)/shard_map/ppermute | solution.py:386
  11.7 13.3 %collective-permute-start.1 = (bf16[512,128]{1,0:T(8,128)(2,1)}, bf16[512,128]{1,0:T(8,128)(2,1)S(1)}, u32[]{:S(2)}, u32[]{:S(2)}) collective-permute-start(bf16[512,128]{1,0:T(8,128)(2,1)} %bitcast.70), channel_id=1, source_target_pairs={{32,0},{64,32},{96,64},{128,96},{160,128},{192,160},{224,192},{0,2... | collective-permute-start | bytes 393224 | tf_op jit(solution)/shard_map/ppermute | solution.py:386
  17.6 11.0 %collective-permute-start = (bf16[512,128]{1,0:T(8,128)(2,1)}, bf16[512,128]{1,0:T(8,128)(2,1)S(1)}, u32[]{:S(2)}, u32[]{:S(2)}) collective-permute-start(bf16[512,128]{1,0:T(8,128)(2,1)} %bitcast.71), channel_id=1, source_target_pairs={{0,32},{32,64},{64,96},{96,128},{128,160},{160,192},{192,224},{224... | collective-permute-start | bytes 393224 | tf_op jit(solution)/shard_map/ppermute | solution.py:386
  20.7 11.9 %copy-start.4 = (s32[1,1,1,128,128]{4,3,2,1,0:T(8,128)S(1)}, s32[1,1,1,128,128]{4,3,2,1,0:T(8,128)}, u32[]{:S(2)}) copy-start(s32[1,1,1,128,128]{4,3,2,1,0:T(8,128)} %param.16) | copy-start | bytes 196612
  20.7 12.0 %copy-start.3 = (s32[1,1,1,128,128]{4,3,2,1,0:T(8,128)S(1)}, s32[1,1,1,128,128]{4,3,2,1,0:T(8,128)}, u32[]{:S(2)}) copy-start(s32[1,1,1,128,128]{4,3,2,1,0:T(8,128)} %param.17) | copy-start | bytes 196612
  28.7 13.9 %collective-permute-start.2 = (bf16[3,512,128]{2,1,0:T(8,128)(2,1)S(1)}, bf16[3,512,128]{2,1,0:T(8,128)(2,1)S(1)}, u32[]{:S(2)}, u32[]{:S(2)}) collective-permute-start(bf16[3,512,128]{2,1,0:T(8,128)(2,1)S(1)} %pad_maximum_fusion), channel_id=1, source_target_pairs={{0,1},{1,2},{2,3},{3,0},{4,5},{5,6},{6,7},{7,4},{8,9},{9,10},{10,1... | collective-permute-start | bytes 1179656 | tf_op jit(solution)/shard_map/ppermute | solution.py:386
  32.9 23.7 %collective-permute-start.8 = (f32[3,16,128]{2,1,0:T(8,128)S(1)}, f32[3,16,128]{2,1,0:T(8,128)S(1)}, u32[]{:S(2)}, u32[]{:S(2)}) collective-permute-start(f32[3,16,128]{2,1,0:T(8,128)S(1)} %pad_maximum_fusion.1), channel_id=1, source_target_pairs={{0,1},{1,2},{2,3},{3,0},{4,5},{5,6},{6,7},{7,4},{8,9},{9,10},{10,1... | collective-permute-start | bytes 73736 | tf_op jit(solution)/shard_map/ppermute | solution.py:386
  34.2 15.4 %collective-permute-start.3 = (bf16[3,512,128]{2,1,0:T(8,128)(2,1)S(1)}, bf16[3,512,128]{2,1,0:T(8,128)(2,1)S(1)}, u32[]{:S(2)}, u32[]{:S(2)}) collective-permute-start(bf16[3,512,128]{2,1,0:T(8,128)(2,1)S(1)} %pad_maximum_fusion), channel_id=1, source_target_pairs={{1,0},{2,1},{3,2},{0,3},{5,4},{6,5},{7,6},{4,7},{9,8},{10,9},{11,1... | collective-permute-start | bytes 1179656 | tf_op jit(solution)/shard_map/ppermute | solution.py:386
  49.6 33.7 %collective-permute-start.5 = (bf16[9,512,128]{2,1,0:T(8,128)(2,1)S(1)}, bf16[9,512,128]{2,1,0:T(8,128)(2,1)S(1)}, u32[]{:S(2)}, u32[]{:S(2)}) collective-permute-start(bf16[9,512,128]{2,1,0:T(8,128)(2,1)S(1)} %constant_dynamic-update-slice_fusion), channel_id=1, source_target_pairs={{4,0},{8,4},{12,8},{16,12},{20,16},{24,20},{28,24},{0,28},{5,1},{9... | collective-permute-start | bytes 3538952 | tf_op jit(solution)/shard_map/ppermute | solution.py:386
  52.1 31.2 %collective-permute-start.4 = (bf16[9,512,128]{2,1,0:T(8,128)(2,1)S(1)}, bf16[9,512,128]{2,1,0:T(8,128)(2,1)}, u32[]{:S(2)}, u32[]{:S(2)}) collective-permute-start(bf16[9,512,128]{2,1,0:T(8,128)(2,1)S(1)} %constant_dynamic-update-slice_fusion), channel_id=1, source_target_pairs={{0,4},{4,8},{8,12},{12,16},{16,20},{20,24},{24,28},{28,0},{1,5},{5... | collective-permute-start | bytes 3538952 | tf_op jit(solution)/shard_map/ppermute | solution.py:386
  53.6 4.6 %collective-permute-start.9 = (f32[3,16,128]{2,1,0:T(8,128)S(1)}, f32[3,16,128]{2,1,0:T(8,128)S(1)}, u32[]{:S(2)}, u32[]{:S(2)}) collective-permute-start(f32[3,16,128]{2,1,0:T(8,128)S(1)} %pad_maximum_fusion.1), channel_id=1, source_target_pairs={{1,0},{2,1},{3,2},{0,3},{5,4},{6,5},{7,6},{4,7},{9,8},{10,9},{11,1... | collective-permute-start | bytes 73736 | tf_op jit(solution)/shard_map/ppermute | solution.py:386
  58.1 8.5 %collective-permute-start.11 = (f32[9,16,128]{2,1,0:T(8,128)S(1)}, f32[9,16,128]{2,1,0:T(8,128)S(1)}, u32[]{:S(2)}, u32[]{:S(2)}) collective-permute-start(f32[9,16,128]{2,1,0:T(8,128)S(1)} %constant_dynamic-update-slice_fusion.5), channel_id=1, source_target_pairs={{4,0},{8,4},{12,8},{16,12},{20,16},{24,20},{28,24},{0,28},{5,1},{9... | collective-permute-start | bytes 221192 | tf_op jit(solution)/shard_map/ppermute | solution.py:386
  60.3 9.4 %collective-permute-start.10 = (f32[9,16,128]{2,1,0:T(8,128)S(1)}, f32[9,16,128]{2,1,0:T(8,128)S(1)}, u32[]{:S(2)}, u32[]{:S(2)}) collective-permute-start(f32[9,16,128]{2,1,0:T(8,128)S(1)} %constant_dynamic-update-slice_fusion.5), channel_id=1, source_target_pairs={{0,4},{4,8},{8,12},{12,16},{16,20},{20,24},{24,28},{28,0},{1,5},{5... | collective-permute-start | bytes 221192 | tf_op jit(solution)/shard_map/ppermute | solution.py:386
  69.8 13.6 %copy-start.5 = (f32[256]{0:T(256)S(1)}, f32[256]{0:T(256)}, u32[]{:S(2)}) copy-start(f32[256]{0:T(256)} %param.23) | copy-start | bytes 3076
  83.5 1.2 copy-start.1
  124.9 5.0 %collective-permute-start.12 = (f32[9,8,256]{2,1,0:T(8,128)S(1)}, f32[9,8,256]{2,1,0:T(8,128)S(1)}, u32[]{:S(2)}, u32[]{:S(2)}) collective-permute-start(f32[9,8,256]{2,1,0:T(8,128)S(1)} %get-tuple-element.6), channel_id=1, source_target_pairs={{0,4},{4,8},{8,12},{12,16},{16,20},{20,24},{24,28},{28,0},{1,5},{5... | collective-permute-start | bytes 221192 | tf_op jit(solution)/shard_map/ppermute | solution.py:483
  124.9 5.0 %collective-permute-start.13 = (f32[9,8,256]{2,1,0:T(8,128)S(1)}, f32[9,8,256]{2,1,0:T(8,128)S(1)}, u32[]{:S(2)}, u32[]{:S(2)}) collective-permute-start(f32[9,8,256]{2,1,0:T(8,128)S(1)} %get-tuple-element.7), channel_id=1, source_target_pairs={{4,0},{8,4},{12,8},{16,12},{20,16},{24,20},{28,24},{0,28},{5,1},{9... | collective-permute-start | bytes 221192 | tf_op jit(solution)/shard_map/ppermute | solution.py:483
  129.9 9.9 %collective-permute-start.14 = (f32[3,8,256]{2,1,0:T(8,128)S(1)}, f32[3,8,256]{2,1,0:T(8,128)S(1)}, u32[]{:S(2)}, u32[]{:S(2)}) collective-permute-start(f32[3,8,256]{2,1,0:T(8,128)S(1)} %get-tuple-element.16), channel_id=1, source_target_pairs={{0,1},{1,2},{2,3},{3,0},{4,5},{5,6},{6,7},{7,4},{8,9},{9,10},{10,1... | collective-permute-start | bytes 73736 | tf_op jit(solution)/shard_map/ppermute | solution.py:483
  137.6 3.8 %collective-permute-start.15 = (f32[3,8,256]{2,1,0:T(8,128)S(1)}, f32[3,8,256]{2,1,0:T(8,128)S(1)}, u32[]{:S(2)}, u32[]{:S(2)}) collective-permute-start(f32[3,8,256]{2,1,0:T(8,128)S(1)} %get-tuple-element.17), channel_id=1, source_target_pairs={{1,0},{2,1},{3,2},{0,3},{5,4},{6,5},{7,6},{4,7},{9,8},{10,9},{11,1... | collective-permute-start | bytes 73736 | tf_op jit(solution)/shard_map/ppermute | solution.py:483
  141.4 8.5 %collective-permute-start.16 = (f32[8,256]{1,0:T(8,128)S(1)}, f32[8,256]{1,0:T(8,128)S(1)}, u32[]{:S(2)}, u32[]{:S(2)}) collective-permute-start(f32[8,256]{1,0:T(8,128)S(1)} %get-tuple-element.18), channel_id=1, source_target_pairs={{0,32},{32,64},{64,96},{96,128},{128,160},{160,192},{192,224},{224... | collective-permute-start | bytes 24584 | tf_op jit(solution)/shard_map/ppermute | solution.py:483
  146.4 7.6 %collective-permute-start.17 = (f32[8,256]{1,0:T(8,128)S(1)}, f32[8,256]{1,0:T(8,128)S(1)}, u32[]{:S(2)}, u32[]{:S(2)}) collective-permute-start(f32[8,256]{1,0:T(8,128)S(1)} %get-tuple-element.19), channel_id=1, source_target_pairs={{32,0},{64,32},{96,64},{128,96},{160,128},{192,160},{224,192},{0,2... | collective-permute-start | bytes 24584 | tf_op jit(solution)/shard_map/ppermute | solution.py:483

commit v3 on v2

--- a/solution.py
+++ b/solution.py
@@ -9,9 +9,23 @@
 spread = 0.3
 coulomb = 0.2
 root_pi = 1.7724538509055159
-chunk = 256
-macro_chunks = 2
-macro = chunk * macro_chunks
+chunk = 512
+tiles = chunk // 128
+atoms = 512
+message = 544
+half_message = message // 2
+own_pieces = tuple((0, atoms, e * atoms) for e in range(5)) + (
+    (0, half_message, 5 * atoms),
+    (0, atoms - half_message, 5 * atoms + half_message),
+    (0, 3 * atoms, 6 * atoms),
+)
+side_pieces = ((0, 3 * atoms, 0), (0, 3 * atoms, 3 * atoms), (0, 3 * atoms, 6 * atoms))
+pieces = (
+    side_pieces
+    + tuple((begin, size, 9 * atoms + at) for begin, size, at in own_pieces)
+    + tuple((begin, size, 18 * atoms + at) for begin, size, at in side_pieces)
+)
+piece_count = len(pieces)
 
 erfc_p = (
     2.326819970068386e-2, -1.387039388740657e-1, 3.687424674597105e-1, -5.824733027278666e-1,
@@ -42,18 +56,24 @@
     return jnp.where(x < 1.0, 1.0 - x * poly(square, erf_t), tail)
 
 
-def geometry_kernel(coords_ref, first_ref, second_ref, mask_ref, out_ref, place_ref, top_ref):
+def geometry_kernel(
+    low_ref, mid_ref, high_ref, own_ref, rows_ref, first_ref, second_ref, mask_ref, out_ref,
+    place_ref, top_ref,
+):
     rows = 32
     wide = 512
-    coords = jnp.concatenate([coords_ref[:, 0:8, :], coords_ref[:, 8:16, :]], axis=2)
-    coords = coords.reshape(216, 256)
-    coords_top = coords.astype(jnp.bfloat16)
-    top_ref[:, 0:256] = coords_top
-    top_ref[:, 256:512] = (coords - coords_top.astype(jnp.float32)).astype(jnp.bfloat16)
+    for side, ref in enumerate((low_ref, mid_ref, high_ref)):
+        parts = ref[...].astype(jnp.float32)
+        for part in range(2):
+            at = part * 16
+            block = jnp.concatenate([parts[:, at : at + 8], parts[:, at + 8 : at + 16]], axis=2)
+            top_ref[side * 72 : side * 72 + 72, part * 256 : part * 256 + 256] = block.reshape(
+                72, 256
+            ).astype(jnp.bfloat16)
 
     def locate(index, carry):
         second = jnp.concatenate(
-            [second_ref[pl.ds(index * 4 + k, 1), :] for k in range(4)], axis=1
+            [rows_ref[pl.ds(index * 4 + k, 1), :] for k in range(4)], axis=1
         )
         low = (second & 255).astype(jnp.float32).astype(jnp.bfloat16)
         high = jnp.broadcast_to(second >> 8, (8, wide))
@@ -101,7 +121,7 @@
             for c in range(4):
                 at = (part & 1) * 8 + c * 2 + (part >> 1)
                 place_i[c] = jnp.where(
-                    hit, pick(coords_ref[13, at : at + 1, :], lane_i), place_i[c]
+                    hit, pick(own_ref[at : at + 1, :], lane_i), place_i[c]
                 )
         slot = second >> 9
         step_x = (slot * 57) >> 9
@@ -142,7 +162,7 @@
     out_ref[:, 12:16, :] = jnp.zeros((128, 4, 128), jnp.float32)
 
 
-def geometry(coords, first, second, mask):
+def geometry(parts, own, rows, first, second, mask):
     return pl.pallas_call(
         geometry_kernel,
         out_shape=jax.ShapeDtypeStruct((128, 16, 128), jnp.float32),
@@ -151,15 +171,22 @@
             pltpu.VMEM((216, 512), jnp.bfloat16),
         ],
         name="geometry",
-    )(coords, first, second, mask)
+    )(*parts, own, rows, first, second, mask)
 
 
 def pair_kernel(
     blocks_ref,
     rows_ref,
-    low_ref,
-    mid_ref,
-    high_ref,
+    *refs,
+):
+    sources, refs = refs[:piece_count], refs[piece_count:]
+    pair_body(blocks_ref, rows_ref, sources, *refs)
+
+
+def pair_body(
+    blocks_ref,
+    rows_ref,
+    sources,
     geo_ref,
     first_ref,
     hidden_ref,
@@ -171,20 +198,31 @@
     out_high,
     stage_ref,
     table_ref,
-    gather_a,
-    gather_b,
-    half_a,
-    half_b,
+    picks_ref,
+    gather_ref,
+    half_ref,
+    slope_ref,
     iota_ref,
     term_ref,
     acc_i_ref,
     acc_j_ref,
     sems,
 ):
-    copies = [
-        pltpu.make_async_copy(source, stage_ref.at[k], sems.at[k])
-        for k, source in enumerate((low_ref, mid_ref, high_ref))
-    ]
+    last = rows_ref.shape[0] - 1
+
+    def picks(index):
+        return pltpu.make_async_copy(
+            rows_ref.at[jnp.minimum(index, last)], picks_ref, sems.at[piece_count]
+        )
+
+    picks(0).start()
+    copies = []
+    for piece, (source, (begin, size, at)) in enumerate(zip(sources, pieces)):
+        copies.append(
+            pltpu.make_async_copy(
+                source.at[pl.ds(begin, size)], stage_ref.at[pl.ds(at, size)], sems.at[piece]
+            )
+        )
     for copy in copies:
         copy.start()
     one = jnp.ones((), jnp.bfloat16)
@@ -195,26 +233,23 @@
     acc_i_ref[...] = jnp.zeros_like(acc_i_ref)
     acc_j_ref[...] = jnp.zeros_like(acc_j_ref)
     term_ref[...] = jnp.zeros_like(term_ref)
-    for k in range(3):
-        copies[k].wait()
-
-        def widen(step, carry, k=k):
-            rows = pl.ds(pl.multiple_of(step * 128, 128), 128)
-            table_ref[pl.ds(pl.multiple_of(k * 4608 + step * 128, 128), 128), :] = stage_ref[
-                k, rows, :
-            ].astype(jnp.float32)
-            return carry
-
-        lax.fori_loop(0, 36, widen, 0)
-
-    def fetch(index, gather_ref):
-        index = jnp.minimum(index, 63)
+    for copy in copies:
+        copy.wait()
+
+    def widen(step, carry):
+        rows = pl.ds(pl.multiple_of(step * 256, 256), 256)
+        table_ref[rows, :] = stage_ref[rows, :].astype(jnp.float32)
+        return carry
+
+    lax.fori_loop(0, 54, widen, 0)
+
+    def fetch():
         for p in range(chunk):
-            row = rows_ref[index * 2 + p // 128, p % 128]
+            row = picks_ref[p // 128, p % 128]
             gather_ref[pl.ds(p, 1), :] = table_ref[pl.ds(row, 1), :]
 
-    def geo_of(index, count):
-        return jnp.concatenate([geo_ref[index + k] for k in range(count)], axis=1)
+    def geo_of(index):
+        return jnp.concatenate([geo_ref[index * tiles + k] for k in range(tiles)], axis=1)
 
     def equal(rows, row):
         width = row.shape[1]
@@ -229,8 +264,8 @@
         )
         return offset, jnp.exp(-(offset / spread) * (offset / spread))
 
-    def enter(index, gather_ref, half_ref):
-        geo = geo_of(jnp.minimum(index, 63) * 2, 2)
+    def enter(index):
+        geo = geo_of(jnp.minimum(index, last))
         offset, basis = basis_of(geo[3:4])
         top = basis.astype(jnp.bfloat16).astype(jnp.float32)
         low = geo[8:9]
@@ -249,30 +284,27 @@
         )
         half_ref[...] = jnp.dot(first_ref[...], operand, preferred_element_type=jnp.float32)
 
-    def leave(index, part, half_ref):
-        lanes = slice(part * chunk, part * chunk + chunk)
-        geo = geo_of(index * 2, 2)
+    def activate():
         half_one = half_ref[...]
         bend_one = jnp.tanh(half_one)
         gain_one = 1.0 + bend_one
         act_one = half_one * gain_one
-        slope_one = gain_one + act_one * (1.0 - bend_one)
-        half_two = jnp.dot(
-            hidden_t_ref[...], act_one.astype(jnp.bfloat16), preferred_element_type=jnp.float32
-        )
+        slope_ref[...] = gain_one + act_one * (1.0 - bend_one)
+        return act_one.astype(jnp.bfloat16)
+
+    def finish(index, act_one):
+        geo = geo_of(index)
+        half_two = jnp.dot(hidden_t_ref[...], act_one, preferred_element_type=jnp.float32)
         bend_two = jnp.tanh(half_two)
         gain_two = 1.0 + bend_two
         act_two = half_two * gain_two
         slope_two = gain_two + act_two * (1.0 - bend_two)
-        energy = jnp.concatenate([energy_ref[...]] * (chunk // 128), axis=1)
+        energy = jnp.concatenate([energy_ref[...]] * tiles, axis=1)
         readout = jnp.sum(act_two * energy, axis=0, keepdims=True)
         back_two = (slope_two * energy).astype(jnp.bfloat16)
-        back_one = (
-            jnp.dot(hidden_ref[...], back_two, preferred_element_type=jnp.float32) * slope_one
-        )
-        back_basis = jnp.dot(
-            back_ref[...], back_one.astype(jnp.bfloat16), preferred_element_type=jnp.float32
-        )
+        back_one = jnp.dot(hidden_ref[...], back_two, preferred_element_type=jnp.float32)
+        back_one = (back_one * slope_ref[...]).astype(jnp.bfloat16)
+        back_basis = jnp.dot(back_ref[...], back_one, preferred_element_type=jnp.float32)
         distance = geo[3:4]
         offset, basis = basis_of(distance)
         total = jnp.sum(
@@ -282,12 +314,11 @@
             keepdims=True,
         ) - (readout * distance)
         push = geo[4:5] * total + geo[5:6]
-        term_ref[0:3, lanes] = geo[0:3] * push
-        term_ref[3:5, lanes] = geo[6:8]
+        term_ref[0:3, :] = geo[0:3] * push
+        term_ref[3:5, :] = geo[6:8]
 
     def deposit(index):
-        width = 2 * chunk
-        geo = geo_of(jnp.maximum(index, 0) * 4, 4)
+        geo = geo_of(jnp.maximum(index, 0))
         terms = term_ref[...]
         own = terms[0:4]
         own_top = own.astype(jnp.bfloat16).astype(jnp.float32)
@@ -310,7 +341,7 @@
         far = jnp.concatenate([-terms[0:3], terms[4:5]], axis=0).astype(jnp.bfloat16)
         hit = equal(64, geo[11:12])
         far_rows = jnp.concatenate(
-            [hit * jnp.broadcast_to(far[c : c + 1], (64, width)) for c in range(4)], axis=0
+            [hit * jnp.broadcast_to(far[c : c + 1], (64, chunk)) for c in range(4)], axis=0
         )
         acc_j_ref[...] += lax.dot_general(
             far_rows,
@@ -319,23 +350,27 @@
             preferred_element_type=jnp.float32,
         )
 
-    fetch(0, gather_a)
-    enter(0, gather_a, half_a)
-    fetch(1, gather_b)
+    picks(0).wait()
+    fetch()
+    picks(1).start()
+    enter(0)
+    picks(1).wait()
+    fetch()
+    picks(2).start()
 
     def block(index, carry):
-        first = index * 2
+        picks(index + 2).wait()
+        act_one = activate()
         deposit(index - 1)
-        enter(first + 1, gather_b, half_b)
-        leave(first, 0, half_a)
-        fetch(first + 2, gather_a)
-        enter(first + 2, gather_a, half_a)
-        leave(first + 1, 1, half_b)
-        fetch(first + 3, gather_b)
+        enter(index + 1)
+        fetch()
+        finish(index, act_one)
+        picks(index + 3).start()
         return carry
 
     blocks = blocks_ref[0]
     lax.fori_loop(0, blocks, block, 0)
+    picks(blocks + 2).wait()
     deposit(blocks - 1)
     acc_i = acc_i_ref[...]
     acc_i = jnp.concatenate([acc_i[0:4] + acc_i[4:8], acc_i[8:12] + acc_i[12:16]], axis=0)
@@ -351,7 +386,7 @@
                 target[step_z * 3 + step_x, c * 2 + half : c * 2 + half + 1, :] = row
 
 
-def pair_sums(block_count, rows, low, mid, high, geo, weights):
+def pair_sums(block_count, rows, features, geo, weights):
     vmem = pl.BlockSpec(memory_space=pltpu.VMEM)
     smem = pl.BlockSpec(memory_space=pltpu.SMEM)
     far = pl.BlockSpec(memory_space=pl.ANY)
@@ -359,24 +394,24 @@
     return pl.pallas_call(
         pair_kernel,
         out_shape=(out, out, out),
-        in_specs=[smem, smem, far, far, far, vmem] + [vmem] * 5,
+        in_specs=[smem, far] + [far] * piece_count + [vmem] * 6,
         out_specs=(vmem, vmem, vmem),
         scratch_shapes=[
-            pltpu.VMEM((3, 4608, 128), jnp.bfloat16),
+            pltpu.VMEM((13824, 128), jnp.bfloat16),
             pltpu.VMEM((13824, 128), jnp.float32),
-            pltpu.VMEM((chunk, 128), jnp.float32),
+            pltpu.SMEM((tiles, 128), jnp.int32),
             pltpu.VMEM((chunk, 128), jnp.float32),
             pltpu.VMEM((256, chunk), jnp.float32),
             pltpu.VMEM((256, chunk), jnp.float32),
             pltpu.VMEM((256, 128), jnp.bfloat16),
-            pltpu.VMEM((8, 2 * chunk), jnp.float32),
+            pltpu.VMEM((8, chunk), jnp.float32),
             pltpu.VMEM((16, 256), jnp.float32),
             pltpu.VMEM((256, 256), jnp.float32),
-            pltpu.SemaphoreType.DMA((3,)),
+            pltpu.SemaphoreType.DMA((piece_count + 1,)),
         ],
         compiler_params=pltpu.CompilerParams(vmem_limit_bytes=48 * 1024 * 1024),
         name="pairs",
-    )(block_count, rows, low, mid, high, geo, *weights)
+    )(block_count, rows, *features, geo, *weights)
 
 
 def swap(block, axis):
@@ -386,21 +421,88 @@
     return lax.ppermute(block, axis, forward), lax.ppermute(block, axis, backward)
 
 
+def lines():
+    length = lax.axis_size("gz")
+    up = []
+    for x in range(lax.axis_size("gx")):
+        for z in range(length):
+            target = (x, z + 1) if z + 1 < length else (x ^ 1, 0)
+            up.append((x * length + z, target[0] * length + target[1]))
+    return up, [(target, source) for source, target in up]
+
+
+def carry_across(block):
+    count = lax.axis_size("gx")
+    return lax.ppermute(
+        block, "gx", [(i, (i + 2) % count if i % 2 == 0 else (i - 2) % count) for i in range(count)]
+    )
+
+
+def collect(brick):
+    up, down = lines()
+    line = ("gx", "gz")
+    u1 = lax.ppermute(brick, line, up)
+    d1 = lax.ppermute(brick, line, down)
+    early = jnp.concatenate([brick[:atoms], u1[:atoms], d1[:atoms]], axis=0)
+    early_low, early_high = swap(early, "gy")
+    u2 = lax.ppermute(u1, line, up)
+    d2 = lax.ppermute(d1, line, down)
+    u3 = lax.ppermute(u2, line, up)
+    d3 = lax.ppermute(d2, line, down)
+    u4 = lax.ppermute(u3[:half_message], line, up)
+    d4 = lax.ppermute(d3[half_message:], line, down)
+    place = lax.axis_index("gz")
+    low = jnp.where(place == 0, u1, d3)
+    high = jnp.where(place == lax.axis_size("gz") - 1, d1, u3)
+    tail = atoms - half_message
+    far_coords = carry_across(
+        jnp.concatenate([low[atoms:], d4[tail:], high[atoms:]], axis=0)
+    )
+    far = carry_across(jnp.concatenate([low[:atoms], u4, d4[:tail], high[:atoms]], axis=0))
+    coords = jnp.concatenate(
+        [part[atoms:] for part in (brick, u1, d1, u3, d3)] + [d4[tail:], far_coords], axis=0
+    )
+    coords_low, coords_high = swap(coords, "gy")
+    late = jnp.concatenate([u3[:atoms], d3[:atoms], u4, d4[:tail]], axis=0)
+    late_low, late_high = swap(late, "gy")
+    far_low, far_high = swap(far, "gy")
+    features = (
+        (early_low, late_low, far_low)
+        + (brick, u1, d1, u3, d3, u4, d4, far)
+        + (early_high, late_high, far_high)
+    )
+    coords = [part.reshape(9, 32, 128) for part in (coords_low, coords, coords_high)]
+    return features, coords
+
+
+def block_of(slot):
+    step_x = slot // 9 - 1
+    step_y = slot // 3 % 3
+    step_z = slot % 3 - 1
+    place = lax.axis_index("gz")
+    bottom = place == 0
+    top = place == lax.axis_size("gz") - 1
+    partner = 1 - 2 * (lax.axis_index("gx") % 2)
+    same = jnp.where(
+        step_z == 0, 0, jnp.where(step_z < 0, jnp.where(bottom, 4, 1), jnp.where(top, 3, 2))
+    )
+    beside = jnp.where(
+        step_z == 0, 5, jnp.where(step_z < 0, jnp.where(bottom, 1, 4), jnp.where(top, 2, 3))
+    )
+    column = jnp.where(
+        step_x == 0, same, jnp.where(step_x == partner, beside, 7 + step_z)
+    )
+    return step_y * 9 + column
+
+
 def split(value):
     top = lax.reduce_precision(value, 8, 7)
     return top, value - top
 
 
-def indices(second_tab, mask_tab, atom_slots):
-    slot = second_tab >> 9
-    step_x = slot // 9
-    step_y = slot // 3 % 3
-    step_z = slot % 3
-    rows = (step_y * 9 + step_z * 3 + step_x) * atom_slots + (second_tab & (atom_slots - 1))
+def busy_blocks(mask_tab):
     busy_tiles = jnp.sum(jnp.any(mask_tab != 0, axis=1).astype(jnp.int32))
-    tiles = macro // 128
-    block_count = ((busy_tiles + tiles - 1) // tiles).reshape(1)
-    return block_count, rows
+    return ((busy_tiles + tiles - 1) // tiles).reshape(1)
 
 
 def arrange(own_feat, w_centre, w_neighbour, w_radial, w_hidden, w_energy):
@@ -454,27 +556,20 @@
     coords_own = jnp.concatenate([positions[0, 0, 0], charges[None, :]], axis=0)
     coords_own = coords_own.reshape(8, 2, 128).transpose(1, 0, 2).reshape(16, 128)
 
-    def collect(block):
-        low, high = swap(block, "gx")
-        line = jnp.stack([low, block, high], axis=0)
-        low, high = swap(line, "gz")
-        plane = jnp.concatenate([low, line, high], axis=0)
-        low, high = swap(plane, "gy")
-        return low, plane, high
-
-    near_coords = jnp.stack(collect(coords_own), axis=0)
-    low, mid, high = [part.reshape(9 * atom_slots, -1) for part in collect(own_feat)]
-    coords_all = (
-        near_coords.reshape(3, 3, 3, 16, 128).transpose(2, 0, 1, 3, 4).reshape(27, 16, 128)
-    )
+    coords_top, coords_rest = split(coords_own)
+    brick = jnp.concatenate(
+        [own_feat, coords_top.astype(jnp.bfloat16), coords_rest.astype(jnp.bfloat16)], axis=0
+    )
+    features, coords = collect(brick)
     first_tab = pair_first[0, 0, 0]
     second_tab = pair_second[0, 0, 0]
     mask_tab = pair_mask[0, 0, 0]
-    geo = geometry(coords_all, first_tab, second_tab, mask_tab)
-
-    block_count, rows = indices(second_tab, mask_tab, atom_slots)
+    rows = block_of(second_tab // atoms) * atoms + second_tab % atoms
+    geo = geometry(coords, coords_own, rows, first_tab, second_tab, mask_tab)
     weights = arrange(own_feat, w_centre, w_neighbour, w_radial, w_hidden, w_energy)
-    out_low, out_mid, out_high = pair_sums(block_count, rows, low, mid, high, geo, weights)
+    out_low, out_mid, out_high = pair_sums(
+        busy_blocks(mask_tab), rows.reshape(-1, tiles, 128), features, geo, weights
+    )
 
     def give(low, mid, high, axis):
         count = lax.axis_size(axis)

time: 156 us -> 140 us (0.90)
  waiting for transfers between devices: 41 us -> 20.2 us
  Pallas kernels: 53 us -> 35.6 us
  starting transfers between devices: 46.9 us -> 59.3 us
  other arithmetic: 2.51 us -> 8.52 us
  local copies, waits for them, and re-layouts: 6.45 us -> 11.9 us
    ppermute x0 -> x10, starting transfers between devices: none -> 19.9 us  [the longest x1 4.03 us: collect(): d1 = lax.ppermute(brick, line, down)]
    ppermute x6 -> x4, waiting for transfers between devices: 17.7 us -> 0.01 us  [swap(): lax.ppermute(block, axis, backward)]
    pallas_call x1, Pallas kernels: 40.2 us -> 22.6 us  [pair_sums(): pl.pallas_call(pair_kernel, out_shape=(out, out, out), in_specs=[smem, fa...]
    ppermute x3, starting transfers between devices: 12.6 us -> 27.5 us  [give(): lax.ppermute(high, axis, forward)]
    ppermute x6 -> x4, starting transfers between devices: 12.6 us -> 0.04 us  [swap(): lax.ppermute(block, axis, forward)]
    ppermute x6 -> x4, waiting for transfers between devices: 12.4 us -> 0.01 us  [swap(): lax.ppermute(block, axis, forward)]
    ppermute x0 -> x10, waiting for transfers between devices: none -> 7.7 us  [the longest x1 2.96 us: collect(): u4 = lax.ppermute(u3[:half_message], line, up)]
    ppermute x6 -> x4, starting transfers between devices: 16.3 us -> 11 us  [swap(): lax.ppermute(block, axis, backward)]
  transfers between devices with their start and end apart: 18 -> 24, of which waited for: 12 -> 11; matrix products, arithmetic and copies ran while one was open for 4% -> 9% of each run, Pallas kernels for 8% -> 9%
where the time goes in v3:
time: 140 us; the launch traced here: 141 us
  starting transfers between devices  59.3 us (42%)
  Pallas kernels  35.6 us (25%)
  waiting for transfers between devices  20.2 us (14%)
  local copies, waits for them, and re-layouts  11.9 us (8%)
  other arithmetic  8.52 us (6%)
  between operations  3.08 us (2%)
  matrix products  2 us (1%)
    ppermute x3, starting transfers between devices, give(): lax.ppermute(high, axis, forward)  27.5 us
    pallas_call x1, Pallas kernels, pair_sums(): pl.pallas_call(pair_kernel, out_shape=(out, out, out), in_specs=[smem, fa...  22.6 us
    pallas_call x1, Pallas kernels, geometry(): pl.pallas_call(geometry_kernel, out_shape=jax.ShapeDtypeStruct((128, 16,...  13 us
    ppermute x4, starting transfers between devices, swap(): lax.ppermute(block, axis, backward)  11 us
    ppermute x3, waiting for transfers between devices, give(): lax.ppermute(low, axis, backward)  8.51 us
    unnamed x51, local copies, waits for them, and re-layouts  6.87 us
    ppermute x1, starting transfers between devices, collect(): d1 = lax.ppermute(brick, line, down)  4.03 us
    ppermute x3, waiting for transfers between devices, give(): lax.ppermute(high, axis, forward)  3.99 us
  transfers between devices with their start and end apart: 24, of which 11 were waited for; matrix products, arithmetic and copies ran while one was open for 9% of the time, Pallas kernels for 9%

profile of v3, /device:TPU:2, one launch (start us, length us, event | category | flops | bytes accessed | tf_op | source)
XLA Modules:
  0.0 140.7 jit_solution(6041113384352897472)
XLA Ops:
  2.0 1.0 fusion.22
  5.6 2.0 %collective-permute-start = (bf16[544,128]{1,0:T(8,128)(2,1)S(1)}, bf16[544,128]{1,0:T(8,128)(2,1)S(1)}, u32[]{:S(2)}, u32[]{:S(2)}) collective-permute-start(bf16[544,128]{1,0:T(8,128)(2,1)S(1)} %pad_maximum_fusion.3.refs_3_), channel_id=1, source_target_pairs={{0,1},{1,2},{2,3},{3,32},{32,33},{33,34},{34,35},{35,0},{64,65},{6... | collective-permute-start | bytes 417800 | tf_op jit(solution)/shard_map/ppermute | solution.py:444
  7.6 4.0 %collective-permute-start.1 = (bf16[544,128]{1,0:T(8,128)(2,1)S(1)}, bf16[544,128]{1,0:T(8,128)(2,1)S(1)}, u32[]{:S(2)}, u32[]{:S(2)}) collective-permute-start(bf16[544,128]{1,0:T(8,128)(2,1)S(1)} %pad_maximum_fusion.3.refs_3_), channel_id=1, source_target_pairs={{1,0},{2,1},{3,2},{32,3},{33,32},{34,33},{35,34},{0,35},{65,64},{6... | collective-permute-start | bytes 417800 | tf_op jit(solution)/shard_map/ppermute | solution.py:445
  12.5 1.1 fusion.4.rows_ref
  13.6 1.0 fusion
  17.0 0.9 slice-done.2
  18.7 2.2 %collective-permute-start.12 = (bf16[1536,128]{1,0:T(8,128)(2,1)}, bf16[1536,128]{1,0:T(8,128)(2,1)S(1)}, u32[]{:S(2)}, u32[]{:S(2)}) collective-permute-start(bf16[1536,128]{1,0:T(8,128)(2,1)} %pad_maximum_fusion), channel_id=1, source_target_pairs={{4,0},{8,4},{12,8},{16,12},{20,16},{24,20},{28,24},{0,28},{5,1},{9... | collective-permute-start | bytes 1179656 | tf_op jit(solution)/shard_map/ppermute | solution.py:421
  20.9 3.2 %collective-permute-start.5 = (bf16[544,128]{1,0:T(8,128)(2,1)S(1)}, bf16[544,128]{1,0:T(8,128)(2,1)S(1)}, u32[]{:S(2)}, u32[]{:S(2)}) collective-permute-start(bf16[544,128]{1,0:T(8,128)(2,1)S(1)} %collective-permute-done.1.refs_5_), channel_id=1, source_target_pairs={{1,0},{2,1},{3,2},{32,3},{33,32},{34,33},{35,34},{0,35},{65,64},{6... | collective-permute-start | bytes 417800 | tf_op jit(solution)/shard_map/ppermute | solution.py:449
  24.7 2.0 %collective-permute-done.5 = bf16[544,128]{1,0:T(8,128)(2,1)S(1)} collective-permute-done((bf16[544,128]{1,0:T(8,128)(2,1)S(1)}, bf16[544,128]{1,0:T(8,128)(2,1)S(1)}, u32[]{:S(2)}, u32[]{:S(2)}) %collective-permute-start.5) | collective-permute-done | bytes 139296 | tf_op jit(solution)/shard_map/ppermute | solution.py:449
  26.7 3.7 %collective-permute-start.6 = (bf16[544,128]{1,0:T(8,128)(2,1)S(1)}, bf16[544,128]{1,0:T(8,128)(2,1)S(1)}, u32[]{:S(2)}, u32[]{:S(2)}) collective-permute-start(bf16[544,128]{1,0:T(8,128)(2,1)S(1)} %collective-permute-done.5), channel_id=1, source_target_pairs={{1,0},{2,1},{3,2},{32,3},{33,32},{34,33},{35,34},{0,35},{65,64},{6... | collective-permute-start | bytes 417800 | tf_op jit(solution)/shard_map/ppermute | solution.py:451
  31.0 2.3 %collective-permute-done.6.refs_7_ = bf16[544,128]{1,0:T(8,128)(2,1)S(1)} collective-permute-done((bf16[544,128]{1,0:T(8,128)(2,1)S(1)}, bf16[544,128]{1,0:T(8,128)(2,1)S(1)}, u32[]{:S(2)}, u32[]{:S(2)}) %collective-permute-start.6) | collective-permute-done | bytes 139296 | tf_op jit(solution)/shard_map/ppermute | solution.py:451
  33.3 3.8 %collective-permute-start.8 = (bf16[272,128]{1,0:T(8,128)(2,1)S(1)}, bf16[272,128]{1,0:T(8,128)(2,1)S(1)}, u32[]{:S(2)}, u32[]{:S(2)}) collective-permute-start(bf16[272,128]{1,0:T(8,128)(2,1)S(1)} %slice.107), channel_id=1, source_target_pairs={{1,0},{2,1},{3,2},{32,3},{33,32},{34,33},{35,34},{0,35},{65,64},{6... | collective-permute-start | bytes 208904 | tf_op jit(solution)/shard_map/ppermute | solution.py:453
  39.6 1.6 %collective-permute-start.15 = (bf16[96,128]{1,0:T(8,128)(2,1)S(1)}, bf16[96,128]{1,0:T(8,128)(2,1)S(1)}, u32[]{:S(2)}, u32[]{:S(2)}) collective-permute-start(bf16[96,128]{1,0:T(8,128)(2,1)S(1)} %pad_maximum_fusion.4), channel_id=1, source_target_pairs={{0,64},{32,224},{64,128},{96,32},{128,192},{160,96},{192,0},{224,1... | collective-permute-start | bytes 73736 | tf_op jit(solution)/shard_map/ppermute | solution.py:436
  41.2 3.0 %collective-permute-done.7.refs_8_ = bf16[272,128]{1,0:T(8,128)(2,1)S(1)} collective-permute-done((bf16[272,128]{1,0:T(8,128)(2,1)S(1)}, bf16[272,128]{1,0:T(8,128)(2,1)S(1)}, u32[]{:S(2)}, u32[]{:S(2)}) %collective-permute-start.7) | collective-permute-done | bytes 69664 | tf_op jit(solution)/shard_map/ppermute | solution.py:452
  45.0 1.5 %collective-permute-start.10 = (bf16[1536,128]{1,0:T(8,128)(2,1)S(1)}, bf16[1536,128]{1,0:T(8,128)(2,1)S(1)}, u32[]{:S(2)}, u32[]{:S(2)}) collective-permute-start(bf16[1536,128]{1,0:T(8,128)(2,1)S(1)} %get-tuple-element.18), channel_id=1, source_target_pairs={{0,64},{32,224},{64,128},{96,32},{128,192},{160,96},{192,0},{224,1... | collective-permute-start | bytes 1179656 | tf_op jit(solution)/shard_map/ppermute | solution.py:436
  47.2 3.0 %collective-permute-start.17 = (bf16[288,128]{1,0:T(8,128)(2,1)}, bf16[288,128]{1,0:T(8,128)(2,1)S(1)}, u32[]{:S(2)}, u32[]{:S(2)}) collective-permute-start(bf16[288,128]{1,0:T(8,128)(2,1)} %constant_dynamic-update-slice_fusion), channel_id=1, source_target_pairs={{4,0},{8,4},{12,8},{16,12},{20,16},{24,20},{28,24},{0,28},{5,1},{9... | collective-permute-start | bytes 221192 | tf_op jit(solution)/shard_map/ppermute | solution.py:421
  50.3 2.9 %collective-permute-start.13 = (bf16[1536,128]{1,0:T(8,128)(2,1)}, bf16[1536,128]{1,0:T(8,128)(2,1)S(1)}, u32[]{:S(2)}, u32[]{:S(2)}) collective-permute-start(bf16[1536,128]{1,0:T(8,128)(2,1)} %get-tuple-element.19), channel_id=1, source_target_pairs={{4,0},{8,4},{12,8},{16,12},{20,16},{24,20},{28,24},{0,28},{5,1},{9... | collective-permute-start | bytes 1179656 | tf_op jit(solution)/shard_map/ppermute | solution.py:421
  53.3 2.9 %collective-permute-start.14 = (bf16[1536,128]{1,0:T(8,128)(2,1)S(1)}, bf16[1536,128]{1,0:T(8,128)(2,1)}, u32[]{:S(2)}, u32[]{:S(2)}) collective-permute-start(bf16[1536,128]{1,0:T(8,128)(2,1)S(1)} %collective-permute-done.10.refs_10_), channel_id=1, source_target_pairs={{4,0},{8,4},{12,8},{16,12},{20,16},{24,20},{28,24},{0,28},{5,1},{9... | collective-permute-start | bytes 1179656 | tf_op jit(solution)/shard_map/ppermute | solution.py:421
  59.1 0.9 maximum_maximum_fusion.refs_15_
  60.1 13.0 %geometry.1.refs_14_ = f32[128,16,128]{2,1,0:T(8,128)} custom-call(bf16[9,32,128]{2,1,0:T(8,128)(2,1)} %bitcast.61, bf16[9,32,128]{2,1,0:T(8,128)(2,1)} %bitcast.12.mid_ref, bf16[9,32,128]{2,1,0:T(8,128)(2,1)} %bitcast.62, f32[16,128]{1,0:T(8,128)} %bitcast.65, s32[128,128]{1,0:T(8,128)} %fusion.9.rows_ref, s32[128,128]{1,0:T(8,128)} %bitcast.63, ...), custom_call_target="tpu_custom_call" | custom-call | tf_op jit(solution)/shard_map/geometry/pallas_call | solution.py:166
  74.7 1.2 copy-done.1
  75.9 22.6 %pairs.1 = (f32[9,8,256]{2,1,0:T(8,128)S(1)}, f32[9,8,256]{2,1,0:T(8,128)S(1)}, f32[9,8,256]{2,1,0:T(8,128)S(1)}) custom-call(s32[1]{0:T(128)} %bitcast.1.blocks_ref, s32[32,4,128]{2,1,0:T(4,128)S(1)} %copy-done.8, bf16[1536,128]{1,0:T(8,128)(2,1)S(1)} %collective-permute-done.2.refs_0_, bf16[1536,128]{1,0:T(8,128)(2,1)S(1)} %collective-permute-done.9.refs_1_, ...), custom_call_target="tpu_custom_call" | custom-call | tf_op jit(solution)/shard_map/pairs/pallas_call | solution.py:394
  98.5 7.0 %collective-permute-start.18 = (f32[9,8,256]{2,1,0:T(8,128)S(1)}, f32[9,8,256]{2,1,0:T(8,128)S(1)}, u32[]{:S(2)}, u32[]{:S(2)}) collective-permute-start(f32[9,8,256]{2,1,0:T(8,128)S(1)} %get-tuple-element.6), channel_id=1, source_target_pairs={{0,4},{4,8},{8,12},{12,16},{16,20},{20,24},{24,28},{28,0},{1,5},{5... | collective-permute-start | bytes 221192 | tf_op jit(solution)/shard_map/ppermute | solution.py:578
  105.5 0.9 collective-permute-done.18
  106.4 1.1 collective-permute-done.19
  107.5 4.3 %collective-permute-start.20 = (f32[3,8,256]{2,1,0:T(8,128)S(1)}, f32[3,8,256]{2,1,0:T(8,128)S(1)}, u32[]{:S(2)}, u32[]{:S(2)}) collective-permute-start(f32[3,8,256]{2,1,0:T(8,128)S(1)} %get-tuple-element.20), channel_id=1, source_target_pairs={{0,1},{1,2},{2,3},{3,0},{4,5},{5,6},{6,7},{7,4},{8,9},{9,10},{10,1... | collective-permute-start | bytes 73736 | tf_op jit(solution)/shard_map/ppermute | solution.py:578
  111.9 0.9 collective-permute-start.21
  112.7 1.7 %collective-permute-done.20 = f32[3,8,256]{2,1,0:T(8,128)S(1)} collective-permute-done((f32[3,8,256]{2,1,0:T(8,128)S(1)}, f32[3,8,256]{2,1,0:T(8,128)S(1)}, u32[]{:S(2)}, u32[]{:S(2)}) %collective-permute-start.20) | collective-permute-done | bytes 24608 | tf_op jit(solution)/shard_map/ppermute | solution.py:578
  114.4 1.2 collective-permute-done.21
  115.7 16.2 %collective-permute-start.22 = (f32[8,256]{1,0:T(8,128)S(1)}, f32[8,256]{1,0:T(8,128)S(1)}, u32[]{:S(2)}, u32[]{:S(2)}) collective-permute-start(f32[8,256]{1,0:T(8,128)S(1)} %get-tuple-element.24), channel_id=1, source_target_pairs={{0,32},{32,64},{64,96},{96,128},{128,160},{160,192},{192,224},{224... | collective-permute-start | bytes 24584 | tf_op jit(solution)/shard_map/ppermute | solution.py:578
  131.9 1.4 collective-permute-done.22
  133.3 6.2 %collective-permute-done.23 = f32[8,256]{1,0:T(8,128)S(1)} collective-permute-done((f32[8,256]{1,0:T(8,128)S(1)}, f32[8,256]{1,0:T(8,128)S(1)}, u32[]{:S(2)}, u32[]{:S(2)}) %collective-permute-start.23) | collective-permute-done | bytes 8224 | tf_op jit(solution)/shard_map/ppermute | solution.py:578
  (129 shorter events, 16.9 us)
Async XLA Ops:
  0.6 12.9 %copy-start = (bf16[128,256]{1,0:T(8,128)(2,1)S(1)}, bf16[128,256]{1,0:T(8,128)(2,1)}, u32[]{:S(2)}) copy-start(bf16[128,256]{1,0:T(8,128)(2,1)} %param.18) | copy-start | bytes 196612
  5.6 6.0 %copy-start.11 = (s32[1,1,1,128,128]{4,3,2,1,0:T(8,128)S(1)}, s32[1,1,1,128,128]{4,3,2,1,0:T(8,128)}, u32[]{:S(2)}) copy-start(s32[1,1,1,128,128]{4,3,2,1,0:T(8,128)} %param.16) | copy-start | bytes 196612
  5.6 10.7 %collective-permute-start = (bf16[544,128]{1,0:T(8,128)(2,1)S(1)}, bf16[544,128]{1,0:T(8,128)(2,1)S(1)}, u32[]{:S(2)}, u32[]{:S(2)}) collective-permute-start(bf16[544,128]{1,0:T(8,128)(2,1)S(1)} %pad_maximum_fusion.3.refs_3_), channel_id=1, source_target_pairs={{0,1},{1,2},{2,3},{3,32},{32,33},{33,34},{34,35},{35,0},{64,65},{6... | collective-permute-start | bytes 417800 | tf_op jit(solution)/shard_map/ppermute | solution.py:444
  7.6 9.4 %collective-permute-start.1 = (bf16[544,128]{1,0:T(8,128)(2,1)S(1)}, bf16[544,128]{1,0:T(8,128)(2,1)S(1)}, u32[]{:S(2)}, u32[]{:S(2)}) collective-permute-start(bf16[544,128]{1,0:T(8,128)(2,1)S(1)} %pad_maximum_fusion.3.refs_3_), channel_id=1, source_target_pairs={{1,0},{2,1},{3,2},{32,3},{33,32},{34,33},{35,34},{0,35},{65,64},{6... | collective-permute-start | bytes 417800 | tf_op jit(solution)/shard_map/ppermute | solution.py:445
  18.7 31.6 %collective-permute-start.12 = (bf16[1536,128]{1,0:T(8,128)(2,1)}, bf16[1536,128]{1,0:T(8,128)(2,1)S(1)}, u32[]{:S(2)}, u32[]{:S(2)}) collective-permute-start(bf16[1536,128]{1,0:T(8,128)(2,1)} %pad_maximum_fusion), channel_id=1, source_target_pairs={{4,0},{8,4},{12,8},{16,12},{20,16},{24,20},{28,24},{0,28},{5,1},{9... | collective-permute-start | bytes 1179656 | tf_op jit(solution)/shard_map/ppermute | solution.py:421
  20.9 10.1 %collective-permute-start.3 = (bf16[544,128]{1,0:T(8,128)(2,1)S(1)}, bf16[544,128]{1,0:T(8,128)(2,1)S(1)}, u32[]{:S(2)}, u32[]{:S(2)}) collective-permute-start(bf16[544,128]{1,0:T(8,128)(2,1)S(1)} %copy-done.7), channel_id=1, source_target_pairs={{0,1},{1,2},{2,3},{3,32},{32,33},{33,34},{34,35},{35,0},{64,65},{6... | collective-permute-start | bytes 417800 | tf_op jit(solution)/shard_map/ppermute | solution.py:448
  20.9 5.8 %collective-permute-start.5 = (bf16[544,128]{1,0:T(8,128)(2,1)S(1)}, bf16[544,128]{1,0:T(8,128)(2,1)S(1)}, u32[]{:S(2)}, u32[]{:S(2)}) collective-permute-start(bf16[544,128]{1,0:T(8,128)(2,1)S(1)} %collective-permute-done.1.refs_5_), channel_id=1, source_target_pairs={{1,0},{2,1},{3,2},{32,3},{33,32},{34,33},{35,34},{0,35},{65,64},{6... | collective-permute-start | bytes 417800 | tf_op jit(solution)/shard_map/ppermute | solution.py:449
  26.7 6.6 %collective-permute-start.6 = (bf16[544,128]{1,0:T(8,128)(2,1)S(1)}, bf16[544,128]{1,0:T(8,128)(2,1)S(1)}, u32[]{:S(2)}, u32[]{:S(2)}) collective-permute-start(bf16[544,128]{1,0:T(8,128)(2,1)S(1)} %collective-permute-done.5), channel_id=1, source_target_pairs={{1,0},{2,1},{3,2},{32,3},{33,32},{34,33},{35,34},{0,35},{65,64},{6... | collective-permute-start | bytes 417800 | tf_op jit(solution)/shard_map/ppermute | solution.py:451
  31.0 6.3 %collective-permute-start.4 = (bf16[544,128]{1,0:T(8,128)(2,1)S(1)}, bf16[544,128]{1,0:T(8,128)(2,1)S(1)}, u32[]{:S(2)}, u32[]{:S(2)}) collective-permute-start(bf16[544,128]{1,0:T(8,128)(2,1)S(1)} %collective-permute-done.3), channel_id=1, source_target_pairs={{0,1},{1,2},{2,3},{3,32},{32,33},{33,34},{34,35},{35,0},{64,65},{6... | collective-permute-start | bytes 417800 | tf_op jit(solution)/shard_map/ppermute | solution.py:450
  33.3 5.7 %collective-permute-start.8 = (bf16[272,128]{1,0:T(8,128)(2,1)S(1)}, bf16[272,128]{1,0:T(8,128)(2,1)S(1)}, u32[]{:S(2)}, u32[]{:S(2)}) collective-permute-start(bf16[272,128]{1,0:T(8,128)(2,1)S(1)} %slice.107), channel_id=1, source_target_pairs={{1,0},{2,1},{3,2},{32,3},{33,32},{34,33},{35,34},{0,35},{65,64},{6... | collective-permute-start | bytes 208904 | tf_op jit(solution)/shard_map/ppermute | solution.py:453
  38.6 5.6 %collective-permute-start.7 = (bf16[272,128]{1,0:T(8,128)(2,1)S(1)}, bf16[272,128]{1,0:T(8,128)(2,1)S(1)}, u32[]{:S(2)}, u32[]{:S(2)}) collective-permute-start(bf16[272,128]{1,0:T(8,128)(2,1)S(1)} %slice.106), channel_id=1, source_target_pairs={{0,1},{1,2},{2,3},{3,32},{32,33},{33,34},{34,35},{35,0},{64,65},{6... | collective-permute-start | bytes 208904 | tf_op jit(solution)/shard_map/ppermute | solution.py:452
  39.6 7.0 %collective-permute-start.15 = (bf16[96,128]{1,0:T(8,128)(2,1)S(1)}, bf16[96,128]{1,0:T(8,128)(2,1)S(1)}, u32[]{:S(2)}, u32[]{:S(2)}) collective-permute-start(bf16[96,128]{1,0:T(8,128)(2,1)S(1)} %pad_maximum_fusion.4), channel_id=1, source_target_pairs={{0,64},{32,224},{64,128},{96,32},{128,192},{160,96},{192,0},{224,1... | collective-permute-start | bytes 73736 | tf_op jit(solution)/shard_map/ppermute | solution.py:436
  45.0 8.2 %collective-permute-start.10 = (bf16[1536,128]{1,0:T(8,128)(2,1)S(1)}, bf16[1536,128]{1,0:T(8,128)(2,1)S(1)}, u32[]{:S(2)}, u32[]{:S(2)}) collective-permute-start(bf16[1536,128]{1,0:T(8,128)(2,1)S(1)} %get-tuple-element.18), channel_id=1, source_target_pairs={{0,64},{32,224},{64,128},{96,32},{128,192},{160,96},{192,0},{224,1... | collective-permute-start | bytes 1179656 | tf_op jit(solution)/shard_map/ppermute | solution.py:436
  46.6 12.4 %copy-start.14 = (bf16[256,256]{0,1:T(8,128)(2,1)S(1)}, bf16[256,256]{0,1:T(8,128)(2,1)}, u32[]{:S(2)}) copy-start(bf16[256,256]{0,1:T(8,128)(2,1)} %get-tuple-element.17) | copy-start | bytes 393220
  46.6 12.5 %copy-start.10 = (bf16[256,512]{1,0:T(8,128)(2,1)S(1)}, bf16[256,512]{1,0:T(8,128)(2,1)}, u32[]{:S(2)}) copy-start(bf16[256,512]{1,0:T(8,128)(2,1)} %fusion) | copy-start | bytes 786436
  47.2 6.0 %collective-permute-start.16 = (bf16[288,128]{1,0:T(8,128)(2,1)}, bf16[288,128]{1,0:T(8,128)(2,1)S(1)}, u32[]{:S(2)}, u32[]{:S(2)}) collective-permute-start(bf16[288,128]{1,0:T(8,128)(2,1)} %constant_dynamic-update-slice_fusion), channel_id=1, source_target_pairs={{0,4},{4,8},{8,12},{12,16},{16,20},{20,24},{24,28},{28,0},{1,5},{5... | collective-permute-start | bytes 221192 | tf_op jit(solution)/shard_map/ppermute | solution.py:421
  47.2 6.1 %collective-permute-start.17 = (bf16[288,128]{1,0:T(8,128)(2,1)}, bf16[288,128]{1,0:T(8,128)(2,1)S(1)}, u32[]{:S(2)}, u32[]{:S(2)}) collective-permute-start(bf16[288,128]{1,0:T(8,128)(2,1)} %constant_dynamic-update-slice_fusion), channel_id=1, source_target_pairs={{4,0},{8,4},{12,8},{16,12},{20,16},{24,20},{28,24},{0,28},{5,1},{9... | collective-permute-start | bytes 221192 | tf_op jit(solution)/shard_map/ppermute | solution.py:421
  50.2 22.9 %collective-permute-start.2 = (bf16[1536,128]{1,0:T(8,128)(2,1)}, bf16[1536,128]{1,0:T(8,128)(2,1)S(1)}, u32[]{:S(2)}, u32[]{:S(2)}) collective-permute-start(bf16[1536,128]{1,0:T(8,128)(2,1)} %pad_maximum_fusion), channel_id=1, source_target_pairs={{0,4},{4,8},{8,12},{12,16},{16,20},{20,24},{24,28},{28,0},{1,5},{5... | collective-permute-start | bytes 1179656 | tf_op jit(solution)/shard_map/ppermute | solution.py:421
  50.3 22.8 %collective-permute-start.13 = (bf16[1536,128]{1,0:T(8,128)(2,1)}, bf16[1536,128]{1,0:T(8,128)(2,1)S(1)}, u32[]{:S(2)}, u32[]{:S(2)}) collective-permute-start(bf16[1536,128]{1,0:T(8,128)(2,1)} %get-tuple-element.19), channel_id=1, source_target_pairs={{4,0},{8,4},{12,8},{16,12},{20,16},{24,20},{28,24},{0,28},{5,1},{9... | collective-permute-start | bytes 1179656 | tf_op jit(solution)/shard_map/ppermute | solution.py:421
  53.2 5.8 %copy-start.17 = (bf16[288,128]{1,0:T(8,128)(2,1)}, bf16[288,128]{1,0:T(8,128)(2,1)S(1)}, u32[]{:S(2)}) copy-start(bf16[288,128]{1,0:T(8,128)(2,1)S(1)} %collective-permute-done.16) | copy-start | bytes 221188
  53.2 19.9 %collective-permute-start.9 = (bf16[1536,128]{1,0:T(8,128)(2,1)}, bf16[1536,128]{1,0:T(8,128)(2,1)S(1)}, u32[]{:S(2)}, u32[]{:S(2)}) collective-permute-start(bf16[1536,128]{1,0:T(8,128)(2,1)} %get-tuple-element.19), channel_id=1, source_target_pairs={{0,4},{4,8},{8,12},{12,16},{16,20},{20,24},{24,28},{28,0},{1,5},{5... | collective-permute-start | bytes 1179656 | tf_op jit(solution)/shard_map/ppermute | solution.py:421
  53.2 19.9 %collective-permute-start.11 = (bf16[1536,128]{1,0:T(8,128)(2,1)S(1)}, bf16[1536,128]{1,0:T(8,128)(2,1)}, u32[]{:S(2)}, u32[]{:S(2)}) collective-permute-start(bf16[1536,128]{1,0:T(8,128)(2,1)S(1)} %collective-permute-done.10.refs_10_), channel_id=1, source_target_pairs={{0,4},{4,8},{8,12},{12,16},{16,20},{20,24},{24,28},{28,0},{1,5},{5... | collective-permute-start | bytes 1179656 | tf_op jit(solution)/shard_map/ppermute | solution.py:421
  53.3 5.8 %copy-start.18 = (bf16[288,128]{1,0:T(8,128)(2,1)}, bf16[288,128]{1,0:T(8,128)(2,1)S(1)}, u32[]{:S(2)}) copy-start(bf16[288,128]{1,0:T(8,128)(2,1)S(1)} %collective-permute-done.17) | copy-start | bytes 221188
  53.3 19.9 %collective-permute-start.14 = (bf16[1536,128]{1,0:T(8,128)(2,1)S(1)}, bf16[1536,128]{1,0:T(8,128)(2,1)}, u32[]{:S(2)}, u32[]{:S(2)}) collective-permute-start(bf16[1536,128]{1,0:T(8,128)(2,1)S(1)} %collective-permute-done.10.refs_10_), channel_id=1, source_target_pairs={{4,0},{8,4},{12,8},{16,12},{20,16},{24,20},{28,24},{0,28},{5,1},{9... | collective-permute-start | bytes 1179656 | tf_op jit(solution)/shard_map/ppermute | solution.py:421
  60.0 13.9 %copy-start.3 = (bf16[544,128]{1,0:T(8,128)(2,1)S(1)}, bf16[544,128]{1,0:T(8,128)(2,1)}, u32[]{:S(2)}) copy-start(bf16[544,128]{1,0:T(8,128)(2,1)} %copy-done.2) | copy-start | bytes 417796
  60.1 13.9 %copy-start.5 = (bf16[544,128]{1,0:T(8,128)(2,1)S(1)}, bf16[544,128]{1,0:T(8,128)(2,1)}, u32[]{:S(2)}) copy-start(bf16[544,128]{1,0:T(8,128)(2,1)} %copy-done.4) | copy-start | bytes 417796
  98.5 7.9 %collective-permute-start.18 = (f32[9,8,256]{2,1,0:T(8,128)S(1)}, f32[9,8,256]{2,1,0:T(8,128)S(1)}, u32[]{:S(2)}, u32[]{:S(2)}) collective-permute-start(f32[9,8,256]{2,1,0:T(8,128)S(1)} %get-tuple-element.6), channel_id=1, source_target_pairs={{0,4},{4,8},{8,12},{12,16},{16,20},{20,24},{24,28},{28,0},{1,5},{5... | collective-permute-start | bytes 221192 | tf_op jit(solution)/shard_map/ppermute | solution.py:578
  105.5 2.0 %collective-permute-start.19 = (f32[9,8,256]{2,1,0:T(8,128)S(1)}, f32[9,8,256]{2,1,0:T(8,128)S(1)}, u32[]{:S(2)}, u32[]{:S(2)}) collective-permute-start(f32[9,8,256]{2,1,0:T(8,128)S(1)} %get-tuple-element.7), channel_id=1, source_target_pairs={{4,0},{8,4},{12,8},{16,12},{20,16},{24,20},{28,24},{0,28},{5,1},{9... | collective-permute-start | bytes 221192 | tf_op jit(solution)/shard_map/ppermute | solution.py:578
  107.5 6.9 %collective-permute-start.20 = (f32[3,8,256]{2,1,0:T(8,128)S(1)}, f32[3,8,256]{2,1,0:T(8,128)S(1)}, u32[]{:S(2)}, u32[]{:S(2)}) collective-permute-start(f32[3,8,256]{2,1,0:T(8,128)S(1)} %get-tuple-element.20), channel_id=1, source_target_pairs={{0,1},{1,2},{2,3},{3,0},{4,5},{5,6},{6,7},{7,4},{8,9},{9,10},{10,1... | collective-permute-start | bytes 73736 | tf_op jit(solution)/shard_map/ppermute | solution.py:578
  111.9 3.8 %collective-permute-start.21 = (f32[3,8,256]{2,1,0:T(8,128)S(1)}, f32[3,8,256]{2,1,0:T(8,128)S(1)}, u32[]{:S(2)}, u32[]{:S(2)}) collective-permute-start(f32[3,8,256]{2,1,0:T(8,128)S(1)} %get-tuple-element.21), channel_id=1, source_target_pairs={{1,0},{2,1},{3,2},{0,3},{5,4},{6,5},{7,6},{4,7},{9,8},{10,9},{11,1... | collective-permute-start | bytes 73736 | tf_op jit(solution)/shard_map/ppermute | solution.py:578
  115.7 17.6 %collective-permute-start.22 = (f32[8,256]{1,0:T(8,128)S(1)}, f32[8,256]{1,0:T(8,128)S(1)}, u32[]{:S(2)}, u32[]{:S(2)}) collective-permute-start(f32[8,256]{1,0:T(8,128)S(1)} %get-tuple-element.24), channel_id=1, source_target_pairs={{0,32},{32,64},{64,96},{96,128},{128,160},{160,192},{192,224},{224... | collective-permute-start | bytes 24584 | tf_op jit(solution)/shard_map/ppermute | solution.py:578
  131.9 7.6 %collective-permute-start.23 = (f32[8,256]{1,0:T(8,128)S(1)}, f32[8,256]{1,0:T(8,128)S(1)}, u32[]{:S(2)}, u32[]{:S(2)}) collective-permute-start(f32[8,256]{1,0:T(8,128)S(1)} %get-tuple-element.25), channel_id=1, source_target_pairs={{32,0},{64,32},{96,64},{128,96},{160,128},{192,160},{224,192},{0,2... | collective-permute-start | bytes 24584 | tf_op jit(solution)/shard_map/ppermute | solution.py:578
  (21 other events, 53.3 us)

commit v4 on v3

--- a/solution.py
+++ b/solution.py
@@ -14,18 +14,35 @@
 atoms = 512
 message = 544
 half_message = message // 2
-own_pieces = tuple((0, atoms, e * atoms) for e in range(5)) + (
-    (0, half_message, 5 * atoms),
-    (0, atoms - half_message, 5 * atoms + half_message),
-    (0, 3 * atoms, 6 * atoms),
+group = 3 * message
+side_bricks = tuple((piece, e * message) for piece in range(3) for e in range(3))
+own_bricks = tuple((piece, 0) for piece in range(5)) + (None,) + tuple(
+    (7, e * message) for e in range(3)
 )
-side_pieces = ((0, 3 * atoms, 0), (0, 3 * atoms, 3 * atoms), (0, 3 * atoms, 6 * atoms))
-pieces = (
-    side_pieces
-    + tuple((begin, size, 9 * atoms + at) for begin, size, at in own_pieces)
-    + tuple((begin, size, 18 * atoms + at) for begin, size, at in side_pieces)
-)
-piece_count = len(pieces)
+
+
+def copy_list():
+    features, coords = [], []
+    for side, (base, bricks) in enumerate(((0, side_bricks), (3, own_bricks), (11, side_bricks))):
+        for e, brick in enumerate(bricks):
+            block = side * 9 + e
+            at = block * atoms
+            if brick is None:
+                rest = atoms - half_message
+                features.append((base + 5, 0, half_message, at))
+                features.append((base + 6, 0, rest, at + half_message))
+                coords.append((base + 6, rest, block))
+            else:
+                piece, begin = brick
+                features.append((base + piece, begin, atoms, at))
+                coords.append((base + piece, begin + atoms, block))
+    return features, coords
+
+
+piece_count = 14
+weight_count = 5
+feature_copies, coord_copies = copy_list()
+copy_count = len(feature_copies) + len(coord_copies) + weight_count + 1
 
 erfc_p = (
     2.326819970068386e-2, -1.387039388740657e-1, 3.687424674597105e-1, -5.824733027278666e-1,
@@ -56,14 +73,16 @@
     return jnp.where(x < 1.0, 1.0 - x * poly(square, erf_t), tail)
 
 
-def geometry_kernel(
-    low_ref, mid_ref, high_ref, own_ref, rows_ref, first_ref, second_ref, mask_ref, out_ref,
-    place_ref, top_ref,
+def geometry_phase(
+    coords_ref, rows_ref, first_ref, second_ref, mask_ref, out_ref, place_ref, top_ref, iota_ref
 ):
     rows = 32
     wide = 512
-    for side, ref in enumerate((low_ref, mid_ref, high_ref)):
-        parts = ref[...].astype(jnp.float32)
+    own = coords_ref[9, 0:16, :].astype(jnp.float32) + coords_ref[9, 16:32, :].astype(
+        jnp.float32
+    )
+    for side in range(3):
+        parts = coords_ref[side * 9 : side * 9 + 9].astype(jnp.float32)
         for part in range(2):
             at = part * 16
             block = jnp.concatenate([parts[:, at : at + 8], parts[:, at + 8 : at + 16]], axis=2)
@@ -73,13 +92,12 @@
 
     def locate(index, carry):
         second = jnp.concatenate(
-            [rows_ref[pl.ds(index * 4 + k, 1), :] for k in range(4)], axis=1
+            [rows_ref[index, k : k + 1, :] for k in range(4)], axis=1
         )
         low = (second & 255).astype(jnp.float32).astype(jnp.bfloat16)
         high = jnp.broadcast_to(second >> 8, (8, wide))
-        iota = lax.broadcasted_iota(jnp.int32, (256, wide), 0).astype(jnp.float32)
         hot = jnp.where(
-            iota.astype(jnp.bfloat16) == jnp.broadcast_to(low, (256, wide)),
+            jnp.concatenate([iota_ref[...]] * 4, axis=1) == jnp.broadcast_to(low, (256, wide)),
             jnp.ones((), jnp.bfloat16),
             jnp.zeros((), jnp.bfloat16),
         )
@@ -99,7 +117,7 @@
                 place_ref[c, pl.ds(index * 4 + k, 1), :] = row[:, k * 128 : k * 128 + 128]
         return carry
 
-    lax.fori_loop(0, 32, locate, 0)
+    lax.fori_loop(0, 32, locate, 0, unroll=2)
 
     def group(index, carry):
         base = pl.multiple_of(index * rows, rows)
@@ -121,7 +139,7 @@
             for c in range(4):
                 at = (part & 1) * 8 + c * 2 + (part >> 1)
                 place_i[c] = jnp.where(
-                    hit, pick(own_ref[at : at + 1, :], lane_i), place_i[c]
+                    hit, pick(own[at : at + 1], lane_i), place_i[c]
                 )
         slot = second >> 9
         step_x = (slot * 57) >> 9
@@ -162,44 +180,115 @@
     out_ref[:, 12:16, :] = jnp.zeros((128, 4, 128), jnp.float32)
 
 
-def geometry(parts, own, rows, first, second, mask):
+def brick_kernel(features_ref, positions_ref, counts_ref, charge_ref, out_ref):
+    features = features_ref[...]
+    weight = jnp.broadcast_to(charge_ref[...], (8, 128))
+    raw = lax.dot_general(
+        weight, features, (((1,), (1,)), ((), ())), preferred_element_type=jnp.float32
+    )[0:1]
+    filled = counts_ref[0]
+    alive = lax.broadcasted_iota(jnp.int32, (1, atoms), 1) < filled
+    total = jnp.sum(jnp.where(alive, raw, 0.0), axis=1, keepdims=True)
+    charges = jnp.where(alive, raw - total / filled.astype(jnp.float32), 0.0)
+    halves = [positions_ref[c : c + 1, 256 * h : 256 * h + 256] for c in range(3) for h in range(2)]
+    halves += [charges[:, 0:256], charges[:, 256:512]]
+    coords = jnp.concatenate(halves, axis=0)
+    coords = jnp.concatenate([coords[:, 0:128], coords[:, 128:256]], axis=0)
+    top = coords.astype(jnp.bfloat16)
+    out_ref[0:atoms, :] = features
+    out_ref[atoms : atoms + 16, :] = top
+    out_ref[atoms + 16 : message, :] = (coords - top.astype(jnp.float32)).astype(jnp.bfloat16)
+
+
+def make_brick(features, positions, counts, w_charge):
+    vmem = pl.BlockSpec(memory_space=pltpu.VMEM)
     return pl.pallas_call(
-        geometry_kernel,
-        out_shape=jax.ShapeDtypeStruct((128, 16, 128), jnp.float32),
-        scratch_shapes=[
-            pltpu.VMEM((4, 128, 128), jnp.float32),
-            pltpu.VMEM((216, 512), jnp.bfloat16),
-        ],
-        name="geometry",
-    )(*parts, own, rows, first, second, mask)
-
-
-def pair_kernel(
-    blocks_ref,
+        brick_kernel,
+        out_shape=jax.ShapeDtypeStruct((message, 128), jnp.bfloat16),
+        in_specs=[vmem, vmem, pl.BlockSpec(memory_space=pltpu.SMEM), vmem],
+        name="brick",
+    )(features, positions, counts, w_charge)
+
+
+def arrange_kernel(
+    brick_ref, centre_ref, neighbour_ref, radial_ref, hidden_ref, energy_ref,
+    first_out, half_out, turned_out, energy_out, back_out,
+):
+    centre = lax.dot_general(
+        centre_ref[...],
+        brick_ref[0:atoms, :],
+        (((0,), (1,)), ((), ())),
+        preferred_element_type=jnp.float32,
+    )
+    first_out[:, 0:512] = (centre.astype(jnp.bfloat16).astype(jnp.float32) * 0.5).astype(
+        jnp.bfloat16
+    )
+    first_out[:, 512:640] = (neighbour_ref[...].astype(jnp.float32).T * 0.5).astype(jnp.bfloat16)
+    radial = radial_ref[...] * 0.5
+    top = radial.astype(jnp.bfloat16).astype(jnp.float32)
+    rest = radial - top
+    side = jnp.concatenate([top, rest, top, jnp.zeros((104, 256), jnp.float32)], axis=0)
+    first_out[:, 640:768] = side.T.astype(jnp.bfloat16)
+    hidden = hidden_ref[...].astype(jnp.float32) * 0.5
+    half_out[...] = hidden.astype(jnp.bfloat16)
+    turned_out[...] = hidden.T.astype(jnp.bfloat16)
+    energy_out[...] = jnp.broadcast_to(energy_ref[...], (128, 256)).T
+    back_out[...] = jnp.concatenate([top, rest], axis=0).astype(jnp.bfloat16)
+
+
+def arrange(brick, w_centre, w_neighbour, w_radial, w_hidden, w_energy):
+    def shape(rows, columns, kind=jnp.bfloat16):
+        return jax.ShapeDtypeStruct((rows, columns), kind)
+
+    return pl.pallas_call(
+        arrange_kernel,
+        out_shape=(
+            shape(256, 768),
+            shape(256, 256),
+            shape(256, 256),
+            shape(256, 128, jnp.float32),
+            shape(16, 256),
+        ),
+        name="arrange",
+    )(brick, w_centre, w_neighbour, w_radial, w_hidden, w_energy.reshape(1, -1))
+
+
+def pair_kernel(rows_ref, pick_first, pick_second, pick_mask, *refs):
+    pair_body(
+        rows_ref,
+        pick_first,
+        pick_second,
+        pick_mask,
+        refs[:piece_count],
+        refs[piece_count : piece_count + weight_count],
+        *refs[piece_count + weight_count :],
+    )
+
+
+def pair_body(
     rows_ref,
-    *refs,
-):
-    sources, refs = refs[:piece_count], refs[piece_count:]
-    pair_body(blocks_ref, rows_ref, sources, *refs)
-
-
-def pair_body(
-    blocks_ref,
-    rows_ref,
+    pick_first,
+    pick_second,
+    pick_mask,
     sources,
-    geo_ref,
+    weights,
+    out_low,
+    out_mid,
+    out_high,
     first_ref,
     hidden_ref,
     hidden_t_ref,
     energy_ref,
     back_ref,
-    out_low,
-    out_mid,
-    out_high,
     stage_ref,
+    coords_ref,
+    place_ref,
+    top_ref,
+    geo_ref,
     table_ref,
     picks_ref,
     gather_ref,
+    feature_ref,
     half_ref,
     slope_ref,
     iota_ref,
@@ -212,17 +301,23 @@
 
     def picks(index):
         return pltpu.make_async_copy(
-            rows_ref.at[jnp.minimum(index, last)], picks_ref, sems.at[piece_count]
+            rows_ref.at[jnp.minimum(index, last)], picks_ref, sems.at[copy_count - 1]
         )
 
     picks(0).start()
-    copies = []
-    for piece, (source, (begin, size, at)) in enumerate(zip(sources, pieces)):
-        copies.append(
-            pltpu.make_async_copy(
-                source.at[pl.ds(begin, size)], stage_ref.at[pl.ds(at, size)], sems.at[piece]
-            )
-        )
+    plan = [
+        (sources[piece].at[pl.ds(begin, 32)], coords_ref.at[block])
+        for piece, begin, block in coord_copies
+    ]
+    plan += [
+        (sources[piece].at[pl.ds(begin, size)], stage_ref.at[pl.ds(at, size)])
+        for piece, begin, size, at in feature_copies
+    ]
+    plan += list(zip(weights, (first_ref, hidden_ref, hidden_t_ref, energy_ref, back_ref)))
+    copies = [
+        pltpu.make_async_copy(source, target, sems.at[k])
+        for k, (source, target) in enumerate(plan)
+    ]
     for copy in copies:
         copy.start()
     one = jnp.ones((), jnp.bfloat16)
@@ -233,7 +328,15 @@
     acc_i_ref[...] = jnp.zeros_like(acc_i_ref)
     acc_j_ref[...] = jnp.zeros_like(acc_j_ref)
     term_ref[...] = jnp.zeros_like(term_ref)
-    for copy in copies:
+    for copy in copies[: len(coord_copies)]:
+        copy.wait()
+    geometry_phase(
+        coords_ref, rows_ref, pick_first, pick_second, pick_mask, geo_ref, place_ref, top_ref,
+        iota_ref,
+    )
+    tile = lax.broadcasted_iota(jnp.int32, (128, 128), 0) + tiles
+    blocks = jnp.max(jnp.where(pick_mask[...] != 0, tile, 0)) // tiles
+    for copy in copies[len(coord_copies) :]:
         copy.wait()
 
     def widen(step, carry):
@@ -243,10 +346,14 @@
 
     lax.fori_loop(0, 54, widen, 0)
 
-    def fetch():
-        for p in range(chunk):
-            row = picks_ref[p // 128, p % 128]
-            gather_ref[pl.ds(p, 1), :] = table_ref[pl.ds(row, 1), :]
+    def fetch(*parts):
+        for part in parts or range(tiles):
+            for p in range(part * 128, part * 128 + 128):
+                row = picks_ref[part, p % 128]
+                gather_ref[pl.ds(p, 1), :] = table_ref[pl.ds(row, 1), :]
+
+    def turn():
+        feature_ref[...] = gather_ref[...].T.astype(jnp.bfloat16)
 
     def geo_of(index):
         return jnp.concatenate([geo_ref[index * tiles + k] for k in range(tiles)], axis=1)
@@ -274,7 +381,7 @@
             [
                 equal(256, jnp.where(side == 0.0, low, 512.0)),
                 equal(256, jnp.where(side == 0.0, 512.0, low)),
-                gather_ref[...].T.astype(jnp.bfloat16),
+                feature_ref[...],
                 jnp.concatenate([top, top, basis - top, jnp.zeros_like(top)], axis=0).astype(
                     jnp.bfloat16
                 ),
@@ -292,18 +399,17 @@
         slope_ref[...] = gain_one + act_one * (1.0 - bend_one)
         return act_one.astype(jnp.bfloat16)
 
-    def finish(index, act_one):
-        geo = geo_of(index)
-        half_two = jnp.dot(hidden_t_ref[...], act_one, preferred_element_type=jnp.float32)
+    def second(half_two):
         bend_two = jnp.tanh(half_two)
         gain_two = 1.0 + bend_two
         act_two = half_two * gain_two
         slope_two = gain_two + act_two * (1.0 - bend_two)
         energy = jnp.concatenate([energy_ref[...]] * tiles, axis=1)
         readout = jnp.sum(act_two * energy, axis=0, keepdims=True)
-        back_two = (slope_two * energy).astype(jnp.bfloat16)
-        back_one = jnp.dot(hidden_ref[...], back_two, preferred_element_type=jnp.float32)
-        back_one = (back_one * slope_ref[...]).astype(jnp.bfloat16)
+        return readout, (slope_two * energy).astype(jnp.bfloat16)
+
+    def finish(index, readout, back_one):
+        geo = geo_of(index)
         back_basis = jnp.dot(back_ref[...], back_one, preferred_element_type=jnp.float32)
         distance = geo[3:4]
         offset, basis = basis_of(distance)
@@ -353,6 +459,7 @@
     picks(0).wait()
     fetch()
     picks(1).start()
+    turn()
     enter(0)
     picks(1).wait()
     fetch()
@@ -361,14 +468,18 @@
     def block(index, carry):
         picks(index + 2).wait()
         act_one = activate()
-        deposit(index - 1)
+        half_two = jnp.dot(hidden_t_ref[...], act_one, preferred_element_type=jnp.float32)
+        turn()
         enter(index + 1)
         fetch()
-        finish(index, act_one)
+        readout, back_two = second(half_two)
+        deposit(index - 1)
+        back_one = jnp.dot(hidden_ref[...], back_two, preferred_element_type=jnp.float32)
+        back_one = (back_one * slope_ref[...]).astype(jnp.bfloat16)
+        finish(index, readout, back_one)
         picks(index + 3).start()
         return carry
 
-    blocks = blocks_ref[0]
     lax.fori_loop(0, blocks, block, 0)
     picks(blocks + 2).wait()
     deposit(blocks - 1)
@@ -386,32 +497,41 @@
                 target[step_z * 3 + step_x, c * 2 + half : c * 2 + half + 1, :] = row
 
 
-def pair_sums(block_count, rows, features, geo, weights):
+def pair_sums(rows, first, second, mask, features, weights):
     vmem = pl.BlockSpec(memory_space=pltpu.VMEM)
-    smem = pl.BlockSpec(memory_space=pltpu.SMEM)
-    far = pl.BlockSpec(memory_space=pl.ANY)
+    far = pl.BlockSpec(memory_space=pltpu.HBM)
     out = jax.ShapeDtypeStruct((9, 8, 256), jnp.float32)
     return pl.pallas_call(
         pair_kernel,
         out_shape=(out, out, out),
-        in_specs=[smem, far] + [far] * piece_count + [vmem] * 6,
+        in_specs=[vmem] * 4 + [far] * (piece_count + weight_count),
         out_specs=(vmem, vmem, vmem),
         scratch_shapes=[
+            pltpu.VMEM((256, 768), jnp.bfloat16),
+            pltpu.VMEM((256, 256), jnp.bfloat16),
+            pltpu.VMEM((256, 256), jnp.bfloat16),
+            pltpu.VMEM((256, 128), jnp.float32),
+            pltpu.VMEM((16, 256), jnp.bfloat16),
             pltpu.VMEM((13824, 128), jnp.bfloat16),
+            pltpu.VMEM((27, 32, 128), jnp.bfloat16),
+            pltpu.VMEM((4, 128, 128), jnp.float32),
+            pltpu.VMEM((216, 512), jnp.bfloat16),
+            pltpu.VMEM((128, 16, 128), jnp.float32),
             pltpu.VMEM((13824, 128), jnp.float32),
             pltpu.SMEM((tiles, 128), jnp.int32),
             pltpu.VMEM((chunk, 128), jnp.float32),
+            pltpu.VMEM((128, chunk), jnp.bfloat16),
             pltpu.VMEM((256, chunk), jnp.float32),
             pltpu.VMEM((256, chunk), jnp.float32),
             pltpu.VMEM((256, 128), jnp.bfloat16),
             pltpu.VMEM((8, chunk), jnp.float32),
             pltpu.VMEM((16, 256), jnp.float32),
             pltpu.VMEM((256, 256), jnp.float32),
-            pltpu.SemaphoreType.DMA((piece_count + 1,)),
+            pltpu.SemaphoreType.DMA((copy_count,)),
         ],
         compiler_params=pltpu.CompilerParams(vmem_limit_bytes=48 * 1024 * 1024),
         name="pairs",
-    )(block_count, rows, *features, geo, *weights)
+    )(rows, first, second, mask, *features, *weights)
 
 
 def swap(block, axis):
@@ -438,15 +558,24 @@
     )
 
 
-def collect(brick):
+def carry_back(block):
+    count = lax.axis_size("gx")
+    return lax.ppermute(
+        block, "gx", [(i, (i - 2) % count if i % 2 == 0 else (i + 2) % count) for i in range(count)]
+    )
+
+
+def collect(brick, prepare):
     up, down = lines()
     line = ("gx", "gz")
     u1 = lax.ppermute(brick, line, up)
     d1 = lax.ppermute(brick, line, down)
-    early = jnp.concatenate([brick[:atoms], u1[:atoms], d1[:atoms]], axis=0)
-    early_low, early_high = swap(early, "gy")
+    early_low, early_high = swap(jnp.concatenate([brick, u1, d1], axis=0), "gy")
+    tied, _ = lax.optimization_barrier((brick, u1))
+    prepared = prepare(tied)
     u2 = lax.ppermute(u1, line, up)
     d2 = lax.ppermute(d1, line, down)
+    u2, d2, prepared = lax.optimization_barrier((u2, d2, prepared))
     u3 = lax.ppermute(u2, line, up)
     d3 = lax.ppermute(d2, line, down)
     u4 = lax.ppermute(u3[:half_message], line, up)
@@ -454,25 +583,15 @@
     place = lax.axis_index("gz")
     low = jnp.where(place == 0, u1, d3)
     high = jnp.where(place == lax.axis_size("gz") - 1, d1, u3)
-    tail = atoms - half_message
-    far_coords = carry_across(
-        jnp.concatenate([low[atoms:], d4[tail:], high[atoms:]], axis=0)
-    )
-    far = carry_across(jnp.concatenate([low[:atoms], u4, d4[:tail], high[:atoms]], axis=0))
-    coords = jnp.concatenate(
-        [part[atoms:] for part in (brick, u1, d1, u3, d3)] + [d4[tail:], far_coords], axis=0
-    )
-    coords_low, coords_high = swap(coords, "gy")
-    late = jnp.concatenate([u3[:atoms], d3[:atoms], u4, d4[:tail]], axis=0)
-    late_low, late_high = swap(late, "gy")
+    far = carry_across(jnp.concatenate([low, u4, d4, high], axis=0))
+    late_low, late_high = swap(jnp.concatenate([u3, d3, u4, d4], axis=0), "gy")
     far_low, far_high = swap(far, "gy")
     features = (
         (early_low, late_low, far_low)
         + (brick, u1, d1, u3, d3, u4, d4, far)
         + (early_high, late_high, far_high)
     )
-    coords = [part.reshape(9, 32, 128) for part in (coords_low, coords, coords_high)]
-    return features, coords
+    return features, prepared
 
 
 def block_of(slot):
@@ -493,43 +612,6 @@
         step_x == 0, same, jnp.where(step_x == partner, beside, 7 + step_z)
     )
     return step_y * 9 + column
-
-
-def split(value):
-    top = lax.reduce_precision(value, 8, 7)
-    return top, value - top
-
-
-def busy_blocks(mask_tab):
-    busy_tiles = jnp.sum(jnp.any(mask_tab != 0, axis=1).astype(jnp.int32))
-    return ((busy_tiles + tiles - 1) // tiles).reshape(1)
-
-
-def arrange(own_feat, w_centre, w_neighbour, w_radial, w_hidden, w_energy):
-    centre_t = jnp.dot(own_feat, w_centre, preferred_element_type=jnp.float32).astype(
-        jnp.bfloat16
-    ).T * jnp.bfloat16(0.5)
-    half = jnp.bfloat16(0.5)
-    radial_top, radial_rest = split(w_radial * 0.5)
-    zero_rows = jnp.zeros_like(radial_top)
-    radial_t = (
-        jnp.concatenate([radial_top, radial_rest, radial_top, zero_rows], axis=0)
-        .astype(jnp.bfloat16)
-        .T
-    )
-    back = jnp.concatenate([radial_top, radial_rest], axis=0).astype(jnp.bfloat16)
-    energy = jnp.broadcast_to(w_energy[:, None], (w_energy.shape[0], 128))
-    first = jnp.concatenate(
-        [centre_t, w_neighbour.T * half, radial_t, jnp.zeros((radial_t.shape[0], 96), jnp.bfloat16)],
-        axis=1,
-    )
-    return (
-        first,
-        w_hidden * half,
-        w_hidden.T * half,
-        energy,
-        back,
-    )
 
 
 def local(
@@ -546,29 +628,19 @@
     w_hidden,
     w_energy,
 ):
-    own_feat = features[0, 0, 0]
-    atom_slots = own_feat.shape[0]
-    raw_charge = jnp.dot(own_feat, w_charge, preferred_element_type=jnp.float32)
-    filled = counts[0, 0, 0]
-    alive_slot = jnp.arange(atom_slots, dtype=jnp.int32) < filled
-    average = jnp.sum(jnp.where(alive_slot, raw_charge, 0.0)) / filled.astype(jnp.float32)
-    charges = jnp.where(alive_slot, raw_charge - average, 0.0)
-    coords_own = jnp.concatenate([positions[0, 0, 0], charges[None, :]], axis=0)
-    coords_own = coords_own.reshape(8, 2, 128).transpose(1, 0, 2).reshape(16, 128)
-
-    coords_top, coords_rest = split(coords_own)
-    brick = jnp.concatenate(
-        [own_feat, coords_top.astype(jnp.bfloat16), coords_rest.astype(jnp.bfloat16)], axis=0
-    )
-    features, coords = collect(brick)
-    first_tab = pair_first[0, 0, 0]
+    brick = make_brick(
+        features[0, 0, 0], positions[0, 0, 0], counts[0, 0], w_charge.reshape(1, -1)
+    )
     second_tab = pair_second[0, 0, 0]
-    mask_tab = pair_mask[0, 0, 0]
-    rows = block_of(second_tab // atoms) * atoms + second_tab % atoms
-    geo = geometry(coords, coords_own, rows, first_tab, second_tab, mask_tab)
-    weights = arrange(own_feat, w_centre, w_neighbour, w_radial, w_hidden, w_energy)
+
+    def prepare(tied):
+        rows = block_of(second_tab // atoms) * atoms + second_tab % atoms
+        weights = arrange(tied, w_centre, w_neighbour, w_radial, w_hidden, w_energy)
+        return rows.reshape(-1, tiles, 128), weights
+
+    pieces, (rows, weights) = collect(brick, prepare)
     out_low, out_mid, out_high = pair_sums(
-        busy_blocks(mask_tab), rows.reshape(-1, tiles, 128), features, geo, weights
+        rows, pair_first[0, 0, 0], second_tab, pair_mask[0, 0, 0], pieces, weights
     )
 
     def give(low, mid, high, axis):
@@ -578,8 +650,14 @@
         return mid + lax.ppermute(high, axis, forward) + lax.ppermute(low, axis, backward)
 
     plane = give(out_low, out_mid, out_high, "gy")
-    line = give(plane[0:3], plane[3:6], plane[6:9], "gz")
-    summed = give(line[0], line[1], line[2], "gx").reshape(4, atom_slots)
+    even = lax.axis_index("gx") % 2 == 0
+    below, centre, above = (plane[x::3] for x in range(3))
+    far = carry_back(jnp.where(even, below, above))
+    near = jnp.where(even, above, below) + far
+    both = jnp.stack([centre, near], axis=0)
+    both = give(both[:, 0], both[:, 1], both[:, 2], "gz")
+    partners = [(i, i ^ 1) for i in range(lax.axis_size("gx"))]
+    summed = (both[0] + lax.ppermute(both[1], "gx", partners)).reshape(4, atoms)
     return (summed[:3][None, None, None], summed[3][None, None, None])
 
 

time: 140 us -> 130 us (0.929)
  waiting for transfers between devices: 20.2 us -> 40.5 us
  local copies, waits for them, and re-layouts: 11.9 us -> 2.57 us
  Pallas kernels: 35.6 us -> 26.3 us
  other arithmetic: 8.52 us -> 0.65 us
  matrix products: 2 us -> 0 us
  between operations: 3.08 us -> 1.46 us
    ppermute x0 -> x2, waiting for transfers between devices: none -> 11.4 us  [the longest x1 5.96 us: carry_back(): lax.ppermute(block, 'gx', [(i, (i - 2) % count if i % 2 == 0 else (i + 2)...]
    pallas_call x2 -> x3, Pallas kernels: 35.6 us -> 26.3 us  [the longest x1 22.3 us: pair_sums(): pl.pallas_call(pair_kernel, out_shape=(out, out, out), in_specs=[vmem] *...]
    ppermute x4 -> x3, starting transfers between devices: 11 us -> 2.65 us  [swap(): lax.ppermute(block, axis, backward)]
    ppermute x4 -> x3, waiting for transfers between devices: 0.01 us -> 7.71 us  [swap(): lax.ppermute(block, axis, forward)]
    ppermute x3 -> x2, waiting for transfers between devices: 8.51 us -> 1.08 us  [give(): lax.ppermute(low, axis, backward)]
    unnamed x51 -> x20, local copies, waits for them, and re-layouts: 6.87 us -> 1.34 us
    ppermute x1, waiting for transfers between devices: 0.01 us -> 3.67 us  [collect(): u2 = lax.ppermute(u1, line, up)]
    ppermute x2 -> x1, waiting for transfers between devices: 0.01 us -> 3.29 us  [carry_across(): lax.ppermute(block, 'gx', [(i, (i + 2) % count if i % 2 == 0 else (i - 2)...]
  transfers between devices with their start and end apart: 24 -> 21, of which waited for: 11 -> 15; matrix products, arithmetic and copies ran while one was open for 9% -> 0% of each run, Pallas kernels for 9% -> 2%
where the time goes in v4:
time: 130 us
  starting transfers between devices  58.8 us (45%)
  waiting for transfers between devices  40.5 us (31%)
  Pallas kernels  26.3 us (20%)
  local copies, waits for them, and re-layouts  2.57 us (2%)
  between operations  1.46 us (1%)
    ppermute x2, starting transfers between devices, give(): lax.ppermute(high, axis, forward)  30.7 us
    pallas_call x1, Pallas kernels, pair_sums(): pl.pallas_call(pair_kernel, out_shape=(out, out, out), in_specs=[vmem] *...  22.3 us
    ppermute x3, waiting for transfers between devices, swap(): lax.ppermute(block, axis, forward)  7.71 us
    ppermute x1, waiting for transfers between devices, carry_back(): lax.ppermute(block, 'gx', [(i, (i - 2) % count if i % 2 == 0 else (i + 2)...  5.96 us
    ppermute x1, starting transfers between devices, collect(): d1 = lax.ppermute(brick, line, down)  5.86 us
    ppermute x1, waiting for transfers between devices, local(): summed = (both[0] + lax.ppermute(both[1], 'gx', partners)).reshape(4, atoms)  5.45 us
    ppermute x2, starting transfers between devices, give(): lax.ppermute(low, axis, backward)  3.81 us
    ppermute x1, waiting for transfers between devices, collect(): u2 = lax.ppermute(u1, line, up)  3.67 us
  transfers between devices with their start and end apart: 21, of which 15 were waited for; matrix products, arithmetic and copies ran while one was open for 0% of the time, Pallas kernels for 2%

profile of v4, /device:TPU:2, one launch (start us, length us, event | category | flops | bytes accessed | tf_op | source)
XLA Modules:
  0.0 130.3 jit_solution(8628462351578191922)
XLA Ops:
  1.3 1.3 copy.24
  2.6 1.9 %brick.1.brick_ref.refs_3_ = bf16[544,128]{1,0:T(8,128)(2,1)} custom-call(bf16[512,128]{1,0:T(8,128)(2,1)} %bitcast.41, f32[3,512]{1,0:T(4,128)} %bitcast.43, s32[1]{0:T(128)} %bitcast.36.counts_ref, bf16[1,128]{1,0:T(2,128)(2,1)} %bitcast.45), custom_call_target="tpu_custom_call" | custom-call | tf_op jit(solution)/shard_map/brick/pallas_call | solution.py:205
  4.4 5.9 %collective-permute-start.2 = (bf16[544,128]{1,0:T(8,128)(2,1)}, bf16[544,128]{1,0:T(8,128)(2,1)S(1)}, u32[]{:S(2)}, u32[]{:S(2)}) collective-permute-start(bf16[544,128]{1,0:T(8,128)(2,1)} %brick.1.brick_ref.refs_3_), channel_id=1, source_target_pairs={{1,0},{2,1},{3,2},{32,3},{33,32},{34,33},{35,34},{0,35},{65,64},{6... | collective-permute-start | bytes 417800 | tf_op jit(solution)/shard_map/ppermute | solution.py:572
  10.3 3.2 %collective-permute-done.2.refs_5_ = bf16[544,128]{1,0:T(8,128)(2,1)S(1)} collective-permute-done((bf16[544,128]{1,0:T(8,128)(2,1)}, bf16[544,128]{1,0:T(8,128)(2,1)S(1)}, u32[]{:S(2)}, u32[]{:S(2)}) %collective-permute-start.2) | collective-permute-done | bytes 139296 | tf_op jit(solution)/shard_map/ppermute | solution.py:572
  13.5 3.6 %collective-permute-start.3 = (bf16[544,128]{1,0:T(8,128)(2,1)S(1)}, bf16[544,128]{1,0:T(8,128)(2,1)S(1)}, u32[]{:S(2)}, u32[]{:S(2)}) collective-permute-start(bf16[544,128]{1,0:T(8,128)(2,1)S(1)} %collective-permute-done.2.refs_5_), channel_id=1, source_target_pairs={{1,0},{2,1},{3,2},{32,3},{33,32},{34,33},{35,34},{0,35},{65,64},{6... | collective-permute-start | bytes 417800 | tf_op jit(solution)/shard_map/ppermute | solution.py:577
  17.6 2.1 %arrange.1 = (bf16[256,768]{1,0:T(8,128)(2,1)}, bf16[256,256]{1,0:T(8,128)(2,1)}, bf16[256,256]{1,0:T(8,128)(2,1)}, f32[256,128]{1,0:T(8,128)}, bf16[16,256]{1,0:T(8,128)(2,1)}) custom-call(bf16[544,128]{1,0:T(8,128)(2,1)} %brick.1.brick_ref.refs_3_, bf16[128,256]{1,0:T(8,128)(2,1)} %centre_ref.1, bf16[128,256]{1,0:T(8,128)(2,1)} %neighbour_ref.1, ...), custom_call_target="tpu_custom_call" | custom-call | tf_op jit(solution)/shard_map/arrange/pallas_call | solution.py:243
  19.7 3.7 %collective-permute-done.1 = bf16[544,128]{1,0:T(8,128)(2,1)S(1)} collective-permute-done((bf16[544,128]{1,0:T(8,128)(2,1)S(1)}, bf16[544,128]{1,0:T(8,128)(2,1)S(1)}, u32[]{:S(2)}, u32[]{:S(2)}) %collective-permute-start.1) | collective-permute-done | bytes 139296 | tf_op jit(solution)/shard_map/ppermute | solution.py:576
  23.4 3.2 %collective-permute-start.6 = (bf16[544,128]{1,0:T(8,128)(2,1)S(1)}, bf16[544,128]{1,0:T(8,128)(2,1)S(1)}, u32[]{:S(2)}, u32[]{:S(2)}) collective-permute-start(bf16[544,128]{1,0:T(8,128)(2,1)S(1)} %collective-permute-done.3), channel_id=1, source_target_pairs={{1,0},{2,1},{3,2},{32,3},{33,32},{34,33},{35,34},{0,35},{65,64},{6... | collective-permute-start | bytes 417800 | tf_op jit(solution)/shard_map/ppermute | solution.py:580
  26.6 3.0 %collective-permute-done.5.refs_6_ = bf16[544,128]{1,0:T(8,128)(2,1)S(1)} collective-permute-done((bf16[544,128]{1,0:T(8,128)(2,1)S(1)}, bf16[544,128]{1,0:T(8,128)(2,1)S(1)}, u32[]{:S(2)}, u32[]{:S(2)}) %collective-permute-start.5) | collective-permute-done | bytes 139296 | tf_op jit(solution)/shard_map/ppermute | solution.py:579
  29.7 3.3 %collective-permute-start.8 = (bf16[272,128]{1,0:T(8,128)(2,1)S(1)}, bf16[272,128]{1,0:T(8,128)(2,1)S(1)}, u32[]{:S(2)}, u32[]{:S(2)}) collective-permute-start(bf16[272,128]{1,0:T(8,128)(2,1)S(1)} %slice.51), channel_id=1, source_target_pairs={{1,0},{2,1},{3,2},{32,3},{33,32},{34,33},{35,34},{0,35},{65,64},{6... | collective-permute-start | bytes 208904 | tf_op jit(solution)/shard_map/ppermute | solution.py:582
  33.1 2.1 %collective-permute-done.7.refs_8_ = bf16[272,128]{1,0:T(8,128)(2,1)S(1)} collective-permute-done((bf16[272,128]{1,0:T(8,128)(2,1)S(1)}, bf16[272,128]{1,0:T(8,128)(2,1)S(1)}, u32[]{:S(2)}, u32[]{:S(2)}) %collective-permute-start.7) | collective-permute-done | bytes 69664 | tf_op jit(solution)/shard_map/ppermute | solution.py:581
  35.2 1.6 %collective-permute-start.10 = (bf16[1632,128]{1,0:T(8,128)(2,1)S(1)}, bf16[1632,128]{1,0:T(8,128)(2,1)S(1)}, u32[]{:S(2)}, u32[]{:S(2)}) collective-permute-start(bf16[1632,128]{1,0:T(8,128)(2,1)S(1)} %pad_maximum_fusion.1), channel_id=1, source_target_pairs={{0,64},{32,224},{64,128},{96,32},{128,192},{160,96},{192,0},{224,1... | collective-permute-start | bytes 1253384 | tf_op jit(solution)/shard_map/ppermute | solution.py:556
  36.9 0.5 collective-permute-start.4
  37.4 2.6 %collective-permute-start.13 = (bf16[1632,128]{1,0:T(8,128)(2,1)S(1)}, bf16[1632,128]{1,0:T(8,128)(2,1)S(1)}, u32[]{:S(2)}, u32[]{:S(2)}) collective-permute-start(bf16[1632,128]{1,0:T(8,128)(2,1)S(1)} %constant_dynamic-update-slice_fusion), channel_id=1, source_target_pairs={{4,0},{8,4},{12,8},{16,12},{20,16},{24,20},{28,24},{0,28},{5,1},{9... | collective-permute-start | bytes 1253384 | tf_op jit(solution)/shard_map/ppermute | solution.py:541
  40.1 3.3 %collective-permute-done.10.refs_10_ = bf16[1632,128]{1,0:T(8,128)(2,1)S(1)} collective-permute-done((bf16[1632,128]{1,0:T(8,128)(2,1)S(1)}, bf16[1632,128]{1,0:T(8,128)(2,1)S(1)}, u32[]{:S(2)}, u32[]{:S(2)}) %collective-permute-start.10) | collective-permute-done | bytes 417824 | tf_op jit(solution)/shard_map/ppermute | solution.py:556
  43.4 1.2 collective-permute-start.11
  44.6 1.1 collective-permute-done.4.refs_0_
  45.7 1.2 collective-permute-done.13.refs_12_
  46.9 3.3 %collective-permute-done.9.refs_1_ = bf16[1632,128]{1,0:T(8,128)(2,1)S(1)} collective-permute-done((bf16[1632,128]{1,0:T(8,128)(2,1)S(1)}, bf16[1632,128]{1,0:T(8,128)(2,1)S(1)}, u32[]{:S(2)}, u32[]{:S(2)}) %collective-permute-start.9) | collective-permute-done | bytes 417824 | tf_op jit(solution)/shard_map/ppermute | solution.py:541
  50.2 1.2 collective-permute-done.14.refs_13_
  51.4 3.3 %collective-permute-done.11.refs_2_ = bf16[1632,128]{1,0:T(8,128)(2,1)S(1)} collective-permute-done((bf16[1632,128]{1,0:T(8,128)(2,1)S(1)}, bf16[1632,128]{1,0:T(8,128)(2,1)S(1)}, u32[]{:S(2)}, u32[]{:S(2)}) %collective-permute-start.11) | collective-permute-done | bytes 417824 | tf_op jit(solution)/shard_map/ppermute | solution.py:541
  54.7 22.3 %pairs.1 = (f32[9,8,256]{2,1,0:T(8,128)S(1)}, f32[9,8,256]{2,1,0:T(8,128)S(1)}, f32[9,8,256]{2,1,0:T(8,128)S(1)}) custom-call(s32[32,4,128]{2,1,0:T(4,128)S(1)} %fusion.3.rows_ref, s32[128,128]{1,0:T(8,128)S(1)} %bitcast.39, s32[128,128]{1,0:T(8,128)S(1)} %bitcast.38, s32[128,128]{1,0:T(8,128)S(1)} %bitcast.40, ...), custom_call_target="tpu_custom_call" | custom-call | tf_op jit(solution)/shard_map/pairs/pallas_call | solution.py:504
  77.0 30.7 %collective-permute-start.15 = (f32[9,8,256]{2,1,0:T(8,128)S(1)}, f32[9,8,256]{2,1,0:T(8,128)S(1)}, u32[]{:S(2)}, u32[]{:S(2)}) collective-permute-start(f32[9,8,256]{2,1,0:T(8,128)S(1)} %get-tuple-element.34), channel_id=1, source_target_pairs={{0,4},{4,8},{8,12},{12,16},{16,20},{20,24},{24,28},{28,0},{1,5},{5... | collective-permute-start | bytes 221192 | tf_op jit(solution)/shard_map/ppermute | solution.py:650
  107.7 0.9 collective-permute-done.15
  108.6 1.1 collective-permute-done.16
  109.8 6.0 %collective-permute-done.17 = f32[3,8,256]{2,1,0:T(8,128)S(1)} collective-permute-done((f32[3,8,256]{2,1,0:T(8,128)S(1)}, f32[3,8,256]{2,1,0:T(8,128)S(1)}, u32[]{:S(2)}, u32[]{:S(2)}) %collective-permute-start.17) | collective-permute-done | bytes 24608 | tf_op jit(solution)/shard_map/ppermute | solution.py:563
  115.9 3.8 %collective-permute-start.19 = (f32[2,8,256]{2,1,0:T(8,128)S(1)}, f32[2,8,256]{2,1,0:T(8,128)S(1)}, u32[]{:S(2)}, u32[]{:S(2)}) collective-permute-start(f32[2,8,256]{2,1,0:T(8,128)S(1)} %get-tuple-element.47), channel_id=1, source_target_pairs={{1,0},{2,1},{3,2},{0,3},{5,4},{6,5},{7,6},{4,7},{9,8},{10,9},{11,1... | collective-permute-start | bytes 49160 | tf_op jit(solution)/shard_map/ppermute | solution.py:650
  119.7 1.7 %collective-permute-done.18 = f32[2,8,256]{2,1,0:T(8,128)S(1)} collective-permute-done((f32[2,8,256]{2,1,0:T(8,128)S(1)}, f32[2,8,256]{2,1,0:T(8,128)S(1)}, u32[]{:S(2)}, u32[]{:S(2)}) %collective-permute-start.18) | collective-permute-done | bytes 16416 | tf_op jit(solution)/shard_map/ppermute | solution.py:650
  121.4 2.2 %collective-permute-start.20 = (f32[8,256]{1,0:T(8,128)S(1)}, f32[8,256]{1,0:T(8,128)S(1)}, u32[]{:S(2)}, u32[]{:S(2)}) collective-permute-start(f32[8,256]{1,0:T(8,128)S(1)} %slice_bitcast_fusion.1), channel_id=1, source_target_pairs={{0,32},{32,0},{64,96},{96,64},{128,160},{160,128},{192,224},{224,1... | collective-permute-start | bytes 24584 | tf_op jit(solution)/shard_map/ppermute | solution.py:660
  123.6 5.5 %collective-permute-done.20 = f32[8,256]{1,0:T(8,128)S(1)} collective-permute-done((f32[8,256]{1,0:T(8,128)S(1)}, f32[8,256]{1,0:T(8,128)S(1)}, u32[]{:S(2)}, u32[]{:S(2)}) %collective-permute-start.20) | collective-permute-done | bytes 8224 | tf_op jit(solution)/shard_map/ppermute | solution.py:660
  129.1 0.6 broadcast_in_dim_squeeze.3
  129.7 0.6 broadcast_in_dim.28
  (51 shorter events, 1.0 us)
Async XLA Ops:
  2.6 14.6 %copy-start.2 = (s32[1,1,1,128,128]{4,3,2,1,0:T(8,128)S(1)}, s32[1,1,1,128,128]{4,3,2,1,0:T(8,128)}, u32[]{:S(2)}) copy-start(s32[1,1,1,128,128]{4,3,2,1,0:T(8,128)} %param.16) | copy-start | bytes 196612
  4.4 9.1 %collective-permute-start.2 = (bf16[544,128]{1,0:T(8,128)(2,1)}, bf16[544,128]{1,0:T(8,128)(2,1)S(1)}, u32[]{:S(2)}, u32[]{:S(2)}) collective-permute-start(bf16[544,128]{1,0:T(8,128)(2,1)} %brick.1.brick_ref.refs_3_), channel_id=1, source_target_pairs={{1,0},{2,1},{3,2},{32,3},{33,32},{34,33},{35,34},{0,35},{65,64},{6... | collective-permute-start | bytes 417800 | tf_op jit(solution)/shard_map/ppermute | solution.py:572
  10.3 6.8 %collective-permute-start = (bf16[544,128]{1,0:T(8,128)(2,1)}, bf16[544,128]{1,0:T(8,128)(2,1)S(1)}, u32[]{:S(2)}, u32[]{:S(2)}) collective-permute-start(bf16[544,128]{1,0:T(8,128)(2,1)} %brick.1.brick_ref.refs_3_), channel_id=1, source_target_pairs={{0,1},{1,2},{2,3},{3,32},{32,33},{33,34},{34,35},{35,0},{64,65},{6... | collective-permute-start | bytes 417800 | tf_op jit(solution)/shard_map/ppermute | solution.py:571
  13.5 6.2 %collective-permute-start.3 = (bf16[544,128]{1,0:T(8,128)(2,1)S(1)}, bf16[544,128]{1,0:T(8,128)(2,1)S(1)}, u32[]{:S(2)}, u32[]{:S(2)}) collective-permute-start(bf16[544,128]{1,0:T(8,128)(2,1)S(1)} %collective-permute-done.2.refs_5_), channel_id=1, source_target_pairs={{1,0},{2,1},{3,2},{32,3},{33,32},{34,33},{35,34},{0,35},{65,64},{6... | collective-permute-start | bytes 417800 | tf_op jit(solution)/shard_map/ppermute | solution.py:577
  17.1 6.3 %collective-permute-start.1 = (bf16[544,128]{1,0:T(8,128)(2,1)S(1)}, bf16[544,128]{1,0:T(8,128)(2,1)S(1)}, u32[]{:S(2)}, u32[]{:S(2)}) collective-permute-start(bf16[544,128]{1,0:T(8,128)(2,1)S(1)} %collective-permute-done.refs_4_), channel_id=1, source_target_pairs={{0,1},{1,2},{2,3},{3,32},{32,33},{33,34},{34,35},{35,0},{64,65},{6... | collective-permute-start | bytes 417800 | tf_op jit(solution)/shard_map/ppermute | solution.py:576
  23.4 6.3 %collective-permute-start.5 = (bf16[544,128]{1,0:T(8,128)(2,1)S(1)}, bf16[544,128]{1,0:T(8,128)(2,1)S(1)}, u32[]{:S(2)}, u32[]{:S(2)}) collective-permute-start(bf16[544,128]{1,0:T(8,128)(2,1)S(1)} %collective-permute-done.1), channel_id=1, source_target_pairs={{0,1},{1,2},{2,3},{3,32},{32,33},{33,34},{34,35},{35,0},{64,65},{6... | collective-permute-start | bytes 417800 | tf_op jit(solution)/shard_map/ppermute | solution.py:579
  23.4 6.3 %collective-permute-start.6 = (bf16[544,128]{1,0:T(8,128)(2,1)S(1)}, bf16[544,128]{1,0:T(8,128)(2,1)S(1)}, u32[]{:S(2)}, u32[]{:S(2)}) collective-permute-start(bf16[544,128]{1,0:T(8,128)(2,1)S(1)} %collective-permute-done.3), channel_id=1, source_target_pairs={{1,0},{2,1},{3,2},{32,3},{33,32},{34,33},{35,34},{0,35},{65,64},{6... | collective-permute-start | bytes 417800 | tf_op jit(solution)/shard_map/ppermute | solution.py:580
  29.7 5.5 %collective-permute-start.7 = (bf16[272,128]{1,0:T(8,128)(2,1)S(1)}, bf16[272,128]{1,0:T(8,128)(2,1)S(1)}, u32[]{:S(2)}, u32[]{:S(2)}) collective-permute-start(bf16[272,128]{1,0:T(8,128)(2,1)S(1)} %slice.50), channel_id=1, source_target_pairs={{0,1},{1,2},{2,3},{3,32},{32,33},{33,34},{34,35},{35,0},{64,65},{6... | collective-permute-start | bytes 208904 | tf_op jit(solution)/shard_map/ppermute | solution.py:581
  29.7 5.5 %collective-permute-start.8 = (bf16[272,128]{1,0:T(8,128)(2,1)S(1)}, bf16[272,128]{1,0:T(8,128)(2,1)S(1)}, u32[]{:S(2)}, u32[]{:S(2)}) collective-permute-start(bf16[272,128]{1,0:T(8,128)(2,1)S(1)} %slice.51), channel_id=1, source_target_pairs={{1,0},{2,1},{3,2},{32,3},{33,32},{34,33},{35,34},{0,35},{65,64},{6... | collective-permute-start | bytes 208904 | tf_op jit(solution)/shard_map/ppermute | solution.py:582
  35.2 1.6 %copy-start = (bf16[544,128]{1,0:T(8,128)(2,1)S(1)}, bf16[544,128]{1,0:T(8,128)(2,1)}, u32[]{:S(2)}) copy-start(bf16[544,128]{1,0:T(8,128)(2,1)} %brick.1.brick_ref.refs_3_) | copy-start | bytes 417796
  35.2 19.4 %copy-start.1 = (bf16[256,768]{1,0:T(8,128)(2,1)S(1)}, bf16[256,768]{1,0:T(8,128)(2,1)}, u32[]{:S(2)}) copy-start(bf16[256,768]{1,0:T(8,128)(2,1)} %get-tuple-element.28.refs_14_) | copy-start | bytes 1179652
  35.2 8.1 %collective-permute-start.10 = (bf16[1632,128]{1,0:T(8,128)(2,1)S(1)}, bf16[1632,128]{1,0:T(8,128)(2,1)S(1)}, u32[]{:S(2)}, u32[]{:S(2)}) collective-permute-start(bf16[1632,128]{1,0:T(8,128)(2,1)S(1)} %pad_maximum_fusion.1), channel_id=1, source_target_pairs={{0,64},{32,224},{64,128},{96,32},{128,192},{160,96},{192,0},{224,1... | collective-permute-start | bytes 1253384 | tf_op jit(solution)/shard_map/ppermute | solution.py:556
  36.8 17.9 %copy-start.5 = (f32[256,128]{1,0:T(8,128)S(1)}, f32[256,128]{1,0:T(8,128)}, u32[]{:S(2)}) copy-start(f32[256,128]{1,0:T(8,128)} %get-tuple-element.31.refs_17_) | copy-start | bytes 393220
  36.8 17.9 %copy-start.6 = (s32[1,1,1,128,128]{4,3,2,1,0:T(8,128)S(1)}, s32[1,1,1,128,128]{4,3,2,1,0:T(8,128)}, u32[]{:S(2)}) copy-start(s32[1,1,1,128,128]{4,3,2,1,0:T(8,128)} %param.15) | copy-start | bytes 196612
  36.8 17.9 %copy-start.7 = (s32[1,1,1,128,128]{4,3,2,1,0:T(8,128)S(1)}, s32[1,1,1,128,128]{4,3,2,1,0:T(8,128)}, u32[]{:S(2)}) copy-start(s32[1,1,1,128,128]{4,3,2,1,0:T(8,128)} %param.17) | copy-start | bytes 196612
  36.8 6.5 %collective-permute-start.12 = (bf16[1632,128]{1,0:T(8,128)(2,1)S(1)}, bf16[1632,128]{1,0:T(8,128)(2,1)S(1)}, u32[]{:S(2)}, u32[]{:S(2)}) collective-permute-start(bf16[1632,128]{1,0:T(8,128)(2,1)S(1)} %pad_maximum_fusion), channel_id=1, source_target_pairs={{4,0},{8,4},{12,8},{16,12},{20,16},{24,20},{28,24},{0,28},{5,1},{9... | collective-permute-start | bytes 1253384 | tf_op jit(solution)/shard_map/ppermute | solution.py:541
  36.9 8.8 %collective-permute-start.4 = (bf16[1632,128]{1,0:T(8,128)(2,1)S(1)}, bf16[1632,128]{1,0:T(8,128)(2,1)S(1)}, u32[]{:S(2)}, u32[]{:S(2)}) collective-permute-start(bf16[1632,128]{1,0:T(8,128)(2,1)S(1)} %pad_maximum_fusion), channel_id=1, source_target_pairs={{0,4},{4,8},{8,12},{12,16},{16,20},{20,24},{24,28},{28,0},{1,5},{5... | collective-permute-start | bytes 1253384 | tf_op jit(solution)/shard_map/ppermute | solution.py:541
  37.4 17.3 %copy-start.3 = (bf16[256,256]{1,0:T(8,128)(2,1)S(1)}, bf16[256,256]{1,0:T(8,128)(2,1)}, u32[]{:S(2)}) copy-start(bf16[256,256]{1,0:T(8,128)(2,1)} %get-tuple-element.29.refs_15_) | copy-start | bytes 393220
  37.4 17.3 %copy-start.4 = (bf16[256,256]{1,0:T(8,128)(2,1)S(1)}, bf16[256,256]{1,0:T(8,128)(2,1)}, u32[]{:S(2)}) copy-start(bf16[256,256]{1,0:T(8,128)(2,1)} %get-tuple-element.30.refs_16_) | copy-start | bytes 393220
  37.4 17.3 %copy-start.8 = (bf16[16,256]{1,0:T(8,128)(2,1)S(1)}, bf16[16,256]{1,0:T(8,128)(2,1)}, u32[]{:S(2)}) copy-start(bf16[16,256]{1,0:T(8,128)(2,1)} %get-tuple-element.32.refs_18_) | copy-start | bytes 24580
  37.4 9.5 %collective-permute-start.13 = (bf16[1632,128]{1,0:T(8,128)(2,1)S(1)}, bf16[1632,128]{1,0:T(8,128)(2,1)S(1)}, u32[]{:S(2)}, u32[]{:S(2)}) collective-permute-start(bf16[1632,128]{1,0:T(8,128)(2,1)S(1)} %constant_dynamic-update-slice_fusion), channel_id=1, source_target_pairs={{4,0},{8,4},{12,8},{16,12},{20,16},{24,20},{28,24},{0,28},{5,1},{9... | collective-permute-start | bytes 1253384 | tf_op jit(solution)/shard_map/ppermute | solution.py:541
  40.0 10.1 %collective-permute-start.9 = (bf16[1632,128]{1,0:T(8,128)(2,1)S(1)}, bf16[1632,128]{1,0:T(8,128)(2,1)S(1)}, u32[]{:S(2)}, u32[]{:S(2)}) collective-permute-start(bf16[1632,128]{1,0:T(8,128)(2,1)S(1)} %constant_dynamic-update-slice_fusion), channel_id=1, source_target_pairs={{0,4},{4,8},{8,12},{12,16},{16,20},{20,24},{24,28},{28,0},{1,5},{5... | collective-permute-start | bytes 1253384 | tf_op jit(solution)/shard_map/ppermute | solution.py:541
  43.3 8.0 %collective-permute-start.14 = (bf16[1632,128]{1,0:T(8,128)(2,1)S(1)}, bf16[1632,128]{1,0:T(8,128)(2,1)S(1)}, u32[]{:S(2)}, u32[]{:S(2)}) collective-permute-start(bf16[1632,128]{1,0:T(8,128)(2,1)S(1)} %collective-permute-done.10.refs_10_), channel_id=1, source_target_pairs={{4,0},{8,4},{12,8},{16,12},{20,16},{24,20},{28,24},{0,28},{5,1},{9... | collective-permute-start | bytes 1253384 | tf_op jit(solution)/shard_map/ppermute | solution.py:541
  43.4 11.3 %collective-permute-start.11 = (bf16[1632,128]{1,0:T(8,128)(2,1)S(1)}, bf16[1632,128]{1,0:T(8,128)(2,1)S(1)}, u32[]{:S(2)}, u32[]{:S(2)}) collective-permute-start(bf16[1632,128]{1,0:T(8,128)(2,1)S(1)} %collective-permute-done.10.refs_10_), channel_id=1, source_target_pairs={{0,4},{4,8},{8,12},{12,16},{16,20},{20,24},{24,28},{28,0},{1,5},{5... | collective-permute-start | bytes 1253384 | tf_op jit(solution)/shard_map/ppermute | solution.py:541
  77.0 31.6 %collective-permute-start.15 = (f32[9,8,256]{2,1,0:T(8,128)S(1)}, f32[9,8,256]{2,1,0:T(8,128)S(1)}, u32[]{:S(2)}, u32[]{:S(2)}) collective-permute-start(f32[9,8,256]{2,1,0:T(8,128)S(1)} %get-tuple-element.34), channel_id=1, source_target_pairs={{0,4},{4,8},{8,12},{12,16},{16,20},{20,24},{24,28},{28,0},{1,5},{5... | collective-permute-start | bytes 221192 | tf_op jit(solution)/shard_map/ppermute | solution.py:650
  107.7 2.0 %collective-permute-start.16 = (f32[9,8,256]{2,1,0:T(8,128)S(1)}, f32[9,8,256]{2,1,0:T(8,128)S(1)}, u32[]{:S(2)}, u32[]{:S(2)}) collective-permute-start(f32[9,8,256]{2,1,0:T(8,128)S(1)} %get-tuple-element.35), channel_id=1, source_target_pairs={{4,0},{8,4},{12,8},{16,12},{20,16},{24,20},{28,24},{0,28},{5,1},{9... | collective-permute-start | bytes 221192 | tf_op jit(solution)/shard_map/ppermute | solution.py:650
  109.7 6.0 %collective-permute-start.17 = (f32[3,8,256]{2,1,0:T(8,128)S(1)}, f32[3,8,256]{2,1,0:T(8,128)S(1)}, u32[]{:S(2)}, u32[]{:S(2)}) collective-permute-start(f32[3,8,256]{2,1,0:T(8,128)S(1)} %slice_select_fusion), channel_id=1, source_target_pairs={{0,192},{32,96},{64,0},{96,160},{128,64},{160,224},{192,128},{224,... | collective-permute-start | bytes 73736 | tf_op jit(solution)/shard_map/ppermute | solution.py:563
  115.8 5.6 %collective-permute-start.18 = (f32[2,8,256]{2,1,0:T(8,128)S(1)}, f32[2,8,256]{2,1,0:T(8,128)S(1)}, u32[]{:S(2)}, u32[]{:S(2)}) collective-permute-start(f32[2,8,256]{2,1,0:T(8,128)S(1)} %get-tuple-element.46), channel_id=1, source_target_pairs={{0,1},{1,2},{2,3},{3,0},{4,5},{5,6},{6,7},{7,4},{8,9},{9,10},{10,1... | collective-permute-start | bytes 49160 | tf_op jit(solution)/shard_map/ppermute | solution.py:650
  115.9 5.5 %collective-permute-start.19 = (f32[2,8,256]{2,1,0:T(8,128)S(1)}, f32[2,8,256]{2,1,0:T(8,128)S(1)}, u32[]{:S(2)}, u32[]{:S(2)}) collective-permute-start(f32[2,8,256]{2,1,0:T(8,128)S(1)} %get-tuple-element.47), channel_id=1, source_target_pairs={{1,0},{2,1},{3,2},{0,3},{5,4},{6,5},{7,6},{4,7},{9,8},{10,9},{11,1... | collective-permute-start | bytes 49160 | tf_op jit(solution)/shard_map/ppermute | solution.py:650
  121.4 7.7 %collective-permute-start.20 = (f32[8,256]{1,0:T(8,128)S(1)}, f32[8,256]{1,0:T(8,128)S(1)}, u32[]{:S(2)}, u32[]{:S(2)}) collective-permute-start(f32[8,256]{1,0:T(8,128)S(1)} %slice_bitcast_fusion.1), channel_id=1, source_target_pairs={{0,32},{32,0},{64,96},{96,64},{128,160},{160,128},{192,224},{224,1... | collective-permute-start | bytes 24584 | tf_op jit(solution)/shard_map/ppermute | solution.py:660
